TPU v7x, 32 devices: a whole 2x2x4 slice. The times are simulated.
32 devices in a mesh: shard: 4 (over x, core), context: 2 (over y), tensor: 4 (over z).
Axes of the slice: x: 2, y: 2, z: 4, core: 2. Of those that a mesh axis runs over, the one named last changes fastest.
Arguments:
- tokens: bfloat16 [8, 768, 960], P('shard', ('context', 'tensor')), may hold values from -6 to 6
- attn_gain: float32 [960], P('shard'), may hold values from 0.25 to 1.75
- w_query: bfloat16 [960, 960], P('shard'), may hold values from -0.1875 to 0.1875
- key_weight: bfloat16 [960, 320], P('shard'), may hold values from -0.1875 to 0.1875
- value_weight: bfloat16 [960, 320], P('shard'), may hold values from -0.1875 to 0.1875
- w_output: bfloat16 [960, 960], P(None, 'shard'), may hold values from -1 to 1
- mlp_gain: float32 [960], P('shard'), may hold values from 0.25 to 1.75
- w_gate: bfloat16 [960, 2560], P('shard', 'tensor'), may hold values from -0.1875 to 0.1875
- w_up: bfloat16 [960, 2560], P('shard', 'tensor'), may hold values from -0.1875 to 0.1875
- w_down: bfloat16 [2560, 960], P('tensor', 'shard'), may hold values from -0.25 to 0.25
- cotangent: bfloat16 [8, 768, 960], P('shard', ('context', 'tensor')), may hold values from -6 to 6
Outputs:
- block_out: bfloat16 [8, 768, 960], P('shard', ('context', 'tensor'))
- tokens_grad: bfloat16 [8, 768, 960], P('shard', ('context', 'tensor'))
- attn_gain_grad: float32 [960], P('shard')
- w_query_grad: float32 [960, 960], P('shard')
- w_key_grad: float32 [960, 320], P('shard')
- w_value_grad: float32 [960, 320], P('shard')
- w_output_grad: float32 [960, 960], P(None, 'shard')
- mlp_gain_grad: float32 [960], P('shard')
- w_gate_grad: float32 [960, 2560], P('shard', 'tensor')
- w_up_grad: float32 [960, 2560], P('shard', 'tensor')
- w_down_grad: float32 [2560, 960], P('tensor', 'shard')
All inputs are finite; a program needn't handle non-finite values.
Results may differ from a plain program's by a relative error of at most 0.022.
Values may be sent and summed in bfloat16 or wider, within the bound.
No kernel may reach another device: no remote copies, remote signals or barrier semaphores. Data moves between devices by JAX's collectives and lax.ppermute only.
A program may use at most 128 MiB of HBM per device.

v0:
```python
import jax
import jax.numpy as jnp
from jax import lax
from jax.sharding import PartitionSpec as P

QUERY_HEADS = 15
KEY_VALUE_HEADS = 5
HEAD_SIZE = 64


EPS = 1e-05


def rope_tables(positions, head_dim):
    half = head_dim // 2
    freq = 10000.0 ** (-jnp.arange(half).astype(jnp.float32) * 2.0 / head_dim)
    angle = positions.astype(jnp.float32)[:, None] * freq[None, :]
    return (jnp.cos(angle), jnp.sin(angle))


def apply_rotation(value_tensor, cosine_lookup, sine_lookup, sign):
    half = value_tensor.shape[-1] // 2
    leading = value_tensor[..., :half]
    trailing = value_tensor[..., half:]
    cos_col = cosine_lookup[:, None, :]
    sin_col = sine_lookup[:, None, :] * sign
    return jnp.concatenate(
        [leading * cos_col - trailing * sin_col, trailing * cos_col + leading * sin_col], -1
    )


def rms_scale(value_tensor):
    return lax.rsqrt(jnp.mean(value_tensor * value_tensor, axis=-1, keepdims=True) + EPS)


def norm_back(grad_norm, value_tensor, scale_rows, gain):
    normed = value_tensor * scale_rows
    scaled = grad_norm * gain
    grad_in = scale_rows * (scaled - normed * jnp.mean(scaled * normed, axis=-1, keepdims=True))
    return (grad_in, jnp.sum(grad_norm * normed, axis=0))


def dot_single_float(left, right):
    return jnp.dot(left, right, preferred_element_type=jnp.float32)


def dot_rows(left, right):
    return lax.dot_general(
        left, right, (((1,), (1,)), ((), ())), preferred_element_type=jnp.float32
    )


def dot_cols(left, right):
    return lax.dot_general(
        left, right, (((0,), (0,)), ((), ())), preferred_element_type=jnp.float32
    )


def masked_scores(query_rotated, key_rot, query_pos, key_pos):
    query_length = query_rotated.shape[0]
    group_count = QUERY_HEADS // KEY_VALUE_HEADS
    grouped_heads = query_rotated.reshape(query_length, KEY_VALUE_HEADS, group_count, HEAD_SIZE)
    scores = jnp.einsum(
        "qkgd,tkd->kgqt", grouped_heads, key_rot, preferred_element_type=jnp.float32
    ) * HEAD_SIZE ** (-0.5)
    allowed = key_pos[None, :] <= query_pos[:, None]
    return (grouped_heads, jnp.where(allowed, scores, -1e30))


def attend(query_rotated, key_rot, value_low, query_pos, key_pos):
    query_length = query_rotated.shape[0]
    grouped_heads, scores = masked_scores(query_rotated, key_rot, query_pos, key_pos)
    peak = jnp.max(scores, axis=-1, keepdims=True)
    expd = jnp.exp(scores - peak)
    total = jnp.sum(expd, axis=-1, keepdims=True)
    probs = (expd / total).astype(jnp.bfloat16)
    mixed = jnp.einsum("kgqt,tkd->qkgd", probs, value_low, preferred_element_type=jnp.float32)
    return (
        mixed.reshape(query_length, QUERY_HEADS * HEAD_SIZE).astype(jnp.bfloat16),
        peak[..., 0] + jnp.log(total[..., 0]),
    )


def attend_back(
    query_rotated,
    key_rot,
    value_low,
    mixture_reduced,
    mixture_gradient,
    log_total,
    query_pos,
    key_pos,
):
    query_length = query_rotated.shape[0]
    group_count = QUERY_HEADS // KEY_VALUE_HEADS
    grouped_heads, scores = masked_scores(query_rotated, key_rot, query_pos, key_pos)
    probs = jnp.exp(scores - log_total[..., None])
    probs_low = probs.astype(jnp.bfloat16)
    gradient_grouped = mixture_gradient.reshape(
        query_length, KEY_VALUE_HEADS, group_count, HEAD_SIZE
    )
    mixture_grouped = mixture_reduced.reshape(query_length, KEY_VALUE_HEADS, group_count, HEAD_SIZE)
    grad_probs = jnp.einsum(
        "qkgd,tkd->kgqt", gradient_grouped, value_low, preferred_element_type=jnp.float32
    )
    delta = jnp.sum(
        gradient_grouped.astype(jnp.float32) * mixture_grouped.astype(jnp.float32), axis=-1
    )
    delta = jnp.transpose(delta, (1, 2, 0))[..., None]
    grad_scores = (probs * (grad_probs - delta) * HEAD_SIZE ** (-0.5)).astype(jnp.bfloat16)
    grad_query = jnp.einsum(
        "kgqt,tkd->qkgd", grad_scores, key_rot, preferred_element_type=jnp.float32
    )
    key_gradient = jnp.einsum(
        "kgqt,qkgd->tkd", grad_scores, grouped_heads, preferred_element_type=jnp.float32
    )
    value_gradient = jnp.einsum(
        "kgqt,qkgd->tkd", probs_low, gradient_grouped, preferred_element_type=jnp.float32
    )
    return (grad_query.reshape(query_length, QUERY_HEADS, HEAD_SIZE), key_gradient, value_gradient)


def body(
    tokens,
    attn_gain,
    w_query,
    key_weight,
    value_weight,
    w_output,
    mlp_gain,
    w_gate,
    w_up,
    w_down,
    cotangent,
):
    sequence_count, local_length, width = tokens.shape
    token_rows = sequence_count * local_length
    group_rank = lax.axis_index(("context", "tensor"))
    complete_length = local_length * lax.axis_size(("context", "tensor"))
    query_pos = group_rank * local_length + jnp.arange(local_length)
    key_pos = jnp.arange(complete_length)
    cosine_lookup, sine_lookup = rope_tables(query_pos, HEAD_SIZE)
    gain_a, gain_m = (
        lax.all_gather(attn_gain, "shard", axis=0, tiled=True),
        lax.all_gather(mlp_gain, "shard", axis=0, tiled=True),
    )
    weights = (
        lax.all_gather(w_query, "shard", axis=0, tiled=True),
        lax.all_gather(key_weight, "shard", axis=0, tiled=True),
        lax.all_gather(value_weight, "shard", axis=0, tiled=True),
        lax.all_gather(w_output, "shard", axis=1, tiled=True),
        lax.all_gather(w_gate, "shard", axis=0, tiled=True),
        lax.all_gather(w_up, "shard", axis=0, tiled=True),
        lax.all_gather(w_down, "shard", axis=1, tiled=True),
    )
    full_query, complete_key, complete_value, full_output, full_gate, full_up, full_down = weights
    tokens_f = tokens.astype(jnp.float32).reshape(token_rows, width)
    scale_a = rms_scale(tokens_f)
    attention_normed = (tokens_f * scale_a * gain_a).astype(jnp.bfloat16)
    query = dot_single_float(attention_normed, full_query).reshape(
        sequence_count, local_length, QUERY_HEADS, HEAD_SIZE
    )
    key = dot_single_float(attention_normed, complete_key).reshape(
        sequence_count, local_length, KEY_VALUE_HEADS, HEAD_SIZE
    )
    value_rows = dot_single_float(attention_normed, complete_value).reshape(
        sequence_count, local_length, KEY_VALUE_HEADS * HEAD_SIZE
    )
    query_rotated = apply_rotation(query, cosine_lookup, sine_lookup, 1.0).astype(jnp.bfloat16)
    key_rot = (
        apply_rotation(key, cosine_lookup, sine_lookup, 1.0)
        .astype(jnp.bfloat16)
        .reshape(sequence_count, local_length, KEY_VALUE_HEADS * HEAD_SIZE)
    )
    value_low = value_rows.astype(jnp.bfloat16)
    gathered_keys, gathered_values = (
        lax.all_gather(key_rot, ("context", "tensor"), axis=1, tiled=True),
        lax.all_gather(value_low, ("context", "tensor"), axis=1, tiled=True),
    )
    gathered_keys = gathered_keys.reshape(
        sequence_count, complete_length, KEY_VALUE_HEADS, HEAD_SIZE
    )
    gathered_values = gathered_values.reshape(
        sequence_count, complete_length, KEY_VALUE_HEADS, HEAD_SIZE
    )

    def forward_one(item):
        return attend(item[0], item[1], item[2], query_pos, key_pos)

    mixture_reduced, log_total = lax.map(
        forward_one, (query_rotated, gathered_keys, gathered_values)
    )
    mix_flat = mixture_reduced.reshape(token_rows, QUERY_HEADS * HEAD_SIZE)
    hidden = tokens_f + dot_single_float(mix_flat, full_output)
    scale_m = rms_scale(hidden)
    normed_m = (hidden * scale_m * gain_m).astype(jnp.bfloat16)
    group_tokens = lax.all_gather(
        normed_m.reshape(sequence_count, local_length, width), "tensor", axis=1, tiled=True
    )
    group_rows = group_tokens.shape[1]
    group_flat = group_tokens.reshape(sequence_count * group_rows, width)
    gate = dot_single_float(group_flat, full_gate)
    up_vals = dot_single_float(group_flat, full_up)
    sigma = jax.nn.sigmoid(gate)
    act = (gate * sigma * up_vals).astype(jnp.bfloat16)
    partial_out = dot_single_float(act, full_down).reshape(sequence_count, group_rows, width)
    mlp_out = (
        lax.psum_scatter(
            partial_out.astype(jnp.bfloat16), "tensor", scatter_dimension=1, tiled=True
        )
        .astype(jnp.float32)
        .reshape(token_rows, width)
    )
    block_out = (hidden + mlp_out).astype(jnp.bfloat16).reshape(sequence_count, local_length, width)
    again = (
        lax.all_gather(w_query, "shard", axis=0, tiled=True),
        lax.all_gather(key_weight, "shard", axis=0, tiled=True),
        lax.all_gather(value_weight, "shard", axis=0, tiled=True),
        lax.all_gather(w_output, "shard", axis=1, tiled=True),
        lax.all_gather(w_gate, "shard", axis=0, tiled=True),
        lax.all_gather(w_up, "shard", axis=0, tiled=True),
        lax.all_gather(w_down, "shard", axis=1, tiled=True),
    )
    full_query, complete_key, complete_value, full_output, full_gate, full_up, full_down = again
    cot_f = cotangent.astype(jnp.float32).reshape(token_rows, width)
    cot_group = lax.all_gather(cotangent, "tensor", axis=1, tiled=True).reshape(
        sequence_count * group_rows, width
    )
    grad_act = dot_rows(cot_group, full_down)
    grad_down_rows = dot_cols(cot_group, act)
    grad_up = (grad_act * gate * sigma).astype(jnp.bfloat16)
    grad_gate = (grad_act * up_vals * sigma * (1.0 + gate * (1.0 - sigma))).astype(jnp.bfloat16)
    partial_in = dot_rows(grad_gate, full_gate) + dot_rows(grad_up, full_up)
    grad_nm = lax.psum_scatter(
        partial_in.reshape(sequence_count, group_rows, width),
        "tensor",
        scatter_dimension=1,
        tiled=True,
    ).reshape(token_rows, width)
    grad_gate_w = dot_cols(group_flat, grad_gate)
    grad_up_w = dot_cols(group_flat, grad_up)
    grad_hn, grad_mgain = norm_back(grad_nm, hidden, scale_m, gain_m)
    grad_hidden = cot_f + grad_hn
    grad_hidden_low = grad_hidden.astype(jnp.bfloat16)
    mixture_gradient = (
        dot_rows(grad_hidden_low, full_output)
        .astype(jnp.bfloat16)
        .reshape(sequence_count, local_length, QUERY_HEADS * HEAD_SIZE)
    )

    def backward_one(item):
        return attend_back(item[0], item[1], item[2], item[3], item[4], item[5], query_pos, key_pos)

    grad_query, key_gradient, value_gradient = lax.map(
        backward_one,
        (
            query_rotated,
            gathered_keys,
            gathered_values,
            mixture_reduced,
            mixture_gradient,
            log_total,
        ),
    )
    local_key, local_value = (
        lax.psum_scatter(
            key_gradient.reshape(
                sequence_count, complete_length, KEY_VALUE_HEADS * HEAD_SIZE
            ).astype(jnp.bfloat16),
            ("context", "tensor"),
            scatter_dimension=1,
            tiled=True,
        ).astype(jnp.float32),
        lax.psum_scatter(
            value_gradient.reshape(
                sequence_count, complete_length, KEY_VALUE_HEADS * HEAD_SIZE
            ).astype(jnp.bfloat16),
            ("context", "tensor"),
            scatter_dimension=1,
            tiled=True,
        ).astype(jnp.float32),
    )
    grad_query = (
        apply_rotation(grad_query, cosine_lookup, sine_lookup, -1.0)
        .reshape(token_rows, QUERY_HEADS * HEAD_SIZE)
        .astype(jnp.bfloat16)
    )
    local_key = (
        apply_rotation(
            local_key.reshape(sequence_count, local_length, KEY_VALUE_HEADS, HEAD_SIZE),
            cosine_lookup,
            sine_lookup,
            -1.0,
        )
        .reshape(token_rows, KEY_VALUE_HEADS * HEAD_SIZE)
        .astype(jnp.bfloat16)
    )
    local_value = local_value.reshape(token_rows, KEY_VALUE_HEADS * HEAD_SIZE).astype(jnp.bfloat16)
    grad_na = (
        dot_rows(grad_query, full_query)
        + dot_rows(local_key, complete_key)
        + dot_rows(local_value, complete_value)
    )
    grad_tn, grad_again = norm_back(grad_na, tokens_f, scale_a, gain_a)
    tokens_grad = (
        (grad_hidden + grad_tn).astype(jnp.bfloat16).reshape(sequence_count, local_length, width)
    )
    term_query = dot_cols(attention_normed, grad_query)
    term_key = dot_cols(attention_normed, local_key)
    term_value = dot_cols(attention_normed, local_value)
    term_output_rows = dot_cols(grad_hidden_low, mix_flat)
    outgoing = (
        term_query[None],
        term_key[None],
        term_value[None],
        term_output_rows[None],
        grad_again[None, :, None],
        grad_mgain[None, :, None],
        grad_gate_w[None],
        grad_up_w[None],
        grad_down_rows[None],
    )
    received = (
        lax.all_to_all(
            outgoing[0].astype(jnp.bfloat16), "shard", split_axis=1, concat_axis=0, tiled=True
        ).astype(jnp.float32),
        lax.all_to_all(
            outgoing[1].astype(jnp.bfloat16), "shard", split_axis=1, concat_axis=0, tiled=True
        ).astype(jnp.float32),
        lax.all_to_all(
            outgoing[2].astype(jnp.bfloat16), "shard", split_axis=1, concat_axis=0, tiled=True
        ).astype(jnp.float32),
        lax.all_to_all(
            outgoing[3].astype(jnp.bfloat16), "shard", split_axis=1, concat_axis=0, tiled=True
        ).astype(jnp.float32),
        lax.all_to_all(
            outgoing[4].astype(jnp.bfloat16), "shard", split_axis=1, concat_axis=0, tiled=True
        ).astype(jnp.float32),
        lax.all_to_all(
            outgoing[5].astype(jnp.bfloat16), "shard", split_axis=1, concat_axis=0, tiled=True
        ).astype(jnp.float32),
        lax.all_to_all(
            outgoing[6].astype(jnp.bfloat16), "shard", split_axis=1, concat_axis=0, tiled=True
        ).astype(jnp.float32),
        lax.all_to_all(
            outgoing[7].astype(jnp.bfloat16), "shard", split_axis=1, concat_axis=0, tiled=True
        ).astype(jnp.float32),
        lax.all_to_all(
            outgoing[8].astype(jnp.bfloat16), "shard", split_axis=1, concat_axis=0, tiled=True
        ).astype(jnp.float32),
    )
    owned = tuple((jnp.sum(piece, axis=0) for piece in received))
    owned_output = owned[3].T
    owned_again = owned[4][:, 0]
    owned_mgain = owned[5][:, 0]
    mlp_sums = (
        lax.psum(owned[6].astype(jnp.bfloat16), "context").astype(jnp.float32),
        lax.psum(owned[7].astype(jnp.bfloat16), "context").astype(jnp.float32),
        lax.psum(owned[8].T.astype(jnp.bfloat16), "context").astype(jnp.float32),
    )
    attn_sums = (
        lax.psum(owned[0].astype(jnp.bfloat16), ("context", "tensor")).astype(jnp.float32),
        lax.psum(owned[1].astype(jnp.bfloat16), ("context", "tensor")).astype(jnp.float32),
        lax.psum(owned[2].astype(jnp.bfloat16), ("context", "tensor")).astype(jnp.float32),
        lax.psum(owned_output.astype(jnp.bfloat16), ("context", "tensor")).astype(jnp.float32),
        lax.psum(owned_again.astype(jnp.bfloat16), ("context", "tensor")).astype(jnp.float32),
        lax.psum(owned_mgain.astype(jnp.bfloat16), ("context", "tensor")).astype(jnp.float32),
    )
    query_total, key_total, value_total, output_total, again_total, mgain_total = attn_sums
    return (
        block_out,
        tokens_grad,
        again_total,
        query_total,
        key_total,
        value_total,
        output_total,
        mgain_total,
        mlp_sums[0],
        mlp_sums[1],
        mlp_sums[2],
    )


def solution(mesh):
    return jax.shard_map(
        body,
        mesh=mesh,
        in_specs=(
            P("shard", ("context", "tensor"), None),
            P("shard"),
            P("shard", None),
            P("shard", None),
            P("shard", None),
            P(None, "shard"),
            P("shard"),
            P("shard", "tensor"),
            P("shard", "tensor"),
            P("tensor", "shard"),
            P("shard", ("context", "tensor"), None),
        ),
        out_specs=(
            P("shard", ("context", "tensor"), None),
            P("shard", ("context", "tensor"), None),
            P("shard"),
            P("shard", None),
            P("shard", None),
            P("shard", None),
            P(None, "shard"),
            P("shard"),
            P("shard", "tensor"),
            P("shard", "tensor"),
            P("tensor", "shard"),
        ),
        check_vma=False,
    )
```

profile of v0, /device:TPU:0, one launch (start us, length us, event | category | flops | bytes accessed | tf_op | source)
XLA Modules:
  0.0 740.1 jit_solution(17978608939246479207)
XLA Ops:
  11.1 9.3 %all-gather.1 = bf16[4,240,320]{1,2,0:T(8,128)(2,1)S(1)} all-gather(bf16[1,240,320]{1,2,0:T(8,128)(2,1)S(1)} %bitcast.376), channel_id=1, replica_groups=mesh['shard'=4,'context'=2,'tensor'=4] {'shard'}, dimensions={0}, use_global_device_ids=true | all-gather | bytes 768000 | tf_op jit(solution)/shard_map/all_gather | solution.py:149
  23.4 7.5 %all-reduce.3 = (f32[960]{0:T(1024)S(1)}, f32[960]{0:T(1024)S(1)}) all-reduce(f32[960]{0:T(1024)S(1)} %dynamic-update-slice, f32[960]{0:T(1024)S(1)} %dynamic-update-slice.1), channel_id=1, replica_groups=mesh['shard'=4,'context'=2,'tensor'=4] {'shard'}, use_global_device_ids=true, to_apply=%add | all-reduce | flops 1920 | bytes 15360
  32.2 35.7 %all_gather.50 = bf16[2,768,320]{2,0,1:T(2,128)(2,1)S(1)} all-gather(bf16[2,96,320]{2,0,1:T(2,128)(2,1)S(1)} %copy.129), channel_id=1, replica_groups=mesh['shard'=4,'context'=2,'tensor'=4] {'context','tensor'}, dimensions={1}, use_global_device_ids=true | all-gather | bytes 1105920 | tf_op jit(solution)/shard_map/all_gather | solution.py:177
  69.3 11.4 %all-gather = bf16[4,240,320]{1,2,0:T(8,128)(2,1)S(1)} all-gather(bf16[1,240,320]{1,2,0:T(8,128)(2,1)} %bitcast.377), channel_id=1, replica_groups=mesh['shard'=4,'context'=2,'tensor'=4] {'shard'}, dimensions={0}, use_global_device_ids=true | all-gather | bytes 768000 | tf_op jit(solution)/shard_map/all_gather | solution.py:150
  84.1 38.0 %all_gather.48 = bf16[2,768,320]{2,1,0:T(8,128)(2,1)} all-gather(bf16[2,96,320]{2,1,0:T(8,128)(2,1)S(1)} %convolution_convert_fusion.6), channel_id=1, replica_groups=mesh['shard'=4,'context'=2,'tensor'=4] {'context','tensor'}, dimensions={1}, use_global_device_ids=true | all-gather | bytes 1105920 | tf_op jit(solution)/shard_map/all_gather | solution.py:178
  130.8 7.8 %while.28 = (s32[]{:T(128)}, bf16[2,96,960]{1,2,0:T(8,128)(2,1)S(1)}, f32[2,5,3,96]{3,2,1,0:T(4,128)S(1)}, bf16[2,768,5,64]{1,3,2,0:T(8,128)(2,1)}, bf16[2,768,5...) while((s32[]{:T(128)}, ...), condition=%wide.region_4.5_spmd.clone, body=%wide.region_1.4_spmd.clone.sunk | while | flops 296551104 | bytes 19840776 | solution.py:190
  145.5 34.8 %all-gather.14.cloned.1.call-done = bf16[2,384,960]{2,1,0:T(8,128)(2,1)} async-done(((bf16[2,96,960]{2,1,0:T(8,128)(2,1)}), bf16[2,384,960]{2,1,0:T(8,128)(2,1)}) %all-gather.14.cloned.1.call-update) | async-done | bytes 1474576 | tf_op jit(solution)/shard_map/all_gather | solution.py:197
  184.8 13.6 %all-gather.18.cloned.1.call-done = bf16[960,640]{1,0:T(8,128)(2,1)} async-done(((bf16[240,640]{1,0:T(8,128)(2,1)}), bf16[960,640]{1,0:T(8,128)(2,1)}) %all-gather.18.cloned.1.call-update) | async-done | bytes 1228816 | tf_op jit(solution)/shard_map/all_gather | solution.py:153
  202.8 14.7 %all-gather.20.cloned.1.call-done = bf16[640,960]{0,1:T(8,128)(2,1)} async-done(((bf16[640,240]{0,1:T(8,128)(2,1)}), bf16[640,960]{0,1:T(8,128)(2,1)}) %all-gather.20.cloned.1.call-update) | async-done | bytes 1228816 | tf_op jit(solution)/shard_map/all_gather | solution.py:154
  217.6 38.7 %all-gather.22.cloned.1.call-done = bf16[2,384,960]{2,1,0:T(8,128)(2,1)} async-done(((bf16[2,96,960]{2,1,0:T(8,128)(2,1)}), bf16[2,384,960]{2,1,0:T(8,128)(2,1)}) %all-gather.22.cloned.1.call-update) | async-done | bytes 1474576 | tf_op jit(solution)/shard_map/all_gather | solution.py:226
  284.6 10.2 %reduce.30 = bf16[960,640]{1,0:T(8,128)(2,1)} reduce(bf16[960,1,640]{2,1,0:T(2,128)(2,1)} %bitcast.343, bf16[]{:T(256)} %broadcast.234), dimensions={1}, to_apply=%bitcast.262.reduce_sub_computation | reduce | bytes 2457602
  309.2 10.2 %reduce.31 = bf16[960,640]{1,0:T(8,128)(2,1)} reduce(bf16[960,1,640]{2,1,0:T(2,128)(2,1)} %bitcast.344, bf16[]{:T(256)} %broadcast.234), dimensions={1}, to_apply=%bitcast.261.reduce_sub_computation | reduce | bytes 2457602
  323.0 6.9 reduce-scatter.6.cloned.1.call-done
  332.8 34.8 %reduce-scatter.4.cloned.1.call-done = bf16[2,96,960]{2,1,0:T(8,128)(2,1)} async-done(((bf16[2,384,960]{2,1,0:T(8,128)(2,1)}), bf16[2,96,960]{2,1,0:T(8,128)(2,1)}) %reduce-scatter.4.cloned.1.call-update) | async-done | bytes 368656 | tf_op jit(solution)/shard_map/reduce_scatter | solution.py:208
  377.1 25.9 %while.29 = (s32[]{:T(128)}, f32[2,96,15,64]{1,3,2,0:T(8,128)}, bf16[2,768,5,64]{1,3,2,0:T(8,128)(2,1)}, bf16[2,768,5,64]{1,3,2,0:T(8,128)(2,1)}, bf16[2,768,5,6...) while((s32[]{:T(128)}, f32[2,96,15,64]{1,3,2,0:T(8,128)}, ...), condition=%wide.region_11.12_spmd.clone, body=%wide.region_9.11_spmd.clone.sunk | while | flops 720394944 | bytes 56168276 | solution.py:254
  413.7 9.1 %reduce.32 = bf16[960,640]{1,0:T(8,128)(2,1)S(1)} reduce(bf16[960,1,640]{2,1,0:T(2,128)(2,1)} %bitcast.345, bf16[]{:T(256)} %broadcast.234), dimensions={1}, to_apply=%bitcast.260.reduce_sub_computation | reduce | bytes 2457602
  436.7 13.8 %reduce.26 = bf16[960,960]{1,0:T(8,128)(2,1)} reduce(bf16[960,1,960]{2,1,0:T(2,128)(2,1)} %bitcast.332, bf16[]{:T(256)} %broadcast.234), dimensions={1}, to_apply=%bitcast.258.reduce_sub_computation | reduce | bytes 3686402
  469.7 13.8 %reduce.27 = bf16[960,960]{1,0:T(8,128)(2,1)} reduce(bf16[960,1,960]{2,1,0:T(2,128)(2,1)} %bitcast.333, bf16[]{:T(256)} %broadcast.234), dimensions={1}, to_apply=%bitcast.259.reduce_sub_computation | reduce | bytes 3686402
  535.0 19.5 %reduce-scatter.8.cloned.1.call-done = bf16[2,96,320]{2,1,0:T(8,128)(2,1)} async-done(((bf16[2,768,320]{2,1,0:T(8,128)(2,1)}), bf16[2,96,320]{2,1,0:T(8,128)(2,1)}) %reduce-scatter.8.cloned.1.call-update) | async-done | bytes 122896 | tf_op jit(solution)/shard_map/reduce_scatter | solution.py:274
  558.8 7.2 reduce.29
  576.2 18.1 %all-reduce.15.cloned.1.call-done = (bf16[240,640]{1,0:T(8,128)(2,1)}, bf16[240,640]{1,0:T(8,128)(2,1)}, bf16[640,240]{0,1:T(8,128)(2,1)}) async-done(((bf16[240,640]{1,0:T(8,128)(2,1)}, bf16[240,640]{1,0:T(8,128)(2,1)}, bf16[640,240]{0,1:T(8,128)(2,1)}), (bf16[240,640]{1,0:T(8,128)(2,1)}, bf16[240,640]{1,0:T(8,128)(2,1)}, bf16[640,240]{0,1:T(8,128)(2,1)})) %all-reduce.15.cloned.1.call-update) | async-done | bytes 921616 | tf_op jit(solution)/shard_map/psum | solution.py:357
  659.4 7.5 %all-to-all-done = bf16[1,960,1]{2,0,1:T(2,128)(2,1)S(1)} async-done(((bf16[1,960,1]{2,0,1:T(2,128)(2,1)}), bf16[1,960,1]{2,0,1:T(2,128)(2,1)S(1)}, u32[]{:S(2)}, u32[]{:S(2)}) %all-to-all-start) | async-done | bytes 1952 | tf_op jit(solution)/shard_map/all_to_all | solution.py:336
  669.0 20.7 %all-reduce.4 = (bf16[240]{0:T(256)(128)(2,1)S(1)}, bf16[240]{0:T(256)(128)(2,1)S(1)}) all-reduce(bf16[240]{0:T(256)(128)(2,1)S(1)} %reduce_sum.179, bf16[240]{0:T(256)(128)(2,1)S(1)} %reduce_sum.185), channel_id=1, replica_groups=mesh['shard'=4,'context'=2,'tensor'=4] {'context','tensor'}, use_global_device_ids=true, to_apply=%region_17.18 | all-reduce | flops 480 | bytes 1920 | tf_op jit(solution)/shard_map/psum | solution.py:366
  690.8 36.7 %all-reduce.13.cloned.1.call-done = (bf16[960,240]{0,1:T(8,128)(2,1)}, bf16[240,960]{1,0:T(8,128)(2,1)}, bf16[240,320]{0,1:T(8,128)(2,1)}, bf16[240,320]{0,1:T(8,128)(2,1)}) async-done(((bf16[960,240]{0,1:T(8,128)(2,1)}, bf16[240,960]{1,0:T(8,128)(2,1)}, bf16[240,320]{0,1:T(8,128)(2,1)}, bf16[240,320]{0,1:T(8,128)(2,1)}), (bf16[960,240]{0,1:T(8,128)(2,1)}, bf16[240,960]{1,0:T(8,128)(2,1)}, ...) | async-done | bytes 1228816 | tf_op jit(solution)/shard_map/psum | solution.py:365
  (325 shorter events, 311.3 us)
Async XLA Ops:
  7.2 117.2 %all-gather.10.cloned.1.call-start = ((), (), s32[]{:S(2)}) async-start(), calls=%async_computation.12 | async-start | bytes 2457600 | tf_op jit(solution)/shard_map/all_gather | solution.py:148
  7.9 130.9 %all-gather.12.cloned.1.call-start = ((), (), s32[]{:S(2)}) async-start(), calls=%async_computation.13 | async-start | bytes 2457600 | tf_op jit(solution)/shard_map/all_gather | solution.py:151
  10.0 135.5 %all-gather.16.cloned.1.call-start = ((), (), s32[]{:S(2)}) async-start(), calls=%async_computation.15 | async-start | bytes 1536000 | tf_op jit(solution)/shard_map/all_gather | solution.py:152
  10.8 169.6 %all-gather.14.cloned.1.call-start = ((), (), s32[]{:S(2)}) async-start(), calls=%async_computation.14 | async-start | bytes 1966080 | tf_op jit(solution)/shard_map/all_gather | solution.py:197
  81.2 43.2 %copy-start.8 = (bf16[4,240,320]{1,0,2:T(4,128)(2,1)}, bf16[4,240,320]{1,0,2:T(4,128)(2,1)S(1)}, u32[]{:S(2)}) copy-start(bf16[4,240,320]{1,0,2:T(4,128)(2,1)S(1)} %copy.126) | copy-start | bytes 1843204
  143.2 55.2 %all-gather.18.cloned.1.call-start = ((), (), s32[]{:S(2)}) async-start(), calls=%async_computation.16 | async-start | bytes 1536000 | tf_op jit(solution)/shard_map/all_gather | solution.py:153
  143.8 73.8 %all-gather.20.cloned.1.call-start = ((), (), s32[]{:S(2)}) async-start(), calls=%async_computation.17 | async-start | bytes 1536000 | tf_op jit(solution)/shard_map/all_gather | solution.py:154
  144.4 111.9 %all-gather.22.cloned.1.call-start = ((), (), s32[]{:S(2)}) async-start(), calls=%async_computation.19 | async-start | bytes 1966080 | tf_op jit(solution)/shard_map/all_gather | solution.py:226
  145.1 184.8 %reduce-scatter.6.cloned.1.call-start = ((), (), s32[]{:S(2)}) async-start(), calls=%async_computation.20 | async-start | bytes 3932160 | tf_op jit(solution)/shard_map/reduce_scatter | solution.py:234
  270.7 96.9 %reduce-scatter.4.cloned.1.call-start = ((), (), s32[]{:S(2)}) async-start(), calls=%async_computation.18 | async-start | bytes 1966080 | tf_op jit(solution)/shard_map/reduce_scatter | solution.py:208
  298.4 74.1 %all-to-all-start.6 = ((bf16[4,2,76800]{2,1,0:T(2,128)(2,1)}), bf16[4,2,76800]{2,1,0:T(2,128)(2,1)}, u32[]{:S(2)}, u32[]{:S(2)}) async-start(bf16[4,2,76800]{2,1,0:T(2,128)(2,1)} %reshape.492), calls=%async_computation.9 | async-start | bytes 2457600 | tf_op jit(solution)/shard_map/all_to_all | solution.py:342
  323.0 44.6 %copy-start.15 = (bf16[2,96,960]{2,1,0:T(8,128)(2,1)S(1)}, bf16[2,96,960]{2,1,0:T(8,128)(2,1)}, u32[]{:S(2)}) copy-start(bf16[2,96,960]{2,1,0:T(8,128)(2,1)} %param.25) | copy-start | bytes 1105924
  372.5 52.1 %all-to-all-start.7 = ((bf16[4,2,76800]{2,1,0:T(2,128)(2,1)}), bf16[4,2,76800]{2,1,0:T(2,128)(2,1)}, u32[]{:S(2)}, u32[]{:S(2)}) async-start(bf16[4,2,76800]{2,1,0:T(2,128)(2,1)} %reshape.494), calls=%async_computation.10 | async-start | bytes 2457600 | tf_op jit(solution)/shard_map/all_to_all | solution.py:345
  376.8 141.6 %all-reduce.11.cloned.1.call-start = ((), (), s32[]{:S(2)}) async-start(), calls=%async_computation.22 | async-start | bytes 2359296
  424.6 30.8 %all-to-all-start.8 = ((bf16[4,2,76800]{2,1,0:T(2,128)(2,1)}), bf16[4,2,76800]{2,1,0:T(2,128)(2,1)S(1)}, u32[]{:S(2)}, u32[]{:S(2)}) async-start(bf16[4,2,76800]{2,1,0:T(2,128)(2,1)} %reshape.496), calls=%async_computation.11 | async-start | bytes 2457600 | tf_op jit(solution)/shard_map/all_to_all | solution.py:348
  428.1 126.4 %reduce-scatter.8.cloned.1.call-start = ((), (), s32[]{:S(2)}) async-start(), calls=%async_computation.21 | async-start | bytes 1327104 | tf_op jit(solution)/shard_map/reduce_scatter | solution.py:274
  455.4 33.0 %all-to-all-start.4 = ((bf16[4,2,115200]{2,1,0:T(2,128)(2,1)}), bf16[4,2,115200]{2,1,0:T(2,128)(2,1)}, u32[]{:S(2)}, u32[]{:S(2)}) async-start(bf16[4,2,115200]{2,1,0:T(2,128)(2,1)} %reshape.484), calls=%async_computation.7 | async-start | bytes 3686400 | tf_op jit(solution)/shard_map/all_to_all | solution.py:333
  488.4 42.9 %all-to-all-start.1 = ((bf16[4,2,115200]{2,1,0:T(2,128)(2,1)}), bf16[4,2,115200]{2,1,0:T(2,128)(2,1)}, u32[]{:S(2)}, u32[]{:S(2)}) async-start(bf16[4,2,115200]{2,1,0:T(2,128)(2,1)} %reshape.486), calls=%async_computation.4 | async-start | bytes 3686400 | tf_op jit(solution)/shard_map/all_to_all | solution.py:324
  492.9 101.4 %all-reduce.15.cloned.1.call-start = ((), (), s32[]{:S(2)}) async-start(), calls=%async_computation.24 | async-start | bytes 1843200 | tf_op jit(solution)/shard_map/psum | solution.py:357
  531.3 37.8 %all-to-all-start.2 = ((bf16[4,2,38400]{2,1,0:T(2,128)(2,1)}), bf16[4,2,38400]{2,1,0:T(2,128)(2,1)S(1)}, u32[]{:S(2)}, u32[]{:S(2)}) async-start(bf16[4,2,38400]{2,1,0:T(2,128)(2,1)} %reshape.488), calls=%async_computation.5 | async-start | bytes 1228800 | tf_op jit(solution)/shard_map/all_to_all | solution.py:327
  569.1 62.9 %all-to-all-start.3 = ((bf16[4,2,38400]{2,1,0:T(2,128)(2,1)}), bf16[4,2,38400]{2,1,0:T(2,128)(2,1)}, u32[]{:S(2)}, u32[]{:S(2)}) async-start(bf16[4,2,38400]{2,1,0:T(2,128)(2,1)} %reshape.490), calls=%async_computation.6 | async-start | bytes 1228800 | tf_op jit(solution)/shard_map/all_to_all | solution.py:330
  632.0 13.4 %all-to-all-start.5 = ((bf16[1,960,1]{2,0,1:T(2,128)(2,1)}), bf16[1,960,1]{2,0,1:T(2,128)(2,1)S(1)}, u32[]{:S(2)}, u32[]{:S(2)}) async-start(bf16[1,960,1]{2,0,1:T(2,128)(2,1)} %convert_element_type.376), calls=%async_computation.8 | async-start | bytes 983040 | tf_op jit(solution)/shard_map/all_to_all | solution.py:339
  635.5 92.1 %all-reduce.13.cloned.1.call-start = ((), (), s32[]{:S(2)}) async-start(), calls=%async_computation.23 | async-start | bytes 2621440 | tf_op jit(solution)/shard_map/psum | solution.py:365
  654.9 11.9 %all-to-all-start = ((bf16[1,960,1]{2,0,1:T(2,128)(2,1)}), bf16[1,960,1]{2,0,1:T(2,128)(2,1)S(1)}, u32[]{:S(2)}, u32[]{:S(2)}) async-start(bf16[1,960,1]{2,0,1:T(2,128)(2,1)} %convert_element_type.375), calls=%async_computation.3 | async-start | bytes 983040 | tf_op jit(solution)/shard_map/all_to_all | solution.py:336
  (47 other events, 222.3 us)
Sparse Core Ops, SparseCore 0:
  9.6 24.8 all-gather.9
  36.6 21.8 all-gather.11
  60.0 21.0 all-gather.15
  143.3 37.0 all-gather.13
  181.8 16.5 all-gather.17
  199.8 17.7 all-gather.19
  219.2 37.0 all-gather.21
  270.8 59.1 reduce-scatter.5
  332.3 35.2 reduce-scatter.3
  407.9 79.4 all-reduce.10
  491.2 63.3 reduce-scatter.7
  557.6 36.6 all-reduce.14
  642.2 85.3 all-reduce.12
where the time goes:
time: 752 us; the launch traced here: 740 us
  waiting for transfers between devices  229 us (30%)
  local copies, waits for them, and re-layouts  149 us (20%)
  blocking collectives  123 us (16%)
  other arithmetic  109 us (14%)
  matrix products  75.7 us (10%)
  starting transfers between devices  37.8 us (5%)
  between operations  16.2 us (2%)
    unnamed x102, local copies, waits for them, and re-layouts  85.5 us
    unnamed x7, other arithmetic  70.5 us
    all_gather x1, waiting for transfers between devices, body(): lax.all_gather(cotangent, 'tensor', axis=1, tiled=True)  38.7 us
    all_gather x1, blocking collectives, body(): lax.all_gather(value_low, ('context', 'tensor'), axis=1, tiled=True)  38 us
    psum x1, waiting for transfers between devices, body(): lax.psum(owned_output.astype(jnp.bfloat16), ('context', 'tensor'))  36.7 us
    all_gather x1, blocking collectives, body(): lax.all_gather(key_rot, ('context', 'tensor'), axis=1, tiled=True)  35.7 us
    all_gather x1, waiting for transfers between devices, body(): lax.all_gather(normed_m.reshape(sequence_count, local_length, width), 'te...  34.8 us
    reduce_scatter x1, waiting for transfers between devices, body(): lax.psum_scatter(partial_out.astype(jnp.bfloat16), 'tensor', scatter_dime...  34.8 us
  transfers between devices with their start and end apart: 22, of which 10 were waited for; matrix products, arithmetic and copies ran while one was open for 42% of the time, Pallas kernels for 0%

commit v1 on v0

v1 whole, which is shorter than its diff:
```python
import functools

import jax
import jax.numpy as jnp
import numpy as np
from jax import lax
from jax.experimental import pallas as pl
from jax.experimental.pallas import tpu as pltpu
from jax.sharding import PartitionSpec as P

QUERY_HEADS = 15
KEY_VALUE_HEADS = 5
HEAD_SIZE = 64
GROUP = QUERY_HEADS // KEY_VALUE_HEADS
EPS = 1e-05
KERNEL_VMEM = 40 * 1024 * 1024


def dot(left, right):
    return jnp.dot(left, right, preferred_element_type=jnp.float32)


def dot_rows(left, right):
    return lax.dot_general(
        left, right, (((1,), (1,)), ((), ())), preferred_element_type=jnp.float32
    )


def dot_cols(left, right):
    return lax.dot_general(
        left, right, (((0,), (0,)), ((), ())), preferred_element_type=jnp.float32
    )


def rms_scale(rows):
    return lax.rsqrt(jnp.mean(rows * rows, axis=-1, keepdims=True) + EPS)


def norm_back(grad_norm, rows, scale_rows, gain):
    normed = rows * scale_rows
    scaled = grad_norm * gain
    return scale_rows * (scaled - normed * jnp.mean(scaled * normed, axis=-1, keepdims=True))


def after(value, *others):
    return lax.optimization_barrier((value, *others))[0]


def bits_of(count):
    return count.bit_length() - 1


def flip_blocks(rows, shards, index):
    width = rows.shape[-1] // shards
    bits = bits_of(shards)
    for place in range(bits):
        step = width << place
        pieces = [rows[..., i * step : (i + 1) * step] for i in range(rows.shape[-1] // step)]
        swapped = jnp.concatenate([pieces[i ^ 1] for i in range(len(pieces))], -1)
        rows = jnp.where((index >> (bits - 1 - place)) & 1 == 1, swapped, rows)
    return rows


def reverse_blocks(rows, shards):
    width = rows.shape[-1] // shards
    bits = bits_of(shards)
    order = [int(format(i, f"0{bits}b")[::-1], 2) for i in range(shards)]
    return jnp.concatenate([rows[..., i * width : (i + 1) * width] for i in order], -1)


def to_relative(rows, shards, index):
    return flip_blocks(reverse_blocks(rows, shards), shards, index)


def from_relative(rows, shards, index):
    return reverse_blocks(flip_blocks(rows, shards, index), shards)


def swap(value, axis, bit):
    size = lax.axis_size(axis)
    return lax.ppermute(value, axis, [(i, i ^ bit) for i in range(size)])


def gather_rows(rows):
    for place in reversed(range(bits_of(lax.axis_size("shard")))):
        rows = jnp.concatenate([rows, swap(rows, "shard", 1 << place)], 0)
    return rows


def scatter_rows(rows):
    for place in range(bits_of(lax.axis_size("shard"))):
        half = rows.shape[0] // 2
        rows = rows[:half] + swap(rows[half:], "shard", 1 << place)
    return rows


def ring(value):
    size = lax.axis_size("tensor")
    return lax.ppermute(value, "tensor", [(i, (i + 1) % size) for i in range(size)])


def ring_gather(rows):
    pieces = [rows]
    for _ in range(lax.axis_size("tensor") - 1):
        pieces.append(ring(pieces[-1]))
    return pieces


def ring_scatter(pieces):
    total = pieces[1]
    for piece in pieces[2:] + pieces[:1]:
        total = piece + ring(total)
    return total


SEND_FIRST = [(0, 0), (1, 2), (2, 1), (3, 3)]
SEND_SECOND = [(0, 2), (1, 0), (2, 3), (3, 1)]


def one_sequence(block, odd):
    first = jnp.where(odd, block[1], block[0])
    second = jnp.where(odd, block[0], block[1])
    return jnp.concatenate(
        [
            lax.ppermute(first, "tensor", SEND_FIRST),
            lax.ppermute(second, "tensor", SEND_SECOND),
        ],
        0,
    )


def both_sequences(rows, odd):
    half = rows.shape[0] // 2
    first = lax.ppermute(rows[:half], "tensor", [(b, a) for a, b in SEND_FIRST])
    second = lax.ppermute(rows[half:], "tensor", [(b, a) for a, b in SEND_SECOND])
    return jnp.stack([jnp.where(odd, second, first), jnp.where(odd, first, second)])


def sum_group(rows):
    axes = ("context", "tensor")
    group = lax.axis_size(axes)
    count = rows.shape[0]
    chunk = -(-count // group)
    if chunk > 16:
        chunk = -(-chunk // 16) * 16
    padded = jnp.pad(rows, ((0, chunk * group - count), (0, 0)))
    parts = lax.all_to_all(padded, axes, split_axis=0, concat_axis=0, tiled=True)
    parts = parts.reshape(group, chunk, rows.shape[1]).astype(jnp.float32)
    total = jnp.sum(parts, axis=0).astype(jnp.bfloat16)
    spread = jnp.broadcast_to(total[None], (group,) + total.shape).reshape(padded.shape)
    return lax.all_to_all(spread, axes, split_axis=0, concat_axis=0, tiled=True)[:count]


def rope_tables(length):
    half = HEAD_SIZE // 2
    freq = np.float32(10000.0) ** (-np.arange(half).astype(np.float32) * 2.0 / HEAD_SIZE)
    angle = np.arange(length).astype(np.float32)[:, None] * freq.astype(np.float32)[None, :]
    cosine, sine = np.cos(angle), np.sin(angle)
    return np.concatenate([cosine, cosine, -sine, sine], 1).astype(np.float32)


def turn(head, table):
    half = HEAD_SIZE // 2
    swapped = jnp.concatenate([head[:, half:], head[:, :half]], 1)
    return head * table[:, :HEAD_SIZE] + swapped * table[:, HEAD_SIZE:]


def turn_back(head, table):
    half = HEAD_SIZE // 2
    swapped = jnp.concatenate([head[:, half:], head[:, :half]], 1)
    return head * table[:, :HEAD_SIZE] - swapped * table[:, HEAD_SIZE:]


def head_cols(index):
    return slice(index * HEAD_SIZE, (index + 1) * HEAD_SIZE)


def attend_kernel(q_ref, k_ref, v_ref, qt_ref, kt_ref, qp_ref, kp_ref, mix_ref, log_ref, qr_ref, kr_ref):
    allowed = kp_ref[...] <= qp_ref[...]
    allowed = jnp.concatenate([allowed.astype(jnp.int32)] * GROUP, 0) > 0
    rows = q_ref.shape[0]
    for g in range(KEY_VALUE_HEADS):
        key = turn(k_ref[:, head_cols(g)], kt_ref[...]).astype(jnp.bfloat16)
        kr_ref[:, head_cols(g)] = key
        value = v_ref[:, head_cols(g)]
        heads = []
        for i in range(GROUP):
            cols = head_cols(g * GROUP + i)
            head = turn(q_ref[:, cols], qt_ref[...]).astype(jnp.bfloat16)
            qr_ref[:, cols] = head
            heads.append(head)
        query = jnp.concatenate(heads, 0)
        scores = dot_rows(query, key) * HEAD_SIZE ** (-0.5)
        scores = jnp.where(allowed, scores, -1e30)
        peak = jnp.max(scores, axis=-1, keepdims=True)
        expd = jnp.exp(scores - peak)
        total = jnp.sum(expd, axis=-1, keepdims=True)
        probs = (expd / total).astype(jnp.bfloat16)
        mixed = dot(probs, value).astype(jnp.bfloat16)
        for i in range(GROUP):
            mix_ref[:, head_cols(g * GROUP + i)] = mixed[i * rows : (i + 1) * rows]
        log_ref[:, g : g + 1] = peak + jnp.log(total)


def attend(query, key, value, query_table, key_table, query_pos, key_pos):
    rows, keys = query.shape[0], key.shape[0]
    return pl.pallas_call(
        attend_kernel,
        out_shape=(
            jax.ShapeDtypeStruct(query.shape, jnp.bfloat16),
            jax.ShapeDtypeStruct((GROUP * rows, 8), jnp.float32),
            jax.ShapeDtypeStruct(query.shape, jnp.bfloat16),
            jax.ShapeDtypeStruct(key.shape, jnp.bfloat16),
        ),
        compiler_params=pltpu.CompilerParams(vmem_limit_bytes=KERNEL_VMEM),
        cost_estimate=pl.CostEstimate(
            flops=4 * rows * keys * QUERY_HEADS * HEAD_SIZE,
            transcendentals=rows * keys * QUERY_HEADS,
            bytes_accessed=4_000_000,
        ),
        name="attend",
    )(query, key, value, query_table, key_table, query_pos, key_pos)


def attend_back_kernel(
    q_ref, k_ref, v_ref, mix_ref, gm_ref, log_ref, qt_ref, kt_ref, qp_ref, kp_ref, gq_ref, gkv_ref
):
    allowed = kp_ref[...] <= qp_ref[...]
    allowed = jnp.concatenate([allowed.astype(jnp.int32)] * GROUP, 0) > 0
    rows = q_ref.shape[0]
    for g in range(KEY_VALUE_HEADS):
        key, value = k_ref[:, head_cols(g)], v_ref[:, head_cols(g)]
        each = [head_cols(g * GROUP + i) for i in range(GROUP)]
        query = jnp.concatenate([q_ref[:, cols] for cols in each], 0)
        mixed = jnp.concatenate([mix_ref[:, cols] for cols in each], 0)
        grad_mix = jnp.concatenate([gm_ref[:, cols] for cols in each], 0)
        scores = dot_rows(query, key) * HEAD_SIZE ** (-0.5)
        scores = jnp.where(allowed, scores, -1e30)
        probs = jnp.exp(scores - log_ref[:, g : g + 1])
        grad_probs = dot_rows(grad_mix, value)
        delta = jnp.sum(
            grad_mix.astype(jnp.float32) * mixed.astype(jnp.float32), axis=-1, keepdims=True
        )
        grad_scores = (probs * (grad_probs - delta) * HEAD_SIZE ** (-0.5)).astype(jnp.bfloat16)
        grad_query = dot(grad_scores, key)
        grad_key = dot_cols(grad_scores, query)
        grad_value = dot_cols(probs.astype(jnp.bfloat16), grad_mix)
        for i in range(GROUP):
            head = turn_back(grad_query[i * rows : (i + 1) * rows], qt_ref[...])
            gq_ref[:, each[i]] = head.astype(jnp.bfloat16)
        gkv_ref[:, head_cols(g)] = turn_back(grad_key, kt_ref[...]).astype(jnp.bfloat16)
        gkv_ref[:, head_cols(KEY_VALUE_HEADS + g)] = grad_value.astype(jnp.bfloat16)


def attend_back(query, key, value, mix, grad_mix, log_total, query_table, key_table, query_pos, key_pos):
    rows, keys = query.shape[0], key.shape[0]
    return pl.pallas_call(
        attend_back_kernel,
        out_shape=(
            jax.ShapeDtypeStruct(query.shape, jnp.bfloat16),
            jax.ShapeDtypeStruct((keys, 2 * key.shape[1]), jnp.bfloat16),
        ),
        compiler_params=pltpu.CompilerParams(vmem_limit_bytes=KERNEL_VMEM),
        cost_estimate=pl.CostEstimate(
            flops=10 * rows * keys * QUERY_HEADS * HEAD_SIZE,
            transcendentals=rows * keys * QUERY_HEADS,
            bytes_accessed=6_000_000,
        ),
        name="attend_back",
    )(query, key, value, mix, grad_mix, log_total, query_table, key_table, query_pos, key_pos)


def body(
    tokens,
    attn_gain,
    w_query,
    key_weight,
    value_weight,
    w_output,
    mlp_gain,
    w_gate,
    w_up,
    w_down,
    cotangent,
):
    _, length, width = tokens.shape
    shards, shard = lax.axis_size("shard"), lax.axis_index("shard")
    context, place = lax.axis_index("context"), lax.axis_index("tensor")
    places = lax.axis_size("tensor")
    rows = 2 * length
    odd = place % 2 == 1
    q_cols, kv_cols, hidden_cols = w_query.shape[1], key_weight.shape[1], w_gate.shape[1]

    sequence, half = place // 2, place % 2

    def blocks_of(which, part):
        first = which * places + 2 * part
        return [first + sequence, first + 1 - sequence]

    starts = [
        block * length
        for which in (context, 1 - context)
        for part in (half, 1 - half)
        for block in blocks_of(which, part)
    ]
    table = jnp.asarray(rope_tables(length * places * lax.axis_size("context")))
    key_table = jnp.concatenate([lax.dynamic_slice_in_dim(table, at, length, 0) for at in starts], 0)
    key_pos = jnp.concatenate([at + jnp.arange(length, dtype=jnp.int32) for at in starts])
    query_table, query_pos = key_table[:rows], key_pos[:rows, None]
    key_pos = key_pos[None, :]

    own = one_sequence(to_relative(tokens, shards, shard), odd)
    beside = swap(own, "tensor", 1)
    across = swap(own, "context", 1)
    across_beside = swap(after(beside, across), "context", 1)
    all_tokens = jnp.concatenate([own, beside, across, across_beside], 0)

    attn_local = jnp.concatenate([w_query, key_weight, value_weight], 1)
    mlp_local = jnp.concatenate([w_gate, w_up, w_down.T], 1)
    gains = gather_rows(jnp.concatenate([attn_gain[:, None], mlp_gain[:, None]], 1))
    gain_a, gain_m = gains[:, 0], gains[:, 1]
    attn_weight = gather_rows(attn_local)
    out_weight = gather_rows(after(w_output.T, attn_weight))
    mlp_weight = gather_rows(after(mlp_local, out_weight))
    w_q, w_kv = attn_weight[:, :q_cols], attn_weight[:, q_cols:]
    w_in, w_dn = mlp_weight[:, : 2 * hidden_cols], mlp_weight[:, 2 * hidden_cols :]

    own_cot = one_sequence(after(to_relative(cotangent, shards, shard), across_beside), odd)
    cot_group = jnp.concatenate(ring_gather(own_cot), 0)

    all_float = all_tokens.astype(jnp.float32)
    all_scale = rms_scale(all_float)
    all_normed = (all_float * all_scale * gain_a).astype(jnp.bfloat16)
    tokens_f, scale_a, normed_a = all_float[:rows], all_scale[:rows], all_normed[:rows]
    query = dot(normed_a, w_q)
    key_value = dot(all_normed, w_kv)
    key, value = key_value[:, :kv_cols], key_value[:, kv_cols:].astype(jnp.bfloat16)
    mix, log_total, query_rot, key_rot = attend(
        query, key, value, query_table, key_table, query_pos, key_pos
    )
    hidden = tokens_f + dot_rows(mix, out_weight)
    scale_m = rms_scale(hidden)
    normed_m = (hidden * scale_m * gain_m).astype(jnp.bfloat16)

    group = jnp.concatenate(ring_gather(normed_m), 0)
    grad_act = dot(cot_group, w_dn)
    inner = dot(group, w_in)
    gate, up_vals = inner[:, :hidden_cols], inner[:, hidden_cols:]
    sigma = jax.nn.sigmoid(gate)
    act = (gate * sigma * up_vals).astype(jnp.bfloat16)
    grad_up = (grad_act * gate * sigma).astype(jnp.bfloat16)
    grad_gate = (grad_act * up_vals * sigma * (1.0 + gate * (1.0 - sigma))).astype(jnp.bfloat16)
    grad_in = jnp.concatenate([grad_gate, grad_up], 1)
    back = dot_rows(grad_in, w_in).astype(jnp.bfloat16)
    grad_nm = ring_scatter([back[i * rows : (i + 1) * rows] for i in range(places)])
    grad_hidden = own_cot.astype(jnp.float32) + norm_back(
        grad_nm.astype(jnp.float32), hidden, scale_m, gain_m
    )
    grad_hidden_low = grad_hidden.astype(jnp.bfloat16)
    grad_mix = dot(grad_hidden_low, out_weight).astype(jnp.bfloat16)

    grad_query, grad_kv = attend_back(
        query_rot, key_rot, value, mix, grad_mix, log_total, query_table, key_table, query_pos, key_pos
    )
    pair = grad_kv[: 2 * rows] + swap(grad_kv[2 * rows :], "context", 1)
    own_kv = pair[:rows] + swap(pair[rows:], "tensor", 1)
    grad_na = dot_rows(grad_query, w_q) + dot_rows(own_kv, w_kv)
    grad_tokens = grad_hidden + norm_back(grad_na, tokens_f, scale_a, gain_a)
    grad_tokens = from_relative(grad_tokens.astype(jnp.bfloat16), shards, shard)
    tokens_grad = both_sequences(grad_tokens, odd)

    forward = dot_rows(act, w_dn).astype(jnp.bfloat16)
    forward = after(forward, grad_nm)
    mlp_out = ring_scatter([forward[i * rows : (i + 1) * rows] for i in range(places)])
    block = (hidden + mlp_out.astype(jnp.float32)).astype(jnp.bfloat16)
    block_out = both_sequences(from_relative(block, shards, shard), odd)

    mlp_term = jnp.concatenate(
        [dot_cols(group, grad_in).astype(jnp.bfloat16), dot_cols(cot_group, act).astype(jnp.bfloat16)], 1
    )
    mlp_term = scatter_rows(mlp_term)
    mlp_total = mlp_term.astype(jnp.float32) + swap(mlp_term, "context", 1).astype(jnp.float32)
    gate_total = mlp_total[:, :hidden_cols]
    up_total = mlp_total[:, hidden_cols : 2 * hidden_cols]
    down_total = mlp_total[:, 2 * hidden_cols :].T
    gain_m_total = jnp.sum(
        w_gate.astype(jnp.float32) * gate_total + w_up.astype(jnp.float32) * up_total, axis=1
    )
    for place_bit in range(bits_of(places)):
        gain_m_total = gain_m_total + swap(gain_m_total, "tensor", 1 << place_bit)
    gain_m_total = gain_m_total / mlp_gain

    out_term = scatter_rows(dot_cols(grad_hidden_low, mix).astype(jnp.bfloat16))
    out_total = sum_group(out_term).astype(jnp.float32).T
    attn_term = jnp.concatenate(
        [
            dot_cols(normed_a, grad_query).astype(jnp.bfloat16),
            dot_cols(all_normed, grad_kv).astype(jnp.bfloat16),
        ],
        1,
    )
    attn_total = sum_group(scatter_rows(attn_term)).astype(jnp.float32)
    gain_a_total = jnp.sum(attn_local.astype(jnp.float32) * attn_total, axis=1) / attn_gain
    return (
        block_out,
        tokens_grad,
        gain_a_total,
        attn_total[:, :q_cols],
        attn_total[:, q_cols : q_cols + kv_cols],
        attn_total[:, q_cols + kv_cols :],
        out_total,
        gain_m_total,
        gate_total,
        up_total,
        down_total,
    )


def solution(mesh):
    specs = (
        P("shard", ("context", "tensor"), None),
        P("shard"),
        P("shard", None),
        P("shard", None),
        P("shard", None),
        P(None, "shard"),
        P("shard"),
        P("shard", "tensor"),
        P("shard", "tensor"),
        P("tensor", "shard"),
    )
    return jax.shard_map(
        body,
        mesh=mesh,
        in_specs=specs + specs[:1],
        out_specs=specs[:1] + specs,
        check_vma=False,
    )
```

time: 752 us -> 354 us (0.47)
  blocking collectives: 123 us -> 0 us
  local copies, waits for them, and re-layouts: 149 us -> 27.9 us
  other arithmetic: 109 us -> 34.2 us
  waiting for transfers between devices: 229 us -> 176 us
  matrix products: 75.7 us -> 26.2 us
  starting transfers between devices: 37.8 us -> 59.9 us
  Pallas kernels: 0 us -> 21.6 us
  between operations: 16.2 us -> 2.17 us
    ppermute x0 -> x42, waiting for transfers between devices: none -> 159 us  [the longest x12 98.9 us: ring(): lax.ppermute(value, 'tensor', [(i, (i + 1) % size) for i in range(size)])]
    all_gather x7 -> x0, waiting for transfers between devices: 102 us -> none  [the longest x1 38.7 us: body(): lax.all_gather(cotangent, 'tensor', axis=1, tiled=True)]
    all_gather x4 -> x0, blocking collectives: 94.4 us -> none  [the longest x1 38 us: body(): lax.all_gather(value_low, ('context', 'tensor'), axis=1, tiled=True)]
    unnamed x102 -> x91, local copies, waits for them, and re-layouts: 85.5 us -> 13.3 us
    unnamed x7 -> x0, other arithmetic: 70.5 us -> none
    reduce_scatter x3 -> x0, waiting for transfers between devices: 61.2 us -> none  [the longest x1 34.8 us: body(): lax.psum_scatter(partial_out.astype(jnp.bfloat16), 'tensor', scatter_dime...]
    psum x2 -> x0, waiting for transfers between devices: 54.9 us -> none  [the longest x1 36.7 us: body(): lax.psum(owned_output.astype(jnp.bfloat16), ('context', 'tensor'))]
    convert_element_type x17 -> x0, local copies, waits for them, and re-layouts: 47.2 us -> none  [the longest x2 7.6 us: body(): local_key, local_value = (lax.psum_scatter(key_gradient.reshape(sequence_...]
  transfers between devices with their start and end apart: 22 -> 46, of which waited for: 10 -> 23; matrix products, arithmetic and copies ran while one was open for 42% -> 22% of each run, Pallas kernels for 0% -> 6%
where the time goes in v1:
time: 354 us; the launch traced here: 348 us
  waiting for transfers between devices  176 us (50%)
  starting transfers between devices  59.9 us (17%)
  other arithmetic  34.2 us (10%)
  local copies, waits for them, and re-layouts  27.9 us (8%)
  matrix products  26.2 us (7%)
  Pallas kernels  21.6 us (6%)
    ppermute x12, waiting for transfers between devices, ring(): lax.ppermute(value, 'tensor', [(i, (i + 1) % size) for i in range(size)])  98.9 us
    ppermute x22, waiting for transfers between devices, swap(): return lax.ppermute(value, axis, [(i, i ^ bit) for i in range(size)])  44.8 us
    ppermute x22, starting transfers between devices, swap(): return lax.ppermute(value, axis, [(i, i ^ bit) for i in range(size)])  22.2 us
    all_to_all x2, waiting for transfers between devices, sum_group(): lax.all_to_all(padded, axes, split_axis=0, concat_axis=0, tiled=True)  16.9 us
    ppermute x2, waiting for transfers between devices, both_sequences(): lax.ppermute(rows[half:], 'tensor', [(b, a) for a, b in SEND_SECOND])  14.8 us
    unnamed x91, local copies, waits for them, and re-layouts  13.3 us
    dot_general x5, matrix products, dot_rows(): lax.dot_general(left, right, (((1,), (1,)), ((), ())), preferred_element_...  11.5 us
    pallas_call x1, Pallas kernels, attend_back(): pl.pallas_call(attend_back_kernel, out_shape=(jax.ShapeDtypeStruct(query....  10.8 us
  transfers between devices with their start and end apart: 46, of which 23 were waited for; matrix products, arithmetic and copies ran while one was open for 22% of the time, Pallas kernels for 6%

profile of v1, /device:TPU:0, one launch (start us, length us, event | category | flops | bytes accessed | tf_op | source)
XLA Modules:
  0.0 347.6 jit_solution(1482750938285628504)
XLA Ops:
  27.3 7.5 %collective-permute-done.7 = bf16[240,1600]{1,0:T(8,128)(2,1)} collective-permute-done((bf16[240,1600]{1,0:T(8,128)(2,1)S(1)}, bf16[240,1600]{1,0:T(8,128)(2,1)}, u32[]{:S(2)}, u32[]{:S(2)}) %collective-permute-start.7) | collective-permute-done | bytes 768032 | tf_op jit(solution)/shard_map/ppermute | solution.py:81
  42.8 8.1 %collective-permute-done.4 = bf16[192,960]{1,0:T(8,128)(2,1)S(1)} collective-permute-done((bf16[192,960]{1,0:T(8,128)(2,1)}, bf16[192,960]{1,0:T(8,128)(2,1)S(1)}, u32[]{:S(2)}, u32[]{:S(2)}) %collective-permute-start.4) | collective-permute-done | bytes 368672 | tf_op jit(solution)/shard_map/ppermute | solution.py:81
  59.3 5.9 %collective-permute-start.18 = (bf16[192,960]{1,0:T(8,128)(2,1)S(1)}, bf16[192,960]{1,0:T(8,128)(2,1)S(1)}, u32[]{:S(2)}, u32[]{:S(2)}) collective-permute-start(bf16[192,960]{1,0:T(8,128)(2,1)S(1)} %get-tuple-element.115), channel_id=1, source_target_pairs={{0,1},{1,2},{2,3},{3,0},{4,5},{5,6},{6,7},{7,4},{8,9},{9,10},{10,1... | collective-permute-start | bytes 1105928 | tf_op jit(solution)/shard_map/ppermute | solution.py:99
  65.2 3.7 %collective-permute-done.9 = bf16[240,960]{0,1:T(8,128)(2,1)S(1)} collective-permute-done((bf16[240,960]{0,1:T(8,128)(2,1)S(1)}, bf16[240,960]{0,1:T(8,128)(2,1)S(1)}, u32[]{:S(2)}, u32[]{:S(2)}) %collective-permute-start.9) | collective-permute-done | bytes 460832 | tf_op jit(solution)/shard_map/ppermute | solution.py:81
  69.8 4.0 %collective-permute-done.18 = bf16[192,960]{1,0:T(8,128)(2,1)S(1)} collective-permute-done((bf16[192,960]{1,0:T(8,128)(2,1)S(1)}, bf16[192,960]{1,0:T(8,128)(2,1)S(1)}, u32[]{:S(2)}, u32[]{:S(2)}) %collective-permute-start.18) | collective-permute-done | bytes 368672 | tf_op jit(solution)/shard_map/ppermute | solution.py:99
  79.2 10.8 %attend.1 = (bf16[192,960]{1,0:T(8,128)(2,1)S(1)}, f32[576,8]{1,0:T(8,128)S(1)}, bf16[192,960]{1,0:T(8,128)(2,1)S(1)}, bf16[768,320]{1,0:T(8,128)(2,1)S(1)}) custom-call(f32[192,960]{1,0:T(8,128)S(1)} %fusion.8.q_ref, f32[768,320]{1,0:T(8,128)S(1)} %slice.359.k_ref, bf16[768,320]{1,0:T(8,128)(2,1)S(1)} %slice.498.v_ref, ...), custom_call_target="tpu_custom_call" | custom-call | flops 566231040 | bytes 4000000 | tf_op jit(solution)/shard_map/attend/pallas_call | solution.py:207
  94.3 12.1 %collective-permute-done.11 = bf16[192,960]{1,0:T(8,128)(2,1)S(1)} collective-permute-done((bf16[192,960]{1,0:T(8,128)(2,1)S(1)}, bf16[192,960]{1,0:T(8,128)(2,1)S(1)}, u32[]{:S(2)}, u32[]{:S(2)}) %collective-permute-start.11) | collective-permute-done | bytes 368672 | tf_op jit(solution)/shard_map/ppermute | solution.py:99
  107.8 13.3 %collective-permute-done.12 = bf16[192,960]{1,0:T(8,128)(2,1)S(1)} collective-permute-done((bf16[192,960]{1,0:T(8,128)(2,1)S(1)}, bf16[192,960]{1,0:T(8,128)(2,1)S(1)}, u32[]{:S(2)}, u32[]{:S(2)}) %collective-permute-start.12) | collective-permute-done | bytes 368672 | tf_op jit(solution)/shard_map/ppermute | solution.py:99
  121.5 10.5 %collective-permute-done.13 = bf16[192,960]{1,0:T(8,128)(2,1)S(1)} collective-permute-done((bf16[192,960]{1,0:T(8,128)(2,1)S(1)}, bf16[192,960]{1,0:T(8,128)(2,1)S(1)}, u32[]{:S(2)}, u32[]{:S(2)}) %collective-permute-start.13) | collective-permute-done | bytes 368672 | tf_op jit(solution)/shard_map/ppermute | solution.py:99
  139.8 8.5 %collective-permute-done.21 = bf16[192,960]{1,0:T(8,128)(2,1)S(1)} collective-permute-done((bf16[192,960]{1,0:T(8,128)(2,1)S(1)}, bf16[192,960]{1,0:T(8,128)(2,1)S(1)}, u32[]{:S(2)}, u32[]{:S(2)}) %collective-permute-start.21) | collective-permute-done | bytes 368672 | tf_op jit(solution)/shard_map/ppermute | solution.py:99
  150.6 7.9 %collective-permute-done.22 = bf16[192,960]{1,0:T(8,128)(2,1)S(1)} collective-permute-done((bf16[192,960]{1,0:T(8,128)(2,1)S(1)}, bf16[192,960]{1,0:T(8,128)(2,1)S(1)}, u32[]{:S(2)}, u32[]{:S(2)}) %collective-permute-start.22) | collective-permute-done | bytes 368672 | tf_op jit(solution)/shard_map/ppermute | solution.py:99
  160.2 9.2 %collective-permute-done.23 = bf16[192,960]{1,0:T(8,128)(2,1)S(1)} collective-permute-done((bf16[192,960]{1,0:T(8,128)(2,1)S(1)}, bf16[192,960]{1,0:T(8,128)(2,1)S(1)}, u32[]{:S(2)}, u32[]{:S(2)}) %collective-permute-start.23) | collective-permute-done | bytes 368672 | tf_op jit(solution)/shard_map/ppermute | solution.py:99
  169.8 12.2 %collective-permute-done.24 = bf16[192,960]{1,0:T(8,128)(2,1)S(1)} collective-permute-done((bf16[192,960]{1,0:T(8,128)(2,1)S(1)}, bf16[192,960]{1,0:T(8,128)(2,1)S(1)}, u32[]{:S(2)}, u32[]{:S(2)}) %collective-permute-start.24) | collective-permute-done | bytes 368672 | tf_op jit(solution)/shard_map/ppermute | solution.py:99
  182.1 12.9 %collective-permute-done.25 = bf16[192,960]{1,0:T(8,128)(2,1)S(1)} collective-permute-done((bf16[192,960]{1,0:T(8,128)(2,1)S(1)}, bf16[192,960]{1,0:T(8,128)(2,1)S(1)}, u32[]{:S(2)}, u32[]{:S(2)}) %collective-permute-start.25) | collective-permute-done | bytes 368672 | tf_op jit(solution)/shard_map/ppermute | solution.py:99
  196.8 8.4 %collective-permute-done.26 = bf16[192,960]{1,0:T(8,128)(2,1)S(1)} collective-permute-done((bf16[192,960]{1,0:T(8,128)(2,1)S(1)}, bf16[192,960]{1,0:T(8,128)(2,1)S(1)}, u32[]{:S(2)}, u32[]{:S(2)}) %collective-permute-start.26) | collective-permute-done | bytes 368672 | tf_op jit(solution)/shard_map/ppermute | solution.py:99
  207.7 10.8 %attend_back.1 = (bf16[192,960]{1,0:T(8,128)(2,1)S(1)}, bf16[768,640]{1,0:T(8,128)(2,1)S(1)}) custom-call(bf16[192,960]{1,0:T(8,128)(2,1)S(1)} %get-tuple-element.28.q_ref, bf16[768,320]{1,0:T(8,128)(2,1)S(1)} %get-tuple-element.29.k_ref, bf16[768,320]{1,0:T(8,128)(2,1)S(1)} %slice.498.v_ref, bf16[192,960]{1,0:T(8,128)(2,1)S(1)} %get-tuple-element.23.mix_ref, ...), custom_call_target="tpu_custom_call" | custom-call | flops 1415577600 | bytes 6000000 | tf_op jit(solution)/shard_map/attend_back/pallas_call | solution.py:257
  226.3 3.7 %collective-permute-done.29 = bf16[384,640]{1,0:T(8,128)(2,1)S(1)} collective-permute-done((bf16[384,640]{1,0:T(8,128)(2,1)S(1)}, bf16[384,640]{1,0:T(8,128)(2,1)S(1)}, u32[]{:S(2)}, u32[]{:S(2)}) %collective-permute-start.29) | collective-permute-done | bytes 491552 | tf_op jit(solution)/shard_map/ppermute | solution.py:81
  241.7 7.7 %collective-permute-done.36 = bf16[240,960]{0,1:T(8,128)(2,1)S(1)} collective-permute-done((bf16[240,960]{0,1:T(8,128)(2,1)S(1)}, bf16[240,960]{0,1:T(8,128)(2,1)S(1)}, u32[]{:S(2)}, u32[]{:S(2)}) %collective-permute-start.36) | collective-permute-done | bytes 460832 | tf_op jit(solution)/shard_map/ppermute | solution.py:81
  255.9 3.8 %multiply_reduce_fusion.2 = (f32[192]{0:T(256)S(1)}, f32[192,960]{1,0:T(8,128)}) fusion(f32[768,960]{1,0:T(8,128)} %copy-done.1, f32[192]{0:T(256)S(1)} %slice.313, f32[960]{0:T(1024)S(1)} %bitcast.55, f32[192,960]{1,0:T(8,128)} %fusion.24, bf16[192,960]{1,0:T(8,128)(2,1)S(1)} %get-tuple-element.31, bf16[960,1600]{1,0:T(8,128)(2,1)} %copy-done), kind=kOutput, calls=%fused_computation.59 | convolution fusion | flops 354815808 | bytes 4650240 | tf_op jit(solution)/shard_map/dot_general | solution.py:24
  274.7 14.4 %all-to-all-done = bf16[8,32,1600]{2,1,0:T(8,128)(2,1)S(1)} async-done(((bf16[8,32,1600]{2,1,0:T(8,128)(2,1)}), bf16[8,32,1600]{2,1,0:T(8,128)(2,1)S(1)}, u32[]{:S(2)}, u32[]{:S(2)}) %all-to-all-start) | async-done | bytes 819232 | tf_op jit(solution)/shard_map/all_to_all | solution.py:147
  297.3 14.8 %collective-permute-done.31 = bf16[96,960]{1,0:T(8,128)(2,1)S(1)} collective-permute-done((bf16[96,960]{1,0:T(8,128)(2,1)S(1)}, bf16[96,960]{1,0:T(8,128)(2,1)S(1)}, u32[]{:S(2)}, u32[]{:S(2)}) %collective-permute-start.31) | collective-permute-done | bytes 184352 | tf_op jit(solution)/shard_map/ppermute | solution.py:135
  315.3 4.8 %all-to-all-start.1 = ((bf16[8,32,1600]{2,1,0:T(8,128)(2,1)}), bf16[8,32,1600]{2,1,0:T(8,128)(2,1)S(1)}, u32[]{:S(2)}, u32[]{:S(2)}) async-start(bf16[8,32,1600]{2,1,0:T(8,128)(2,1)} %broadcast_in_dim.32), calls=%async_computation.1 | async-start | bytes 1703936 | tf_op jit(solution)/shard_map/all_to_all | solution.py:151
  325.9 7.0 %collective-permute-done.40 = f32[240]{0:T(256)S(1)} collective-permute-done((f32[240]{0:T(256)S(1)}, f32[240]{0:T(256)S(1)}, u32[]{:S(2)}, u32[]{:S(2)}) %collective-permute-start.40) | collective-permute-done | bytes 992 | tf_op jit(solution)/shard_map/ppermute | solution.py:81
  332.9 4.5 %collective-permute-start.41 = (f32[240]{0:T(256)S(1)}, f32[240]{0:T(256)S(1)}, u32[]{:S(2)}, u32[]{:S(2)}) collective-permute-start(f32[240]{0:T(256)S(1)} %add.284), channel_id=1, source_target_pairs={{0,2},{1,3},{2,0},{3,1},{4,6},{5,7},{6,4},{7,5},{8,10},{9,11},{10,... | collective-permute-start | bytes 2888 | tf_op jit(solution)/shard_map/ppermute | solution.py:81
  (283 shorter events, 138.9 us)
Async XLA Ops:
  1.9 19.1 %collective-permute-start.5 = (f32[240,2]{0,1:T(2,128)}, f32[240,2]{0,1:T(2,128)}, u32[]{:S(2)}, u32[]{:S(2)}) collective-permute-start(f32[240,2]{0,1:T(2,128)} %pad_maximum_fusion.21), channel_id=1, source_target_pairs={{0,16},{8,24},{16,0},{24,8},{1,17},{9,25},{17,1},{25,9},{2,18},{10... | collective-permute-start | bytes 5768 | tf_op jit(solution)/shard_map/ppermute | solution.py:81
  7.6 16.4 %collective-permute-start.1 = (bf16[96,960]{1,0:T(8,128)(2,1)}, bf16[96,960]{1,0:T(8,128)(2,1)S(1)}, u32[]{:S(2)}, u32[]{:S(2)}) collective-permute-start(bf16[96,960]{1,0:T(8,128)(2,1)} %get-tuple-element.107), channel_id=1, source_target_pairs={{0,2},{1,0},{2,3},{3,1},{4,6},{5,4},{6,7},{7,5},{8,10},{9,8},{10,1... | collective-permute-start | bytes 552968 | tf_op jit(solution)/shard_map/ppermute | solution.py:126
  14.0 20.9 %collective-permute-start.7 = (bf16[240,1600]{1,0:T(8,128)(2,1)S(1)}, bf16[240,1600]{1,0:T(8,128)(2,1)}, u32[]{:S(2)}, u32[]{:S(2)}) collective-permute-start(bf16[240,1600]{1,0:T(8,128)(2,1)S(1)} %concatenate.119), channel_id=1, source_target_pairs={{0,16},{8,24},{16,0},{24,8},{1,17},{9,25},{17,1},{25,9},{2,18},{10... | collective-permute-start | bytes 2304008 | tf_op jit(solution)/shard_map/ppermute | solution.py:81
  15.6 37.3 %collective-permute-start.14 = (bf16[240,1920]{1,0:T(8,128)(2,1)}, bf16[240,1920]{1,0:T(8,128)(2,1)}, u32[]{:S(2)}, u32[]{:S(2)}) collective-permute-start(bf16[240,1920]{1,0:T(8,128)(2,1)} %pad_maximum_fusion.11), channel_id=1, source_target_pairs={{0,16},{8,24},{16,0},{24,8},{1,17},{9,25},{17,1},{25,9},{2,18},{10... | collective-permute-start | bytes 2764808 | tf_op jit(solution)/shard_map/ppermute | solution.py:81
  22.4 15.9 %collective-permute-start.6 = (f32[480,2]{0,1:T(2,128)}, f32[480,2]{0,1:T(2,128)}, u32[]{:S(2)}, u32[]{:S(2)}) collective-permute-start(f32[480,2]{0,1:T(2,128)} %pad_maximum_fusion.20), channel_id=1, source_target_pairs={{0,8},{8,0},{16,24},{24,16},{1,9},{9,1},{17,25},{25,17},{2,10},{10... | collective-permute-start | bytes 11528 | tf_op jit(solution)/shard_map/ppermute | solution.py:81
  37.3 17.2 %collective-permute-start.8 = (bf16[480,1600]{1,0:T(8,128)(2,1)}, bf16[480,1600]{1,0:T(8,128)(2,1)}, u32[]{:S(2)}, u32[]{:S(2)}) collective-permute-start(bf16[480,1600]{1,0:T(8,128)(2,1)} %pad_maximum_fusion.6), channel_id=1, source_target_pairs={{0,8},{8,0},{16,24},{24,16},{1,9},{9,1},{17,25},{25,17},{2,10},{10... | collective-permute-start | bytes 4608008 | tf_op jit(solution)/shard_map/ppermute | solution.py:81
  57.4 63.7 %collective-permute-start.15 = (bf16[480,1920]{1,0:T(8,128)(2,1)S(1)}, bf16[480,1920]{1,0:T(8,128)(2,1)S(1)}, u32[]{:S(2)}, u32[]{:S(2)}) collective-permute-start(bf16[480,1920]{1,0:T(8,128)(2,1)S(1)} %pad_maximum_fusion.4), channel_id=1, source_target_pairs={{0,8},{8,0},{16,24},{24,16},{1,9},{9,1},{17,25},{25,17},{2,10},{10... | collective-permute-start | bytes 5529608 | tf_op jit(solution)/shard_map/ppermute | solution.py:81
  59.3 14.4 %collective-permute-start.18 = (bf16[192,960]{1,0:T(8,128)(2,1)S(1)}, bf16[192,960]{1,0:T(8,128)(2,1)S(1)}, u32[]{:S(2)}, u32[]{:S(2)}) collective-permute-start(bf16[192,960]{1,0:T(8,128)(2,1)S(1)} %get-tuple-element.115), channel_id=1, source_target_pairs={{0,1},{1,2},{2,3},{3,0},{4,5},{5,6},{6,7},{7,4},{8,9},{9,10},{10,1... | collective-permute-start | bytes 1105928 | tf_op jit(solution)/shard_map/ppermute | solution.py:99
  69.3 20.7 %collective-permute-start.10 = (bf16[480,960]{0,1:T(8,128)(2,1)S(1)}, bf16[480,960]{0,1:T(8,128)(2,1)}, u32[]{:S(2)}, u32[]{:S(2)}) collective-permute-start(bf16[480,960]{0,1:T(8,128)(2,1)S(1)} %pad_maximum_fusion.10), channel_id=1, source_target_pairs={{0,8},{8,0},{16,24},{24,16},{1,9},{9,1},{17,25},{25,17},{2,10},{10... | collective-permute-start | bytes 2764808 | tf_op jit(solution)/shard_map/ppermute | solution.py:81
  73.8 20.5 %collective-permute-start.19 = (bf16[192,960]{1,0:T(8,128)(2,1)S(1)}, bf16[192,960]{1,0:T(8,128)(2,1)S(1)}, u32[]{:S(2)}, u32[]{:S(2)}) collective-permute-start(bf16[192,960]{1,0:T(8,128)(2,1)S(1)} %collective-permute-done.18), channel_id=1, source_target_pairs={{0,1},{1,2},{2,3},{3,0},{4,5},{5,6},{6,7},{7,4},{8,9},{9,10},{10,1... | collective-permute-start | bytes 1105928 | tf_op jit(solution)/shard_map/ppermute | solution.py:99
  94.3 26.9 %collective-permute-start.20 = (bf16[192,960]{1,0:T(8,128)(2,1)S(1)}, bf16[192,960]{1,0:T(8,128)(2,1)S(1)}, u32[]{:S(2)}, u32[]{:S(2)}) collective-permute-start(bf16[192,960]{1,0:T(8,128)(2,1)S(1)} %collective-permute-done.19), channel_id=1, source_target_pairs={{0,1},{1,2},{2,3},{3,0},{4,5},{5,6},{6,7},{7,4},{8,9},{9,10},{10,1... | collective-permute-start | bytes 1105928 | tf_op jit(solution)/shard_map/ppermute | solution.py:99
  106.5 14.7 %collective-permute-start.12 = (bf16[192,960]{1,0:T(8,128)(2,1)S(1)}, bf16[192,960]{1,0:T(8,128)(2,1)S(1)}, u32[]{:S(2)}, u32[]{:S(2)}) collective-permute-start(bf16[192,960]{1,0:T(8,128)(2,1)S(1)} %collective-permute-done.11), channel_id=1, source_target_pairs={{0,1},{1,2},{2,3},{3,0},{4,5},{5,6},{6,7},{7,4},{8,9},{9,10},{10,1... | collective-permute-start | bytes 1105928 | tf_op jit(solution)/shard_map/ppermute | solution.py:99
  158.7 36.9 %collective-permute-start.37 = (bf16[480,1920]{1,0:T(8,128)(2,1)S(1)}, bf16[480,1920]{1,0:T(8,128)(2,1)S(1)}, u32[]{:S(2)}, u32[]{:S(2)}) collective-permute-start(bf16[480,1920]{1,0:T(8,128)(2,1)S(1)} %pad_maximum_fusion.3), channel_id=1, source_target_pairs={{0,8},{8,0},{16,24},{24,16},{1,9},{9,1},{17,25},{25,17},{2,10},{10... | collective-permute-start | bytes 5529608 | tf_op jit(solution)/shard_map/ppermute | solution.py:81
  196.2 36.9 %collective-permute-start.38 = (bf16[240,1920]{1,0:T(8,128)(2,1)S(1)}, bf16[240,1920]{1,0:T(8,128)(2,1)S(1)}, u32[]{:S(2)}, u32[]{:S(2)}) collective-permute-start(bf16[240,1920]{1,0:T(8,128)(2,1)S(1)} %slice.414), channel_id=1, source_target_pairs={{0,16},{8,24},{16,0},{24,8},{1,17},{9,25},{17,1},{25,9},{2,18},{10... | collective-permute-start | bytes 2764808 | tf_op jit(solution)/shard_map/ppermute | solution.py:81
  226.3 71.0 %collective-permute-start.27 = (bf16[96,960]{1,0:T(8,128)(2,1)}, bf16[96,960]{1,0:T(8,128)(2,1)}, u32[]{:S(2)}, u32[]{:S(2)}) collective-permute-start(bf16[96,960]{1,0:T(8,128)(2,1)} %get-tuple-element.84), channel_id=1, source_target_pairs={{2,0},{0,1},{3,2},{1,3},{6,4},{4,5},{7,6},{5,7},{10,8},{8,9},{11,1... | collective-permute-start | bytes 552968 | tf_op jit(solution)/shard_map/ppermute | solution.py:135
  230.0 67.3 %collective-permute-start.28 = (bf16[96,960]{1,0:T(8,128)(2,1)}, bf16[96,960]{1,0:T(8,128)(2,1)}, u32[]{:S(2)}, u32[]{:S(2)}) collective-permute-start(bf16[96,960]{1,0:T(8,128)(2,1)} %get-tuple-element.85), channel_id=1, source_target_pairs={{0,0},{2,1},{1,2},{3,3},{4,4},{6,5},{5,6},{7,7},{8,8},{10,9},{9,10... | collective-permute-start | bytes 552968 | tf_op jit(solution)/shard_map/ppermute | solution.py:134
  233.3 86.9 %collective-permute-start.39 = (bf16[240,1920]{1,0:T(8,128)(2,1)S(1)}, bf16[240,1920]{1,0:T(8,128)(2,1)}, u32[]{:S(2)}, u32[]{:S(2)}) collective-permute-start(bf16[240,1920]{1,0:T(8,128)(2,1)S(1)} %slice_add_fusion.1), channel_id=1, source_target_pairs={{0,4},{4,0},{1,5},{5,1},{2,6},{6,2},{3,7},{7,3},{8,12},{12,8},{9,1... | collective-permute-start | bytes 2764808 | tf_op jit(solution)/shard_map/ppermute | solution.py:81
  239.5 22.7 %collective-permute-start.34 = (bf16[240,1600]{1,0:T(8,128)(2,1)}, bf16[240,1600]{1,0:T(8,128)(2,1)}, u32[]{:S(2)}, u32[]{:S(2)}) collective-permute-start(bf16[240,1600]{1,0:T(8,128)(2,1)} %slice.401), channel_id=1, source_target_pairs={{0,16},{8,24},{16,0},{24,8},{1,17},{9,25},{17,1},{25,9},{2,18},{10... | collective-permute-start | bytes 2304008 | tf_op jit(solution)/shard_map/ppermute | solution.py:81
  252.4 14.6 %all-to-all-start.2 = ((bf16[8,32,960]{2,1,0:T(8,128)(2,1)}), bf16[8,32,960]{2,1,0:T(8,128)(2,1)S(1)}, u32[]{:S(2)}, u32[]{:S(2)}) async-start(bf16[8,32,960]{2,1,0:T(8,128)(2,1)} %bitcast.17), calls=%async_computation.2 | async-start | bytes 1048576 | tf_op jit(solution)/shard_map/all_to_all | solution.py:147
  267.8 21.3 %all-to-all-start = ((bf16[8,32,1600]{2,1,0:T(8,128)(2,1)}), bf16[8,32,1600]{2,1,0:T(8,128)(2,1)S(1)}, u32[]{:S(2)}, u32[]{:S(2)}) async-start(bf16[8,32,1600]{2,1,0:T(8,128)(2,1)} %bitcast.44), calls=%async_computation | async-start | bytes 1703936 | tf_op jit(solution)/shard_map/all_to_all | solution.py:147
  290.8 23.5 %all-to-all-start.3 = ((bf16[8,32,960]{2,1,0:T(8,128)(2,1)}), bf16[8,32,960]{2,1,0:T(8,128)(2,1)S(1)}, u32[]{:S(2)}, u32[]{:S(2)}) async-start(bf16[8,32,960]{2,1,0:T(8,128)(2,1)} %broadcast_in_dim.33), calls=%async_computation.3 | async-start | bytes 1048576 | tf_op jit(solution)/shard_map/all_to_all | solution.py:151
  294.7 17.5 %collective-permute-start.31 = (bf16[96,960]{1,0:T(8,128)(2,1)S(1)}, bf16[96,960]{1,0:T(8,128)(2,1)S(1)}, u32[]{:S(2)}, u32[]{:S(2)}) collective-permute-start(bf16[96,960]{1,0:T(8,128)(2,1)S(1)} %get-tuple-element.70), channel_id=1, source_target_pairs={{2,0},{0,1},{3,2},{1,3},{6,4},{4,5},{7,6},{5,7},{10,8},{8,9},{11,1... | collective-permute-start | bytes 552968 | tf_op jit(solution)/shard_map/ppermute | solution.py:135
  296.7 15.5 %collective-permute-start.32 = (bf16[96,960]{1,0:T(8,128)(2,1)S(1)}, bf16[96,960]{1,0:T(8,128)(2,1)S(1)}, u32[]{:S(2)}, u32[]{:S(2)}) collective-permute-start(bf16[96,960]{1,0:T(8,128)(2,1)S(1)} %get-tuple-element.71), channel_id=1, source_target_pairs={{0,0},{2,1},{1,2},{3,3},{4,4},{6,5},{5,6},{7,7},{8,8},{10,9},{9,10... | collective-permute-start | bytes 552968 | tf_op jit(solution)/shard_map/ppermute | solution.py:134
  315.3 28.0 %all-to-all-start.1 = ((bf16[8,32,1600]{2,1,0:T(8,128)(2,1)}), bf16[8,32,1600]{2,1,0:T(8,128)(2,1)S(1)}, u32[]{:S(2)}, u32[]{:S(2)}) async-start(bf16[8,32,1600]{2,1,0:T(8,128)(2,1)} %broadcast_in_dim.32), calls=%async_computation.1 | async-start | bytes 1703936 | tf_op jit(solution)/shard_map/all_to_all | solution.py:151
  (57 other events, 695.4 us)

commit v2 on v1

--- a/solution.py
+++ b/solution.py
@@ -1,5 +1,3 @@
-import functools
-
 import jax
 import jax.numpy as jnp
 import numpy as np
@@ -12,6 +10,7 @@
 KEY_VALUE_HEADS = 5
 HEAD_SIZE = 64
 GROUP = QUERY_HEADS // KEY_VALUE_HEADS
+SCALE = HEAD_SIZE ** (-0.5)
 EPS = 1e-05
 KERNEL_VMEM = 40 * 1024 * 1024
 
@@ -81,62 +80,44 @@
     return lax.ppermute(value, axis, [(i, i ^ bit) for i in range(size)])
 
 
+def gather_pieces(rows, gate=None):
+    pieces = [rows]
+    for place in reversed(range(bits_of(lax.axis_size("shard")))):
+        if len(pieces) > 2:
+            pieces = [jnp.concatenate(pieces, 0)]
+        sent = pieces if gate is None else [after(piece, *gate) for piece in pieces]
+        gate = None
+        pieces = pieces + [swap(piece, "shard", 1 << place) for piece in sent]
+    return pieces
+
+
 def gather_rows(rows):
-    for place in reversed(range(bits_of(lax.axis_size("shard")))):
-        rows = jnp.concatenate([rows, swap(rows, "shard", 1 << place)], 0)
-    return rows
-
-
-def scatter_rows(rows):
-    for place in range(bits_of(lax.axis_size("shard"))):
+    return jnp.concatenate(gather_pieces(rows), 0)
+
+
+def scatter_rows(rows, first, last):
+    for place in range(first, last):
         half = rows.shape[0] // 2
         rows = rows[:half] + swap(rows[half:], "shard", 1 << place)
     return rows
 
 
-def ring(value):
+def shift(value, count):
     size = lax.axis_size("tensor")
-    return lax.ppermute(value, "tensor", [(i, (i + 1) % size) for i in range(size)])
-
-
-def ring_gather(rows):
-    pieces = [rows]
-    for _ in range(lax.axis_size("tensor") - 1):
-        pieces.append(ring(pieces[-1]))
-    return pieces
-
-
-def ring_scatter(pieces):
-    total = pieces[1]
-    for piece in pieces[2:] + pieces[:1]:
-        total = piece + ring(total)
-    return total
-
-
-SEND_FIRST = [(0, 0), (1, 2), (2, 1), (3, 3)]
-SEND_SECOND = [(0, 2), (1, 0), (2, 3), (3, 1)]
-
-
-def one_sequence(block, odd):
-    first = jnp.where(odd, block[1], block[0])
-    second = jnp.where(odd, block[0], block[1])
-    return jnp.concatenate(
-        [
-            lax.ppermute(first, "tensor", SEND_FIRST),
-            lax.ppermute(second, "tensor", SEND_SECOND),
-        ],
-        0,
-    )
-
-
-def both_sequences(rows, odd):
-    half = rows.shape[0] // 2
-    first = lax.ppermute(rows[:half], "tensor", [(b, a) for a, b in SEND_FIRST])
-    second = lax.ppermute(rows[half:], "tensor", [(b, a) for a, b in SEND_SECOND])
-    return jnp.stack([jnp.where(odd, second, first), jnp.where(odd, first, second)])
-
-
-def sum_group(rows):
+    return lax.ppermute(value, "tensor", [(i, (i + count) % size) for i in range(size)])
+
+
+def one_sequence(block, upper):
+    mine = jnp.where(upper, block[1], block[0])
+    other = jnp.where(upper, block[0], block[1])
+    return jnp.concatenate([mine, swap(other, "tensor", 2)], 0)
+
+
+def both_sequences(mine, other, upper):
+    return jnp.stack([jnp.where(upper, other, mine), jnp.where(upper, mine, other)])
+
+
+def group_sum_parts(rows):
     axes = ("context", "tensor")
     group = lax.axis_size(axes)
     count = rows.shape[0]
@@ -146,8 +127,14 @@
     padded = jnp.pad(rows, ((0, chunk * group - count), (0, 0)))
     parts = lax.all_to_all(padded, axes, split_axis=0, concat_axis=0, tiled=True)
     parts = parts.reshape(group, chunk, rows.shape[1]).astype(jnp.float32)
-    total = jnp.sum(parts, axis=0).astype(jnp.bfloat16)
-    spread = jnp.broadcast_to(total[None], (group,) + total.shape).reshape(padded.shape)
+    return jnp.sum(parts, axis=0).astype(jnp.bfloat16)
+
+
+def group_collect(part, count):
+    axes = ("context", "tensor")
+    group = lax.axis_size(axes)
+    spread = jnp.broadcast_to(part[None], (group,) + part.shape)
+    spread = spread.reshape(group * part.shape[0], part.shape[1])
     return lax.all_to_all(spread, axes, split_axis=0, concat_axis=0, tiled=True)[:count]
 
 
@@ -176,8 +163,8 @@
 
 
 def attend_kernel(q_ref, k_ref, v_ref, qt_ref, kt_ref, qp_ref, kp_ref, mix_ref, log_ref, qr_ref, kr_ref):
-    allowed = kp_ref[...] <= qp_ref[...]
-    allowed = jnp.concatenate([allowed.astype(jnp.int32)] * GROUP, 0) > 0
+    hidden = jnp.where(kp_ref[...] <= qp_ref[...], 0.0, -1e30)
+    hidden = jnp.concatenate([hidden] * GROUP, 0)
     rows = q_ref.shape[0]
     for g in range(KEY_VALUE_HEADS):
         key = turn(k_ref[:, head_cols(g)], kt_ref[...]).astype(jnp.bfloat16)
@@ -186,17 +173,15 @@
         heads = []
         for i in range(GROUP):
             cols = head_cols(g * GROUP + i)
-            head = turn(q_ref[:, cols], qt_ref[...]).astype(jnp.bfloat16)
+            head = turn(q_ref[:, cols], qt_ref[...]).astype(jnp.bfloat16) * SCALE
             qr_ref[:, cols] = head
             heads.append(head)
         query = jnp.concatenate(heads, 0)
-        scores = dot_rows(query, key) * HEAD_SIZE ** (-0.5)
-        scores = jnp.where(allowed, scores, -1e30)
+        scores = dot_rows(query, key) + hidden
         peak = jnp.max(scores, axis=-1, keepdims=True)
         expd = jnp.exp(scores - peak)
         total = jnp.sum(expd, axis=-1, keepdims=True)
-        probs = (expd / total).astype(jnp.bfloat16)
-        mixed = dot(probs, value).astype(jnp.bfloat16)
+        mixed = (dot(expd.astype(jnp.bfloat16), value) / total).astype(jnp.bfloat16)
         for i in range(GROUP):
             mix_ref[:, head_cols(g * GROUP + i)] = mixed[i * rows : (i + 1) * rows]
         log_ref[:, g : g + 1] = peak + jnp.log(total)
@@ -225,8 +210,8 @@
 def attend_back_kernel(
     q_ref, k_ref, v_ref, mix_ref, gm_ref, log_ref, qt_ref, kt_ref, qp_ref, kp_ref, gq_ref, gkv_ref
 ):
-    allowed = kp_ref[...] <= qp_ref[...]
-    allowed = jnp.concatenate([allowed.astype(jnp.int32)] * GROUP, 0) > 0
+    hidden = jnp.where(kp_ref[...] <= qp_ref[...], 0.0, -1e30)
+    hidden = jnp.concatenate([hidden] * GROUP, 0)
     rows = q_ref.shape[0]
     for g in range(KEY_VALUE_HEADS):
         key, value = k_ref[:, head_cols(g)], v_ref[:, head_cols(g)]
@@ -234,15 +219,14 @@
         query = jnp.concatenate([q_ref[:, cols] for cols in each], 0)
         mixed = jnp.concatenate([mix_ref[:, cols] for cols in each], 0)
         grad_mix = jnp.concatenate([gm_ref[:, cols] for cols in each], 0)
-        scores = dot_rows(query, key) * HEAD_SIZE ** (-0.5)
-        scores = jnp.where(allowed, scores, -1e30)
+        scores = dot_rows(query, key) + hidden
         probs = jnp.exp(scores - log_ref[:, g : g + 1])
         grad_probs = dot_rows(grad_mix, value)
         delta = jnp.sum(
             grad_mix.astype(jnp.float32) * mixed.astype(jnp.float32), axis=-1, keepdims=True
         )
-        grad_scores = (probs * (grad_probs - delta) * HEAD_SIZE ** (-0.5)).astype(jnp.bfloat16)
-        grad_query = dot(grad_scores, key)
+        grad_scores = (probs * (grad_probs - delta)).astype(jnp.bfloat16)
+        grad_query = dot(grad_scores, key) * SCALE
         grad_key = dot_cols(grad_scores, query)
         grad_value = dot_cols(probs.astype(jnp.bfloat16), grad_mix)
         for i in range(GROUP):
@@ -288,20 +272,13 @@
     context, place = lax.axis_index("context"), lax.axis_index("tensor")
     places = lax.axis_size("tensor")
     rows = 2 * length
-    odd = place % 2 == 1
+    upper = place // 2 == 1
     q_cols, kv_cols, hidden_cols = w_query.shape[1], key_weight.shape[1], w_gate.shape[1]
 
-    sequence, half = place // 2, place % 2
-
-    def blocks_of(which, part):
-        first = which * places + 2 * part
-        return [first + sequence, first + 1 - sequence]
-
     starts = [
-        block * length
+        (which * places + (place ^ step)) * length
         for which in (context, 1 - context)
-        for part in (half, 1 - half)
-        for block in blocks_of(which, part)
+        for step in (0, 2, 1, 3)
     ]
     table = jnp.asarray(rope_tables(length * places * lax.axis_size("context")))
     key_table = jnp.concatenate([lax.dynamic_slice_in_dim(table, at, length, 0) for at in starts], 0)
@@ -309,7 +286,7 @@
     query_table, query_pos = key_table[:rows], key_pos[:rows, None]
     key_pos = key_pos[None, :]
 
-    own = one_sequence(to_relative(tokens, shards, shard), odd)
+    own = one_sequence(to_relative(tokens, shards, shard), upper)
     beside = swap(own, "tensor", 1)
     across = swap(own, "context", 1)
     across_beside = swap(after(beside, across), "context", 1)
@@ -317,16 +294,22 @@
 
     attn_local = jnp.concatenate([w_query, key_weight, value_weight], 1)
     mlp_local = jnp.concatenate([w_gate, w_up, w_down.T], 1)
+    attn_pieces = gather_pieces(attn_local)
     gains = gather_rows(jnp.concatenate([attn_gain[:, None], mlp_gain[:, None]], 1))
     gain_a, gain_m = gains[:, 0], gains[:, 1]
-    attn_weight = gather_rows(attn_local)
-    out_weight = gather_rows(after(w_output.T, attn_weight))
-    mlp_weight = gather_rows(after(mlp_local, out_weight))
+    out_pieces = gather_pieces(w_output.T, attn_pieces[1:2])
+    mlp_pieces = gather_pieces(mlp_local, out_pieces[1:2])
+    attn_weight = jnp.concatenate(attn_pieces, 0)
+    out_weight = jnp.concatenate(out_pieces, 0)
+    mlp_weight = jnp.concatenate(mlp_pieces, 0)
     w_q, w_kv = attn_weight[:, :q_cols], attn_weight[:, q_cols:]
     w_in, w_dn = mlp_weight[:, : 2 * hidden_cols], mlp_weight[:, 2 * hidden_cols :]
 
-    own_cot = one_sequence(after(to_relative(cotangent, shards, shard), across_beside), odd)
-    cot_group = jnp.concatenate(ring_gather(own_cot), 0)
+    cots = [after(to_relative(cotangent, shards, shard), beside)]
+    cots.append(shift(cots[0], 1))
+    cots = [after(cots[0], cots[1]), cots[1], shift(cots[1], 1)]
+    cots.append(shift(cots[0], -1))
+    all_tokens = after(all_tokens, cots[1])
 
     all_float = all_tokens.astype(jnp.float32)
     all_scale = rms_scale(all_float)
@@ -342,56 +325,60 @@
     scale_m = rms_scale(hidden)
     normed_m = (hidden * scale_m * gain_m).astype(jnp.bfloat16)
 
-    group = jnp.concatenate(ring_gather(normed_m), 0)
-    grad_act = dot(cot_group, w_dn)
-    inner = dot(group, w_in)
-    gate, up_vals = inner[:, :hidden_cols], inner[:, hidden_cols:]
-    sigma = jax.nn.sigmoid(gate)
-    act = (gate * sigma * up_vals).astype(jnp.bfloat16)
-    grad_up = (grad_act * gate * sigma).astype(jnp.bfloat16)
-    grad_gate = (grad_act * up_vals * sigma * (1.0 + gate * (1.0 - sigma))).astype(jnp.bfloat16)
-    grad_in = jnp.concatenate([grad_gate, grad_up], 1)
-    back = dot_rows(grad_in, w_in).astype(jnp.bfloat16)
-    grad_nm = ring_scatter([back[i * rows : (i + 1) * rows] for i in range(places)])
+    normed_m, cots[2], cots[3] = lax.optimization_barrier((normed_m, cots[2], cots[3]))
+
+    def cot_of(k):
+        above = ((place - k) % places) // 2 == 1
+        pair = (cots[k], cots[(k + 2) % places])
+        return jnp.concatenate([jnp.where(above, one[1], one[0]) for one in pair], 0)
+
+    cots = [cot_of(k) for k in range(places)]
+    own_cot = cots[0]
+    barrier = lax.optimization_barrier
+
+    group, acts, grads_in, backs = [normed_m], [], [], []
+    arriving = shift(normed_m, 1)
+    for k, cot in enumerate(cots):
+        if k > 0:
+            group.append(arriving)
+            if k + 1 < places:
+                arriving = shift(after(arriving, backs[-1]), 1)
+        rows_in = group[k]
+        grad_act = dot(cot, w_dn)
+        inner = dot(rows_in, w_in)
+        gate, up_vals = inner[:, :hidden_cols], inner[:, hidden_cols:]
+        sigma = jax.nn.sigmoid(gate)
+        acts.append((gate * sigma * up_vals).astype(jnp.bfloat16))
+        grad_up = (grad_act * gate * sigma).astype(jnp.bfloat16)
+        grad_gate = (grad_act * up_vals * sigma * (1.0 + gate * (1.0 - sigma))).astype(jnp.bfloat16)
+        grads_in.append(jnp.concatenate([grad_gate, grad_up], 1))
+        backs.append(dot_rows(grads_in[-1], w_in).astype(jnp.bfloat16))
+    grad_nm = backs[1]
+    for k in [*range(2, places), 0]:
+        grad_nm = backs[k] + shift(grad_nm, 1)
     grad_hidden = own_cot.astype(jnp.float32) + norm_back(
         grad_nm.astype(jnp.float32), hidden, scale_m, gain_m
     )
     grad_hidden_low = grad_hidden.astype(jnp.bfloat16)
     grad_mix = dot(grad_hidden_low, out_weight).astype(jnp.bfloat16)
 
+    bits = bits_of(shards)
+    group, grad_in = jnp.concatenate(group, 0), jnp.concatenate(grads_in, 0)
+    act, cot_group = jnp.concatenate(acts, 0), jnp.concatenate(cots, 0)
+    mlp_term = jnp.concatenate(
+        [dot_cols(group, grad_in).astype(jnp.bfloat16), dot_cols(cot_group, act).astype(jnp.bfloat16)], 1
+    )
+    mlp_term = scatter_rows(mlp_term, 0, bits)
+    out_term = scatter_rows(dot_cols(grad_hidden_low, mix).astype(jnp.bfloat16), 0, 1)
+    forward = [dot_rows(act, w_dn).astype(jnp.bfloat16) for act in acts]
+    total = shift(after(forward[1], grad_mix), 1)
+
     grad_query, grad_kv = attend_back(
         query_rot, key_rot, value, mix, grad_mix, log_total, query_table, key_table, query_pos, key_pos
     )
-    pair = grad_kv[: 2 * rows] + swap(grad_kv[2 * rows :], "context", 1)
-    own_kv = pair[:rows] + swap(pair[rows:], "tensor", 1)
-    grad_na = dot_rows(grad_query, w_q) + dot_rows(own_kv, w_kv)
-    grad_tokens = grad_hidden + norm_back(grad_na, tokens_f, scale_a, gain_a)
-    grad_tokens = from_relative(grad_tokens.astype(jnp.bfloat16), shards, shard)
-    tokens_grad = both_sequences(grad_tokens, odd)
-
-    forward = dot_rows(act, w_dn).astype(jnp.bfloat16)
-    forward = after(forward, grad_nm)
-    mlp_out = ring_scatter([forward[i * rows : (i + 1) * rows] for i in range(places)])
-    block = (hidden + mlp_out.astype(jnp.float32)).astype(jnp.bfloat16)
-    block_out = both_sequences(from_relative(block, shards, shard), odd)
-
-    mlp_term = jnp.concatenate(
-        [dot_cols(group, grad_in).astype(jnp.bfloat16), dot_cols(cot_group, act).astype(jnp.bfloat16)], 1
-    )
-    mlp_term = scatter_rows(mlp_term)
-    mlp_total = mlp_term.astype(jnp.float32) + swap(mlp_term, "context", 1).astype(jnp.float32)
-    gate_total = mlp_total[:, :hidden_cols]
-    up_total = mlp_total[:, hidden_cols : 2 * hidden_cols]
-    down_total = mlp_total[:, 2 * hidden_cols :].T
-    gain_m_total = jnp.sum(
-        w_gate.astype(jnp.float32) * gate_total + w_up.astype(jnp.float32) * up_total, axis=1
-    )
-    for place_bit in range(bits_of(places)):
-        gain_m_total = gain_m_total + swap(gain_m_total, "tensor", 1 << place_bit)
-    gain_m_total = gain_m_total / mlp_gain
-
-    out_term = scatter_rows(dot_cols(grad_hidden_low, mix).astype(jnp.bfloat16))
-    out_total = sum_group(out_term).astype(jnp.float32).T
+    grad_query, grad_kv, mlp_term, out_term, total = barrier(
+        (grad_query, grad_kv, mlp_term, out_term, total)
+    )
     attn_term = jnp.concatenate(
         [
             dot_cols(normed_a, grad_query).astype(jnp.bfloat16),
@@ -399,8 +386,42 @@
         ],
         1,
     )
-    attn_total = sum_group(scatter_rows(attn_term)).astype(jnp.float32)
+    attn_term = scatter_rows(attn_term, 0, bits)
+    out_term = scatter_rows(out_term, 1, bits)
+    pair = grad_kv[: 2 * rows] + swap(grad_kv[2 * rows :], "context", 1)
+    total = shift(forward[2] + total, 1)
+    mlp_across = swap(mlp_term, "context", 1)
+    attn_term, out_term, pair, total, mlp_across = barrier(
+        (attn_term, out_term, pair, total, mlp_across)
+    )
+
+    attn_part, out_part = group_sum_parts(attn_term), group_sum_parts(out_term)
+    own_kv = pair[:rows] + swap(pair[rows:], "tensor", 1)
+    grad_na = dot_rows(grad_query, w_q) + dot_rows(own_kv, w_kv)
+    grad_tokens = grad_hidden + norm_back(grad_na, tokens_f, scale_a, gain_a)
+    grad_tokens = from_relative(grad_tokens.astype(jnp.bfloat16), shards, shard)
+    total = shift(forward[3] + total, 1)
+    block = hidden + forward[0].astype(jnp.float32) + total.astype(jnp.float32)
+    block = from_relative(block.astype(jnp.bfloat16), shards, shard)
+    attn_part, out_part, grad_tokens, block = barrier((attn_part, out_part, grad_tokens, block))
+
+    back_rows = swap(jnp.concatenate([block[length:], grad_tokens[length:]], 0), "tensor", 2)
+    block_out = both_sequences(block[:length], back_rows[:length], upper)
+    tokens_grad = both_sequences(grad_tokens[:length], back_rows[length:], upper)
+    out_total = group_collect(out_part, out_term.shape[0]).astype(jnp.float32).T
+    attn_total = group_collect(attn_part, attn_term.shape[0]).astype(jnp.float32)
     gain_a_total = jnp.sum(attn_local.astype(jnp.float32) * attn_total, axis=1) / attn_gain
+
+    mlp_total = mlp_term.astype(jnp.float32) + mlp_across.astype(jnp.float32)
+    gate_total = mlp_total[:, :hidden_cols]
+    up_total = mlp_total[:, hidden_cols : 2 * hidden_cols]
+    down_total = mlp_total[:, 2 * hidden_cols :].T
+    gain_m_total = jnp.sum(
+        w_gate.astype(jnp.float32) * gate_total + w_up.astype(jnp.float32) * up_total, axis=1
+    )
+    for place_bit in range(bits_of(places)):
+        gain_m_total = gain_m_total + swap(gain_m_total, "tensor", 1 << place_bit)
+    gain_m_total = gain_m_total / mlp_gain
     return (
         block_out,
         tokens_grad,

time: 354 us -> 349 us (0.986)
  blocking collectives: 0 us -> 17.4 us
  starting transfers between devices: 59.9 us -> 46.9 us
  local copies, waits for them, and re-layouts: 27.9 us -> 17.8 us
    ppermute x20 -> x12, waiting for transfers between devices: 114 us -> 41.3 us  [shift(): lax.ppermute(value, 'tensor', [(i, (i + count) % size) for i in range(siz...]
    ppermute x22 -> x28, waiting for transfers between devices: 44.8 us -> 114 us  [swap(): return lax.ppermute(value, axis, [(i, i ^ bit) for i in range(size)])]
    all_to_all x0 -> x1, blocking collectives: none -> 17.4 us  [group_collect(): lax.all_to_all(spread, axes, split_axis=0, concat_axis=0, tiled=True)]
    ppermute x20 -> x12, starting transfers between devices: 22.4 us -> 9.67 us  [shift(): lax.ppermute(value, 'tensor', [(i, (i + count) % size) for i in range(siz...]
    unnamed x91 -> x81, local copies, waits for them, and re-layouts: 13.3 us -> 7.66 us
    all_to_all x4 -> x3, starting transfers between devices: 15.4 us -> 11.2 us  [the longest x2 7.69 us: group_sum_parts(): lax.all_to_all(padded, axes, split_axis=0, concat_axis=0, tiled=True)]
    ppermute x22 -> x28, starting transfers between devices: 22.2 us -> 26 us  [swap(): return lax.ppermute(value, axis, [(i, i ^ bit) for i in range(size)])]
    all_to_all x4 -> x3, waiting for transfers between devices: 17 us -> 20.8 us  [the longest x2 20.8 us: group_sum_parts(): lax.all_to_all(padded, axes, split_axis=0, concat_axis=0, tiled=True)]
  transfers between devices with their start and end apart: 46 -> 43, of which waited for: 23 -> 24; matrix products, arithmetic and copies ran while one was open for 22% -> 20% of each run, Pallas kernels for 6% -> 6%
where the time goes in v2:
time: 349 us; the launch traced here: 343 us
  waiting for transfers between devices  176 us (50%)
  starting transfers between devices  46.9 us (13%)
  other arithmetic  34.4 us (10%)
  matrix products  28.1 us (8%)
  Pallas kernels  19.9 us (6%)
  local copies, waits for them, and re-layouts  17.8 us (5%)
  blocking collectives  17.4 us (5%)
    ppermute x28, waiting for transfers between devices, swap(): return lax.ppermute(value, axis, [(i, i ^ bit) for i in range(size)])  114 us
    ppermute x12, waiting for transfers between devices, shift(): lax.ppermute(value, 'tensor', [(i, (i + count) % size) for i in range(siz...  41.3 us
    ppermute x28, starting transfers between devices, swap(): return lax.ppermute(value, axis, [(i, i ^ bit) for i in range(size)])  26 us
    all_to_all x2, waiting for transfers between devices, group_sum_parts(): lax.all_to_all(padded, axes, split_axis=0, concat_axis=0, tiled=True)  20.8 us
    all_to_all x1, blocking collectives, group_collect(): lax.all_to_all(spread, axes, split_axis=0, concat_axis=0, tiled=True)  17.4 us
    dot_general x11, matrix products, dot_rows(): lax.dot_general(left, right, (((1,), (1,)), ((), ())), preferred_element_...  12.2 us
    pallas_call x1, Pallas kernels, attend_back(): pl.pallas_call(attend_back_kernel, out_shape=(jax.ShapeDtypeStruct(query....  10.1 us
    pallas_call x1, Pallas kernels, attend(): pl.pallas_call(attend_kernel, out_shape=(jax.ShapeDtypeStruct(query.shape...  9.79 us
  transfers between devices with their start and end apart: 43, of which 24 were waited for; matrix products, arithmetic and copies ran while one was open for 20% of the time, Pallas kernels for 6%

profile of v2, /device:TPU:0, one launch (start us, length us, event | category | flops | bytes accessed | tf_op | source)
XLA Modules:
  0.0 343.1 jit_solution(12789533637491775906)
XLA Ops:
  26.8 5.5 %collective-permute-done.1 = bf16[192,960]{1,0:T(8,128)(2,1)} collective-permute-done((bf16[192,960]{1,0:T(8,128)(2,1)}, bf16[192,960]{1,0:T(8,128)(2,1)}, u32[]{:S(2)}, u32[]{:S(2)}) %collective-permute-start.1) | collective-permute-done | bytes 368672 | tf_op jit(solution)/shard_map/ppermute | solution.py:80
  37.8 5.5 %collective-permute-done.3 = bf16[192,960]{1,0:T(8,128)(2,1)S(1)} collective-permute-done((bf16[192,960]{1,0:T(8,128)(2,1)}, bf16[192,960]{1,0:T(8,128)(2,1)S(1)}, u32[]{:S(2)}, u32[]{:S(2)}) %collective-permute-start.3) | collective-permute-done | bytes 368672 | tf_op jit(solution)/shard_map/ppermute | solution.py:80
  48.3 6.1 %collective-permute-done.11 = bf16[240,960]{0,1:T(8,128)(2,1)S(1)} collective-permute-done((bf16[240,960]{0,1:T(8,128)(2,1)S(1)}, bf16[240,960]{0,1:T(8,128)(2,1)S(1)}, u32[]{:S(2)}, u32[]{:S(2)}) %collective-permute-start.11) | collective-permute-done | bytes 460832 | tf_op jit(solution)/shard_map/ppermute | solution.py:80
  54.4 3.6 %collective-permute-start.15 = (bf16[2,96,960]{2,1,0:T(8,128)(2,1)S(1)}, bf16[2,96,960]{2,1,0:T(8,128)(2,1)S(1)}, u32[]{:S(2)}, u32[]{:S(2)}) collective-permute-start(bf16[2,96,960]{2,1,0:T(8,128)(2,1)S(1)} %copy-done.13), channel_id=1, source_target_pairs={{0,3},{1,0},{2,1},{3,2},{4,7},{5,4},{6,5},{7,6},{8,11},{9,8},{10,9... | collective-permute-start | bytes 1105928 | tf_op jit(solution)/shard_map/ppermute | solution.py:107
  65.2 9.8 %attend.1 = (bf16[192,960]{1,0:T(8,128)(2,1)S(1)}, f32[576,8]{1,0:T(8,128)S(1)}, bf16[192,960]{1,0:T(8,128)(2,1)S(1)}, bf16[768,320]{1,0:T(8,128)(2,1)S(1)}) custom-call(f32[192,960]{1,0:T(8,128)S(1)} %fusion.19.q_ref, f32[768,320]{1,0:T(8,128)S(1)} %slice.389.k_ref, bf16[768,320]{1,0:T(8,128)(2,1)S(1)} %slice.540.v_ref, ...), custom_call_target="tpu_custom_call" | custom-call | flops 566231040 | bytes 4000000 | tf_op jit(solution)/shard_map/attend/pallas_call | solution.py:192
  77.2 20.3 %collective-permute-done.16 = bf16[240,1920]{1,0:T(8,128)(2,1)S(1)} collective-permute-done((bf16[240,1920]{1,0:T(8,128)(2,1)S(1)}, bf16[240,1920]{1,0:T(8,128)(2,1)S(1)}, u32[]{:S(2)}, u32[]{:S(2)}) %collective-permute-start.16) | collective-permute-done | bytes 921632 | tf_op jit(solution)/shard_map/ppermute | solution.py:80
  100.1 7.7 %pad_maximum_fusion.1 = bf16[960,1280]{1,0:T(8,128)(2,1)S(1)} fusion(bf16[240,1920]{1,0:T(8,128)(2,1)S(1)} %collective-permute-done.18, bf16[240,1920]{1,0:T(8,128)(2,1)S(1)} %collective-permute-done.17, bf16[240,1920]{1,0:T(8,128)(2,1)S(1)} %collective-permute-done.16, bf16[240,640]{1,0:T(8,128)(2,1)S(1)} %bitcast.87, bf16[240,640]{1,0:T(8,128)(2,1)S(1)} %copy-done.7, ...), kind=kLoop, calls=%fused_computation.8 | loop fusion | flops 14745600 | bytes 6144000 | tf_op jit(solution)/shard_map/concatenate | solution.py:304
  114.6 9.3 %collective-permute-done.20 = bf16[192,960]{1,0:T(8,128)(2,1)S(1)} collective-permute-done((bf16[192,960]{1,0:T(8,128)(2,1)S(1)}, bf16[192,960]{1,0:T(8,128)(2,1)S(1)}, u32[]{:S(2)}, u32[]{:S(2)}) %collective-permute-start.20) | collective-permute-done | bytes 368672 | tf_op jit(solution)/shard_map/ppermute | solution.py:107
  125.3 7.1 %collective-permute-done.22 = bf16[192,960]{1,0:T(8,128)(2,1)S(1)} collective-permute-done((bf16[192,960]{1,0:T(8,128)(2,1)S(1)}, bf16[192,960]{1,0:T(8,128)(2,1)S(1)}, u32[]{:S(2)}, u32[]{:S(2)}) %collective-permute-start.22) | collective-permute-done | bytes 368672 | tf_op jit(solution)/shard_map/ppermute | solution.py:107
  133.5 7.3 %collective-permute-done.21 = bf16[192,960]{1,0:T(8,128)(2,1)S(1)} collective-permute-done((bf16[192,960]{1,0:T(8,128)(2,1)S(1)}, bf16[192,960]{1,0:T(8,128)(2,1)S(1)}, u32[]{:S(2)}, u32[]{:S(2)}) %collective-permute-start.21) | collective-permute-done | bytes 368672 | tf_op jit(solution)/shard_map/ppermute | solution.py:107
  149.6 12.3 %collective-permute-done.24 = bf16[192,960]{1,0:T(8,128)(2,1)S(1)} collective-permute-done((bf16[192,960]{1,0:T(8,128)(2,1)S(1)}, bf16[192,960]{1,0:T(8,128)(2,1)S(1)}, u32[]{:S(2)}, u32[]{:S(2)}) %collective-permute-start.24) | collective-permute-done | bytes 368672 | tf_op jit(solution)/shard_map/ppermute | solution.py:107
  166.4 10.1 %attend_back.1 = (bf16[192,960]{1,0:T(8,128)(2,1)S(1)}, bf16[768,640]{1,0:T(8,128)(2,1)S(1)}) custom-call(bf16[192,960]{1,0:T(8,128)(2,1)S(1)} %get-tuple-element.46.q_ref, bf16[768,320]{1,0:T(8,128)(2,1)S(1)} %get-tuple-element.47.k_ref, bf16[768,320]{1,0:T(8,128)(2,1)S(1)} %slice.540.v_ref, bf16[192,960]{1,0:T(8,128)(2,1)S(1)} %get-tuple-element.48.mix_ref, ...), custom_call_target="tpu_custom_call" | custom-call | flops 1415577600 | bytes 6000000 | tf_op jit(solution)/shard_map/attend_back/pallas_call | solution.py:241
  176.7 10.2 %collective-permute-done.26 = bf16[240,1920]{1,0:T(8,128)(2,1)S(1)} collective-permute-done((bf16[240,1920]{1,0:T(8,128)(2,1)S(1)}, bf16[240,1920]{1,0:T(8,128)(2,1)S(1)}, u32[]{:S(2)}, u32[]{:S(2)}) %collective-permute-start.26) | collective-permute-done | bytes 921632 | tf_op jit(solution)/shard_map/ppermute | solution.py:80
  196.8 8.8 %collective-permute-done.31 = bf16[240,960]{1,0:T(8,128)(2,1)S(1)} collective-permute-done((bf16[240,960]{1,0:T(8,128)(2,1)S(1)}, bf16[240,960]{1,0:T(8,128)(2,1)S(1)}, u32[]{:S(2)}, u32[]{:S(2)}) %collective-permute-start.31) | collective-permute-done | bytes 460832 | tf_op jit(solution)/shard_map/ppermute | solution.py:80
  205.8 16.2 %collective-permute-done.30 = bf16[240,1600]{1,0:T(8,128)(2,1)S(1)} collective-permute-done((bf16[240,1600]{1,0:T(8,128)(2,1)S(1)}, bf16[240,1600]{1,0:T(8,128)(2,1)S(1)}, u32[]{:S(2)}, u32[]{:S(2)}) %collective-permute-start.30) | collective-permute-done | bytes 768032 | tf_op jit(solution)/shard_map/ppermute | solution.py:80
  229.3 4.1 %all-to-all-start.1 = ((bf16[8,32,960]{2,1,0:T(8,128)(2,1)}), bf16[8,32,960]{2,1,0:T(8,128)(2,1)}, u32[]{:S(2)}, u32[]{:S(2)}) async-start(bf16[8,32,960]{2,1,0:T(8,128)(2,1)} %bitcast.89), calls=%async_computation.1 | async-start | bytes 1048576 | tf_op jit(solution)/shard_map/all_to_all | solution.py:128
  233.5 8.3 %collective-permute-done.35 = bf16[192,640]{1,0:T(8,128)(2,1)} collective-permute-done((bf16[192,640]{1,0:T(8,128)(2,1)}, bf16[192,640]{1,0:T(8,128)(2,1)}, u32[]{:S(2)}, u32[]{:S(2)}) %collective-permute-start.35) | collective-permute-done | bytes 245792 | tf_op jit(solution)/shard_map/ppermute | solution.py:80
  250.6 3.5 %all-to-all-start = ((bf16[8,32,1600]{2,1,0:T(8,128)(2,1)}), bf16[8,32,1600]{2,1,0:T(8,128)(2,1)S(1)}, u32[]{:S(2)}, u32[]{:S(2)}) async-start(bf16[8,32,1600]{2,1,0:T(8,128)(2,1)} %bitcast.17), calls=%async_computation | async-start | bytes 1703936 | tf_op jit(solution)/shard_map/all_to_all | solution.py:128
  257.3 19.3 %all-to-all-done = bf16[8,32,1600]{2,1,0:T(8,128)(2,1)S(1)} async-done(((bf16[8,32,1600]{2,1,0:T(8,128)(2,1)}), bf16[8,32,1600]{2,1,0:T(8,128)(2,1)S(1)}, u32[]{:S(2)}, u32[]{:S(2)}) %all-to-all-start) | async-done | bytes 819232 | tf_op jit(solution)/shard_map/all_to_all | solution.py:128
  276.8 17.4 %all_to_all.36 = bf16[8,32,960]{2,1,0:T(8,128)(2,1)S(1)} all-to-all(bf16[8,32,960]{2,1,0:T(8,128)(2,1)S(1)} %broadcast_in_dim.33), channel_id=1, replica_groups=mesh['shard'=4,'context'=2,'tensor'=4] {'context','tensor'}, dimensions={0} | all-to-all | bytes 983040 | tf_op jit(solution)/shard_map/all_to_all | solution.py:138
  295.1 3.5 %all-to-all-start.2 = ((bf16[8,32,1600]{2,1,0:T(8,128)(2,1)}), bf16[8,32,1600]{2,1,0:T(8,128)(2,1)S(1)}, u32[]{:S(2)}, u32[]{:S(2)}) async-start(bf16[8,32,1600]{2,1,0:T(8,128)(2,1)} %broadcast_in_dim.32), calls=%async_computation.2 | async-start | bytes 1703936 | tf_op jit(solution)/shard_map/all_to_all | solution.py:138
  306.1 13.0 %collective-permute-done.38 = f32[240]{0:T(256)S(1)} collective-permute-done((f32[240]{0:T(256)S(1)}, f32[240]{0:T(256)S(1)}, u32[]{:S(2)}, u32[]{:S(2)}) %collective-permute-start.38) | collective-permute-done | bytes 992 | tf_op jit(solution)/shard_map/ppermute | solution.py:80
  319.0 4.6 %collective-permute-start.39 = (f32[240]{0:T(256)S(1)}, f32[240]{0:T(256)S(1)}, u32[]{:S(2)}, u32[]{:S(2)}) collective-permute-start(f32[240]{0:T(256)S(1)} %add.310), channel_id=1, source_target_pairs={{0,2},{1,3},{2,0},{3,1},{4,6},{5,7},{6,4},{7,5},{8,10},{9,11},{10,... | collective-permute-start | bytes 2888 | tf_op jit(solution)/shard_map/ppermute | solution.py:80
  323.6 11.5 %collective-permute-done.39 = f32[240]{0:T(256)S(1)} collective-permute-done((f32[240]{0:T(256)S(1)}, f32[240]{0:T(256)S(1)}, u32[]{:S(2)}, u32[]{:S(2)}) %collective-permute-start.39) | collective-permute-done | bytes 992 | tf_op jit(solution)/shard_map/ppermute | solution.py:80
  (278 shorter events, 115.4 us)
Async XLA Ops:
  1.3 24.0 %collective-permute-start.5 = (f32[240,2]{0,1:T(2,128)S(1)}, f32[240,2]{0,1:T(2,128)S(1)}, u32[]{:S(2)}, u32[]{:S(2)}) collective-permute-start(f32[240,2]{0,1:T(2,128)S(1)} %pad_maximum_fusion.24), channel_id=1, source_target_pairs={{0,16},{8,24},{16,0},{24,8},{1,17},{9,25},{17,1},{25,9},{2,18},{10... | collective-permute-start | bytes 5768 | tf_op jit(solution)/shard_map/ppermute | solution.py:80
  4.3 21.2 %collective-permute-start.6 = (f32[240,2]{0,1:T(2,128)S(1)}, f32[240,2]{0,1:T(2,128)S(1)}, u32[]{:S(2)}, u32[]{:S(2)}) collective-permute-start(f32[240,2]{0,1:T(2,128)S(1)} %pad_maximum_fusion.24), channel_id=1, source_target_pairs={{0,8},{8,0},{16,24},{24,16},{1,9},{9,1},{17,25},{25,17},{2,10},{10... | collective-permute-start | bytes 5768 | tf_op jit(solution)/shard_map/ppermute | solution.py:80
  11.2 26.5 %collective-permute-start.8 = (bf16[240,1600]{1,0:T(8,128)(2,1)S(1)}, bf16[240,1600]{1,0:T(8,128)(2,1)}, u32[]{:S(2)}, u32[]{:S(2)}) collective-permute-start(bf16[240,1600]{1,0:T(8,128)(2,1)S(1)} %concatenate.132), channel_id=1, source_target_pairs={{0,16},{8,24},{16,0},{24,8},{1,17},{9,25},{17,1},{25,9},{2,18},{10... | collective-permute-start | bytes 2304008 | tf_op jit(solution)/shard_map/ppermute | solution.py:80
  25.5 32.5 %collective-permute-start.9 = (bf16[240,1600]{1,0:T(8,128)(2,1)S(1)}, bf16[240,1600]{1,0:T(8,128)(2,1)S(1)}, u32[]{:S(2)}, u32[]{:S(2)}) collective-permute-start(bf16[240,1600]{1,0:T(8,128)(2,1)S(1)} %concatenate.132), channel_id=1, source_target_pairs={{0,8},{8,0},{16,24},{24,16},{1,9},{9,1},{17,25},{25,17},{2,10},{10... | collective-permute-start | bytes 2304008 | tf_op jit(solution)/shard_map/ppermute | solution.py:80
  26.5 48.4 %collective-permute-start.12 = (bf16[240,960]{0,1:T(8,128)(2,1)}, bf16[240,960]{0,1:T(8,128)(2,1)S(1)}, u32[]{:S(2)}, u32[]{:S(2)}) collective-permute-start(bf16[240,960]{0,1:T(8,128)(2,1)} %bitcast.101), channel_id=1, source_target_pairs={{0,8},{8,0},{16,24},{24,16},{1,9},{9,1},{17,25},{25,17},{2,10},{10... | collective-permute-start | bytes 1382408 | tf_op jit(solution)/shard_map/ppermute | solution.py:80
  37.7 60.1 %collective-permute-start.17 = (bf16[240,1920]{1,0:T(8,128)(2,1)S(1)}, bf16[240,1920]{1,0:T(8,128)(2,1)S(1)}, u32[]{:S(2)}, u32[]{:S(2)}) collective-permute-start(bf16[240,1920]{1,0:T(8,128)(2,1)S(1)} %copy-done.20), channel_id=1, source_target_pairs={{0,8},{8,0},{16,24},{24,16},{1,9},{9,1},{17,25},{25,17},{2,10},{10... | collective-permute-start | bytes 2764808 | tf_op jit(solution)/shard_map/ppermute | solution.py:80
  54.4 22.4 %collective-permute-start.15 = (bf16[2,96,960]{2,1,0:T(8,128)(2,1)S(1)}, bf16[2,96,960]{2,1,0:T(8,128)(2,1)S(1)}, u32[]{:S(2)}, u32[]{:S(2)}) collective-permute-start(bf16[2,96,960]{2,1,0:T(8,128)(2,1)S(1)} %copy-done.13), channel_id=1, source_target_pairs={{0,3},{1,0},{2,1},{3,2},{4,7},{5,4},{6,5},{7,6},{8,11},{9,8},{10,9... | collective-permute-start | bytes 1105928 | tf_op jit(solution)/shard_map/ppermute | solution.py:107
  58.0 18.8 %collective-permute-start.14 = (bf16[2,96,960]{2,1,0:T(8,128)(2,1)S(1)}, bf16[2,96,960]{2,1,0:T(8,128)(2,1)S(1)}, u32[]{:S(2)}, u32[]{:S(2)}) collective-permute-start(bf16[2,96,960]{2,1,0:T(8,128)(2,1)S(1)} %collective-permute-done.4), channel_id=1, source_target_pairs={{0,1},{1,2},{2,3},{3,0},{4,5},{5,6},{6,7},{7,4},{8,9},{9,10},{10,1... | collective-permute-start | bytes 1105928 | tf_op jit(solution)/shard_map/ppermute | solution.py:107
  58.1 17.5 %collective-permute-start.13 = (bf16[240,960]{0,1:T(8,128)(2,1)S(1)}, bf16[240,960]{0,1:T(8,128)(2,1)S(1)}, u32[]{:S(2)}, u32[]{:S(2)}) collective-permute-start(bf16[240,960]{0,1:T(8,128)(2,1)S(1)} %collective-permute-done.11), channel_id=1, source_target_pairs={{0,8},{8,0},{16,24},{24,16},{1,9},{9,1},{17,25},{25,17},{2,10},{10... | collective-permute-start | bytes 1382408 | tf_op jit(solution)/shard_map/ppermute | solution.py:80
  75.0 22.6 %collective-permute-start.16 = (bf16[240,1920]{1,0:T(8,128)(2,1)S(1)}, bf16[240,1920]{1,0:T(8,128)(2,1)S(1)}, u32[]{:S(2)}, u32[]{:S(2)}) collective-permute-start(bf16[240,1920]{1,0:T(8,128)(2,1)S(1)} %copy-done.20), channel_id=1, source_target_pairs={{0,16},{8,24},{16,0},{24,8},{1,17},{9,25},{17,1},{25,9},{2,18},{10... | collective-permute-start | bytes 2764808 | tf_op jit(solution)/shard_map/ppermute | solution.py:80
  76.9 33.3 %collective-permute-start.19 = (bf16[192,960]{1,0:T(8,128)(2,1)S(1)}, bf16[192,960]{1,0:T(8,128)(2,1)S(1)}, u32[]{:S(2)}, u32[]{:S(2)}) collective-permute-start(bf16[192,960]{1,0:T(8,128)(2,1)S(1)} %multiply_convert_fusion.1), channel_id=1, source_target_pairs={{0,1},{1,2},{2,3},{3,0},{4,5},{5,6},{6,7},{7,4},{8,9},{9,10},{10,1... | collective-permute-start | bytes 1105928 | tf_op jit(solution)/shard_map/ppermute | solution.py:107
  112.6 19.8 %collective-permute-start.22 = (bf16[192,960]{1,0:T(8,128)(2,1)S(1)}, bf16[192,960]{1,0:T(8,128)(2,1)S(1)}, u32[]{:S(2)}, u32[]{:S(2)}) collective-permute-start(bf16[192,960]{1,0:T(8,128)(2,1)S(1)} %convolution_convert_fusion.12), channel_id=1, source_target_pairs={{0,1},{1,2},{2,3},{3,0},{4,5},{5,6},{6,7},{7,4},{8,9},{9,10},{10,1... | collective-permute-start | bytes 1105928 | tf_op jit(solution)/shard_map/ppermute | solution.py:107
  145.8 17.6 %collective-permute-start.25 = (bf16[480,1920]{1,0:T(8,128)(2,1)S(1)}, bf16[480,1920]{1,0:T(8,128)(2,1)S(1)}, u32[]{:S(2)}, u32[]{:S(2)}) collective-permute-start(bf16[480,1920]{1,0:T(8,128)(2,1)S(1)} %pad_maximum_fusion.7), channel_id=1, source_target_pairs={{0,8},{8,0},{16,24},{24,16},{1,9},{9,1},{17,25},{25,17},{2,10},{10... | collective-permute-start | bytes 5529608 | tf_op jit(solution)/shard_map/ppermute | solution.py:80
  164.0 22.9 %collective-permute-start.26 = (bf16[240,1920]{1,0:T(8,128)(2,1)S(1)}, bf16[240,1920]{1,0:T(8,128)(2,1)S(1)}, u32[]{:S(2)}, u32[]{:S(2)}) collective-permute-start(bf16[240,1920]{1,0:T(8,128)(2,1)S(1)} %slice.406), channel_id=1, source_target_pairs={{0,16},{8,24},{16,0},{24,8},{1,17},{9,25},{17,1},{25,9},{2,18},{10... | collective-permute-start | bytes 2764808 | tf_op jit(solution)/shard_map/ppermute | solution.py:80
  166.1 20.8 %collective-permute-start.28 = (bf16[192,960]{1,0:T(8,128)(2,1)S(1)}, bf16[192,960]{1,0:T(8,128)(2,1)S(1)}, u32[]{:S(2)}, u32[]{:S(2)}) collective-permute-start(bf16[192,960]{1,0:T(8,128)(2,1)S(1)} %convolution_convert_fusion.8), channel_id=1, source_target_pairs={{0,1},{1,2},{2,3},{3,0},{4,5},{5,6},{6,7},{7,4},{8,9},{9,10},{10,1... | collective-permute-start | bytes 1105928 | tf_op jit(solution)/shard_map/ppermute | solution.py:107
  194.0 28.0 %collective-permute-start.30 = (bf16[240,1600]{1,0:T(8,128)(2,1)S(1)}, bf16[240,1600]{1,0:T(8,128)(2,1)S(1)}, u32[]{:S(2)}, u32[]{:S(2)}) collective-permute-start(bf16[240,1600]{1,0:T(8,128)(2,1)S(1)} %slice.412), channel_id=1, source_target_pairs={{0,16},{8,24},{16,0},{24,8},{1,17},{9,25},{17,1},{25,9},{2,18},{10... | collective-permute-start | bytes 2304008 | tf_op jit(solution)/shard_map/ppermute | solution.py:80
  195.2 26.9 %collective-permute-start.33 = (bf16[192,960]{1,0:T(8,128)(2,1)S(1)}, bf16[192,960]{1,0:T(8,128)(2,1)S(1)}, u32[]{:S(2)}, u32[]{:S(2)}) collective-permute-start(bf16[192,960]{1,0:T(8,128)(2,1)S(1)} %fusion.40), channel_id=1, source_target_pairs={{0,1},{1,2},{2,3},{3,0},{4,5},{5,6},{6,7},{7,4},{8,9},{9,10},{10,1... | collective-permute-start | bytes 1105928 | tf_op jit(solution)/shard_map/ppermute | solution.py:107
  195.3 28.0 %collective-permute-start.34 = (bf16[240,1920]{1,0:T(8,128)(2,1)S(1)}, bf16[240,1920]{1,0:T(8,128)(2,1)S(1)}, u32[]{:S(2)}, u32[]{:S(2)}) collective-permute-start(bf16[240,1920]{1,0:T(8,128)(2,1)S(1)} %slice_add_fusion.1), channel_id=1, source_target_pairs={{0,4},{4,0},{1,5},{5,1},{2,6},{6,2},{3,7},{7,3},{8,12},{12,8},{9,1... | collective-permute-start | bytes 2764808 | tf_op jit(solution)/shard_map/ppermute | solution.py:80
  224.1 17.7 %collective-permute-start.35 = (bf16[192,640]{1,0:T(8,128)(2,1)}, bf16[192,640]{1,0:T(8,128)(2,1)}, u32[]{:S(2)}, u32[]{:S(2)}) collective-permute-start(bf16[192,640]{1,0:T(8,128)(2,1)} %slice.345), channel_id=1, source_target_pairs={{0,1},{1,0},{2,3},{3,2},{4,5},{5,4},{6,7},{7,6},{8,9},{9,8},{10,11... | collective-permute-start | bytes 737288 | tf_op jit(solution)/shard_map/ppermute | solution.py:80
  225.4 22.4 %collective-permute-start.36 = (bf16[192,960]{1,0:T(8,128)(2,1)}, bf16[192,960]{1,0:T(8,128)(2,1)S(1)}, u32[]{:S(2)}, u32[]{:S(2)}) collective-permute-start(bf16[192,960]{1,0:T(8,128)(2,1)} %fusion.41), channel_id=1, source_target_pairs={{0,1},{1,2},{2,3},{3,0},{4,5},{5,6},{6,7},{7,4},{8,9},{9,10},{10,1... | collective-permute-start | bytes 1105928 | tf_op jit(solution)/shard_map/ppermute | solution.py:107
  229.3 21.3 %all-to-all-start.1 = ((bf16[8,32,960]{2,1,0:T(8,128)(2,1)}), bf16[8,32,960]{2,1,0:T(8,128)(2,1)}, u32[]{:S(2)}, u32[]{:S(2)}) async-start(bf16[8,32,960]{2,1,0:T(8,128)(2,1)} %bitcast.89), calls=%async_computation.1 | async-start | bytes 1048576 | tf_op jit(solution)/shard_map/all_to_all | solution.py:128
  250.6 26.0 %all-to-all-start = ((bf16[8,32,1600]{2,1,0:T(8,128)(2,1)}), bf16[8,32,1600]{2,1,0:T(8,128)(2,1)S(1)}, u32[]{:S(2)}, u32[]{:S(2)}) async-start(bf16[8,32,1600]{2,1,0:T(8,128)(2,1)} %bitcast.17), calls=%async_computation | async-start | bytes 1703936 | tf_op jit(solution)/shard_map/all_to_all | solution.py:128
  295.1 43.5 %all-to-all-start.2 = ((bf16[8,32,1600]{2,1,0:T(8,128)(2,1)}), bf16[8,32,1600]{2,1,0:T(8,128)(2,1)S(1)}, u32[]{:S(2)}, u32[]{:S(2)}) async-start(bf16[8,32,1600]{2,1,0:T(8,128)(2,1)} %broadcast_in_dim.32), calls=%async_computation.2 | async-start | bytes 1703936 | tf_op jit(solution)/shard_map/all_to_all | solution.py:138
  300.3 35.3 %collective-permute-start.37 = (bf16[192,960]{1,0:T(8,128)(2,1)S(1)}, bf16[192,960]{1,0:T(8,128)(2,1)S(1)}, u32[]{:S(2)}, u32[]{:S(2)}) collective-permute-start(bf16[192,960]{1,0:T(8,128)(2,1)S(1)} %pad_maximum_fusion.16), channel_id=1, source_target_pairs={{0,2},{1,3},{2,0},{3,1},{4,6},{5,7},{6,4},{7,5},{8,10},{9,11},{10,... | collective-permute-start | bytes 1105928 | tf_op jit(solution)/shard_map/ppermute | solution.py:80
  (53 other events, 584.5 us)

commit v3 on v2

--- a/solution.py
+++ b/solution.py
@@ -80,13 +80,17 @@
     return lax.ppermute(value, axis, [(i, i ^ bit) for i in range(size)])
 
 
-def gather_pieces(rows, gate=None):
+def gather_pieces(rows, gate=None, later=None):
     pieces = [rows]
     for place in reversed(range(bits_of(lax.axis_size("shard")))):
         if len(pieces) > 2:
             pieces = [jnp.concatenate(pieces, 0)]
-        sent = pieces if gate is None else [after(piece, *gate) for piece in pieces]
-        gate = None
+        sent = pieces
+        if gate is not None:
+            sent = [after(piece, *gate) for piece in pieces]
+            gate = None
+        elif later is not None:
+            sent = pieces[:1] + [after(piece, later) for piece in pieces[1:]]
         pieces = pieces + [swap(piece, "shard", 1 << place) for piece in sent]
     return pieces
 
@@ -105,12 +109,6 @@
 def shift(value, count):
     size = lax.axis_size("tensor")
     return lax.ppermute(value, "tensor", [(i, (i + count) % size) for i in range(size)])
-
-
-def one_sequence(block, upper):
-    mine = jnp.where(upper, block[1], block[0])
-    other = jnp.where(upper, block[0], block[1])
-    return jnp.concatenate([mine, swap(other, "tensor", 2)], 0)
 
 
 def both_sequences(mine, other, upper):
@@ -273,7 +271,7 @@
     places = lax.axis_size("tensor")
     rows = 2 * length
     upper = place // 2 == 1
-    q_cols, kv_cols, hidden_cols = w_query.shape[1], key_weight.shape[1], w_gate.shape[1]
+    kv_cols, hidden_cols = key_weight.shape[1], w_gate.shape[1]
 
     starts = [
         (which * places + (place ^ step)) * length
@@ -286,24 +284,28 @@
     query_table, query_pos = key_table[:rows], key_pos[:rows, None]
     key_pos = key_pos[None, :]
 
-    own = one_sequence(to_relative(tokens, shards, shard), upper)
+    mine = jnp.where(upper, tokens[1], tokens[0])
+    moved = swap(jnp.where(upper, tokens[0], tokens[1]), "tensor", 2)
+    own = jnp.concatenate([to_relative(mine, shards, shard), to_relative(moved, shards, shard)], 0)
     beside = swap(own, "tensor", 1)
     across = swap(own, "context", 1)
+
     across_beside = swap(after(beside, across), "context", 1)
     all_tokens = jnp.concatenate([own, beside, across, across_beside], 0)
 
-    attn_local = jnp.concatenate([w_query, key_weight, value_weight], 1)
+    attn_local = jnp.concatenate([key_weight, value_weight, w_query], 1)
+    out_local = w_output.T
+    gap = -attn_local.shape[1] % 128
+    first_pieces = gather_pieces(
+        jnp.concatenate([attn_local, jnp.zeros_like(attn_local[:, :gap]), out_local], 1)
+    )
+    gains = gather_rows(after(jnp.concatenate([attn_gain[:, None], mlp_gain[:, None]], 1), moved))
+    gain_a, gain_m = gains[:, 0], gains[:, 1]
+    ends = (2 * kv_cols, attn_local.shape[1], attn_local.shape[1] + gap)
+    w_kv = jnp.concatenate([piece[:, : ends[0]] for piece in first_pieces], 0)
+    w_q = jnp.concatenate([piece[:, ends[0] : ends[1]] for piece in first_pieces], 0)
+    out_weight = jnp.concatenate([piece[:, ends[2] :] for piece in first_pieces], 0)
     mlp_local = jnp.concatenate([w_gate, w_up, w_down.T], 1)
-    attn_pieces = gather_pieces(attn_local)
-    gains = gather_rows(jnp.concatenate([attn_gain[:, None], mlp_gain[:, None]], 1))
-    gain_a, gain_m = gains[:, 0], gains[:, 1]
-    out_pieces = gather_pieces(w_output.T, attn_pieces[1:2])
-    mlp_pieces = gather_pieces(mlp_local, out_pieces[1:2])
-    attn_weight = jnp.concatenate(attn_pieces, 0)
-    out_weight = jnp.concatenate(out_pieces, 0)
-    mlp_weight = jnp.concatenate(mlp_pieces, 0)
-    w_q, w_kv = attn_weight[:, :q_cols], attn_weight[:, q_cols:]
-    w_in, w_dn = mlp_weight[:, : 2 * hidden_cols], mlp_weight[:, 2 * hidden_cols :]
 
     cots = [after(to_relative(cotangent, shards, shard), beside)]
     cots.append(shift(cots[0], 1))
@@ -321,6 +323,9 @@
     mix, log_total, query_rot, key_rot = attend(
         query, key, value, query_table, key_table, query_pos, key_pos
     )
+    mlp_pieces = gather_pieces(mlp_local, (query,), mix)
+    w_in = jnp.concatenate([piece[:, : 2 * hidden_cols] for piece in mlp_pieces], 0)
+    w_dn = jnp.concatenate([piece[:, 2 * hidden_cols :] for piece in mlp_pieces], 0)
     hidden = tokens_f + dot_rows(mix, out_weight)
     scale_m = rms_scale(hidden)
     normed_m = (hidden * scale_m * gain_m).astype(jnp.bfloat16)
@@ -340,7 +345,7 @@
     arriving = shift(normed_m, 1)
     for k, cot in enumerate(cots):
         if k > 0:
-            group.append(arriving)
+            group.append(arriving if k < 3 else after(arriving, grad_nm))
             if k + 1 < places:
                 arriving = shift(after(arriving, backs[-1]), 1)
         rows_in = group[k]
@@ -353,49 +358,52 @@
         grad_gate = (grad_act * up_vals * sigma * (1.0 + gate * (1.0 - sigma))).astype(jnp.bfloat16)
         grads_in.append(jnp.concatenate([grad_gate, grad_up], 1))
         backs.append(dot_rows(grads_in[-1], w_in).astype(jnp.bfloat16))
-    grad_nm = backs[1]
-    for k in [*range(2, places), 0]:
-        grad_nm = backs[k] + shift(grad_nm, 1)
-    grad_hidden = own_cot.astype(jnp.float32) + norm_back(
-        grad_nm.astype(jnp.float32), hidden, scale_m, gain_m
-    )
+        if k > 0:
+            grad_nm = backs[k] if k == 1 else backs[k] + shift(grad_nm, 1)
+    bits = bits_of(shards)
+    group, grad_in = after(jnp.concatenate(group, 0), grad_nm), jnp.concatenate(grads_in, 0)
+    act, cot_group = after(jnp.concatenate(acts, 0), grad_nm), jnp.concatenate(cots, 0)
+    mlp_term = jnp.concatenate(
+        [dot_cols(group, grad_in).astype(jnp.bfloat16), dot_cols(cot_group, act).astype(jnp.bfloat16)], 1
+    )
+    mlp_term = scatter_rows(mlp_term, 0, 1)
+    half_cols = mlp_term.shape[1] // 2
+    first, second = mlp_term[:, :half_cols], mlp_term[:, half_cols:]
+    later = context == 1
+    mlp_kept, mlp_sent = jnp.where(later, second, first), jnp.where(later, first, second)
+
+    mlp_kept, mlp_sent, last = barrier((mlp_kept, mlp_sent, backs[0]))
+    grad_nm = (last + shift(grad_nm, 1)).astype(jnp.float32)
+    grad_hidden = own_cot.astype(jnp.float32) + norm_back(grad_nm, hidden, scale_m, gain_m)
+    gain_m_term = jnp.sum(grad_nm * (hidden * scale_m), axis=0)
     grad_hidden_low = grad_hidden.astype(jnp.bfloat16)
     grad_mix = dot(grad_hidden_low, out_weight).astype(jnp.bfloat16)
-
-    bits = bits_of(shards)
-    group, grad_in = jnp.concatenate(group, 0), jnp.concatenate(grads_in, 0)
-    act, cot_group = jnp.concatenate(acts, 0), jnp.concatenate(cots, 0)
-    mlp_term = jnp.concatenate(
-        [dot_cols(group, grad_in).astype(jnp.bfloat16), dot_cols(cot_group, act).astype(jnp.bfloat16)], 1
-    )
-    mlp_term = scatter_rows(mlp_term, 0, bits)
-    out_term = scatter_rows(dot_cols(grad_hidden_low, mix).astype(jnp.bfloat16), 0, 1)
+    mlp_half = mlp_kept + swap(mlp_sent, "context", 1)
+    out_term = scatter_rows(dot_cols(grad_hidden_low, mix).astype(jnp.bfloat16), 0, bits)
     forward = [dot_rows(act, w_dn).astype(jnp.bfloat16) for act in acts]
     total = shift(after(forward[1], grad_mix), 1)
 
     grad_query, grad_kv = attend_back(
         query_rot, key_rot, value, mix, grad_mix, log_total, query_table, key_table, query_pos, key_pos
     )
-    grad_query, grad_kv, mlp_term, out_term, total = barrier(
-        (grad_query, grad_kv, mlp_term, out_term, total)
-    )
+    grad_query, grad_kv, mlp_half, out_term, total = barrier(
+        (grad_query, grad_kv, mlp_half, out_term, total)
+    )
+    out_total = lax.psum(out_term, ("context", "tensor")).astype(jnp.float32).T
     attn_term = jnp.concatenate(
         [
+            dot_cols(all_normed, grad_kv).astype(jnp.bfloat16),
             dot_cols(normed_a, grad_query).astype(jnp.bfloat16),
-            dot_cols(all_normed, grad_kv).astype(jnp.bfloat16),
+            gain_m_term.astype(jnp.bfloat16)[:, None],
         ],
         1,
     )
     attn_term = scatter_rows(attn_term, 0, bits)
-    out_term = scatter_rows(out_term, 1, bits)
     pair = grad_kv[: 2 * rows] + swap(grad_kv[2 * rows :], "context", 1)
     total = shift(forward[2] + total, 1)
-    mlp_across = swap(mlp_term, "context", 1)
-    attn_term, out_term, pair, total, mlp_across = barrier(
-        (attn_term, out_term, pair, total, mlp_across)
-    )
-
-    attn_part, out_part = group_sum_parts(attn_term), group_sum_parts(out_term)
+    attn_term, pair, total, mlp_half = barrier((attn_term, pair, total, mlp_half))
+
+    attn_part = group_sum_parts(attn_term)
     own_kv = pair[:rows] + swap(pair[rows:], "tensor", 1)
     grad_na = dot_rows(grad_query, w_q) + dot_rows(own_kv, w_kv)
     grad_tokens = grad_hidden + norm_back(grad_na, tokens_f, scale_a, gain_a)
@@ -403,32 +411,30 @@
     total = shift(forward[3] + total, 1)
     block = hidden + forward[0].astype(jnp.float32) + total.astype(jnp.float32)
     block = from_relative(block.astype(jnp.bfloat16), shards, shard)
-    attn_part, out_part, grad_tokens, block = barrier((attn_part, out_part, grad_tokens, block))
+    mlp_half = scatter_rows(mlp_half, 1, bits)
+    attn_part, grad_tokens, block, mlp_half = barrier((attn_part, grad_tokens, block, mlp_half))
 
     back_rows = swap(jnp.concatenate([block[length:], grad_tokens[length:]], 0), "tensor", 2)
     block_out = both_sequences(block[:length], back_rows[:length], upper)
     tokens_grad = both_sequences(grad_tokens[:length], back_rows[length:], upper)
-    out_total = group_collect(out_part, out_term.shape[0]).astype(jnp.float32).T
     attn_total = group_collect(attn_part, attn_term.shape[0]).astype(jnp.float32)
+    attn_total, gain_m_total = attn_total[:, :-1], attn_total[:, -1]
     gain_a_total = jnp.sum(attn_local.astype(jnp.float32) * attn_total, axis=1) / attn_gain
 
-    mlp_total = mlp_term.astype(jnp.float32) + mlp_across.astype(jnp.float32)
+    mlp_other = swap(mlp_half, "context", 1)
+    mlp_total = jnp.concatenate(
+        [jnp.where(later, mlp_other, mlp_half), jnp.where(later, mlp_half, mlp_other)], 1
+    ).astype(jnp.float32)
     gate_total = mlp_total[:, :hidden_cols]
     up_total = mlp_total[:, hidden_cols : 2 * hidden_cols]
     down_total = mlp_total[:, 2 * hidden_cols :].T
-    gain_m_total = jnp.sum(
-        w_gate.astype(jnp.float32) * gate_total + w_up.astype(jnp.float32) * up_total, axis=1
-    )
-    for place_bit in range(bits_of(places)):
-        gain_m_total = gain_m_total + swap(gain_m_total, "tensor", 1 << place_bit)
-    gain_m_total = gain_m_total / mlp_gain
     return (
         block_out,
         tokens_grad,
         gain_a_total,
-        attn_total[:, :q_cols],
-        attn_total[:, q_cols : q_cols + kv_cols],
-        attn_total[:, q_cols + kv_cols :],
+        attn_total[:, 2 * kv_cols :],
+        attn_total[:, :kv_cols],
+        attn_total[:, kv_cols : 2 * kv_cols],
         out_total,
         gain_m_total,
         gate_total,

time: 349 us -> 352 us (level)
  local copies, waits for them, and re-layouts: 17.8 us -> 36.7 us
  blocking collectives: 17.4 us -> 0 us
  between operations: 2.55 us -> 16.6 us
  starting transfers between devices: 46.9 us -> 34.4 us
  other arithmetic: 34.4 us -> 26.8 us
  matrix products: 28.1 us -> 33.9 us
    psum x0 -> x1, waiting for transfers between devices: none -> 31.8 us  [body(): out_total = lax.psum(out_term, ('context', 'tensor')).astype(jnp.float32).T]
    all_to_all x2 -> x1, waiting for transfers between devices: 20.8 us -> 0.01 us  [group_sum_parts(): lax.all_to_all(padded, axes, split_axis=0, concat_axis=0, tiled=True)]
    ppermute x28 -> x24, waiting for transfers between devices: 114 us -> 96.3 us  [swap(): return lax.ppermute(value, axis, [(i, i ^ bit) for i in range(size)])]
    all_to_all x1 -> x0, blocking collectives: 17.4 us -> none  [group_collect(): lax.all_to_all(spread, axes, split_axis=0, concat_axis=0, tiled=True)]
    ppermute x12, waiting for transfers between devices: 41.3 us -> 50.7 us  [shift(): lax.ppermute(value, 'tensor', [(i, (i + count) % size) for i in range(siz...]
    concatenate x5, other arithmetic: 11.7 us -> 3.42 us  [the longest x1 2.32 us: body(): jnp.concatenate([piece[:, :2 * hidden_cols] for piece in mlp_pieces], 0)]
    dot_general x5, matrix products: 6.37 us -> 14.5 us  [dot_cols(): lax.dot_general(left, right, (((0,), (0,)), ((), ())), preferred_element_...]
    concatenate x1 -> x3, local copies, waits for them, and re-layouts: 0.38 us -> 7.87 us  [the longest x1 5.63 us: body(): jnp.concatenate([dot_cols(all_normed, grad_kv).astype(jnp.bfloat16), dot_...]
  transfers between devices with their start and end apart: 43 -> 39, of which waited for: 24 -> 22; matrix products, arithmetic and copies ran while one was open for 20% -> 18% of each run, Pallas kernels for 6% -> 6%
where the time goes in v3:
time: 352 us; the launch traced here: 347 us
  waiting for transfers between devices  179 us (51%)
  local copies, waits for them, and re-layouts  36.7 us (10%)
  starting transfers between devices  34.4 us (10%)
  matrix products  33.9 us (10%)
  other arithmetic  26.8 us (8%)
  Pallas kernels  19.8 us (6%)
  between operations  16.6 us (5%)
    ppermute x24, waiting for transfers between devices, swap(): return lax.ppermute(value, axis, [(i, i ^ bit) for i in range(size)])  96.3 us
    ppermute x12, waiting for transfers between devices, shift(): lax.ppermute(value, 'tensor', [(i, (i + count) % size) for i in range(siz...  50.7 us
    psum x1, waiting for transfers between devices, body(): out_total = lax.psum(out_term, ('context', 'tensor')).astype(jnp.float32).T  31.8 us
    ppermute x24, starting transfers between devices, swap(): return lax.ppermute(value, axis, [(i, i ^ bit) for i in range(size)])  20.9 us
    dot_general x5, matrix products, dot_cols(): lax.dot_general(left, right, (((0,), (0,)), ((), ())), preferred_element_...  14.5 us
    dot_general x11, matrix products, dot_rows(): lax.dot_general(left, right, (((1,), (1,)), ((), ())), preferred_element_...  11.7 us
    unnamed x191, local copies, waits for them, and re-layouts  10.8 us
    pallas_call x1, Pallas kernels, attend_back(): pl.pallas_call(attend_back_kernel, out_shape=(jax.ShapeDtypeStruct(query....  10.1 us
  transfers between devices with their start and end apart: 39, of which 22 were waited for; matrix products, arithmetic and copies ran while one was open for 18% of the time, Pallas kernels for 6%

profile of v3, /device:TPU:0, one launch (start us, length us, event | category | flops | bytes accessed | tf_op | source)
XLA Modules:
  0.0 347.0 jit_solution(6924769498787732275)
XLA Ops:
  9.0 4.0 %collective-permute-start = (bf16[96,960]{1,0:T(8,128)(2,1)}, bf16[96,960]{1,0:T(8,128)(2,1)}, u32[]{:S(2)}, u32[]{:S(2)}) collective-permute-start(bf16[96,960]{1,0:T(8,128)(2,1)} %get-tuple-element.216), channel_id=1, source_target_pairs={{0,2},{1,3},{2,0},{3,1},{4,6},{5,7},{6,4},{7,5},{8,10},{9,11},{10,... | collective-permute-start | bytes 552968 | tf_op jit(solution)/shard_map/ppermute | solution.py:80
  31.0 17.8 %collective-permute-done.5 = f32[240,2]{0,1:T(2,128)S(1)} collective-permute-done((f32[240,2]{0,1:T(2,128)S(1)}, f32[240,2]{0,1:T(2,128)S(1)}, u32[]{:S(2)}, u32[]{:S(2)}) %collective-permute-start.5) | collective-permute-done | bytes 1952 | tf_op jit(solution)/shard_map/ppermute | solution.py:80
  56.5 6.4 %collective-permute-done.3 = bf16[192,960]{1,0:T(8,128)(2,1)S(1)} collective-permute-done((bf16[192,960]{1,0:T(8,128)(2,1)}, bf16[192,960]{1,0:T(8,128)(2,1)S(1)}, u32[]{:S(2)}, u32[]{:S(2)}) %collective-permute-start.3) | collective-permute-done | bytes 368672 | tf_op jit(solution)/shard_map/ppermute | solution.py:80
  63.0 2.8 collective-permute-done.4
  78.9 9.7 %attend.1 = (bf16[192,960]{1,0:T(8,128)(2,1)S(1)}, f32[576,8]{1,0:T(8,128)S(1)}, bf16[192,960]{1,0:T(8,128)(2,1)S(1)}, bf16[768,320]{1,0:T(8,128)(2,1)S(1)}) custom-call(f32[192,960]{1,0:T(8,128)S(1)} %fusion.58.q_ref, f32[768,320]{1,0:T(8,128)S(1)} %slice.489.k_ref, bf16[768,320]{1,0:T(8,128)(2,1)S(1)} %slice.642.v_ref, ...), custom_call_target="tpu_custom_call" | custom-call | flops 566231040 | bytes 4000000 | tf_op jit(solution)/shard_map/attend/pallas_call | solution.py:190
  90.5 10.0 %collective-permute-done.14 = bf16[240,1920]{1,0:T(8,128)(2,1)S(1)} collective-permute-done((bf16[240,1920]{1,0:T(8,128)(2,1)}, bf16[240,1920]{1,0:T(8,128)(2,1)S(1)}, u32[]{:S(2)}, u32[]{:S(2)}) %collective-permute-start.14) | collective-permute-done | bytes 921632 | tf_op jit(solution)/shard_map/ppermute | solution.py:80
  110.3 11.4 %collective-permute-done.17 = bf16[192,960]{1,0:T(8,128)(2,1)S(1)} collective-permute-done((bf16[192,960]{1,0:T(8,128)(2,1)S(1)}, bf16[192,960]{1,0:T(8,128)(2,1)S(1)}, u32[]{:S(2)}, u32[]{:S(2)}) %collective-permute-start.17) | collective-permute-done | bytes 368672 | tf_op jit(solution)/shard_map/ppermute | solution.py:111
  123.0 7.1 %collective-permute-done.19 = bf16[192,960]{1,0:T(8,128)(2,1)S(1)} collective-permute-done((bf16[192,960]{1,0:T(8,128)(2,1)S(1)}, bf16[192,960]{1,0:T(8,128)(2,1)S(1)}, u32[]{:S(2)}, u32[]{:S(2)}) %collective-permute-start.19) | collective-permute-done | bytes 368672 | tf_op jit(solution)/shard_map/ppermute | solution.py:111
  131.3 7.3 %collective-permute-done.18 = bf16[192,960]{1,0:T(8,128)(2,1)S(1)} collective-permute-done((bf16[192,960]{1,0:T(8,128)(2,1)S(1)}, bf16[192,960]{1,0:T(8,128)(2,1)S(1)}, u32[]{:S(2)}, u32[]{:S(2)}) %collective-permute-start.18) | collective-permute-done | bytes 368672 | tf_op jit(solution)/shard_map/ppermute | solution.py:111
  140.0 6.2 %collective-permute-done.20 = bf16[192,960]{1,0:T(8,128)(2,1)S(1)} collective-permute-done((bf16[192,960]{1,0:T(8,128)(2,1)S(1)}, bf16[192,960]{1,0:T(8,128)(2,1)S(1)}, u32[]{:S(2)}, u32[]{:S(2)}) %collective-permute-start.20) | collective-permute-done | bytes 368672 | tf_op jit(solution)/shard_map/ppermute | solution.py:111
  148.0 8.7 %convolution_convert_fusion = bf16[960,1280]{1,0:T(8,128)(2,1)S(1)} fusion(bf16[768,960]{1,0:T(8,128)(2,1)S(1)} %pad_maximum_fusion.4, bf16[192,640]{1,0:T(8,128)(2,1)S(1)} %get-tuple-element.161, bf16[192,640]{1,0:T(8,128)(2,1)S(1)} %get-tuple-element.160, bf16[192,640]{1,0:T(8,128)(2,1)S(1)} %get-tuple-element.163, ...), kind=kOutput, calls=%fused_computation.2 | convolution fusion | flops 1904394240 | bytes 5898240 | tf_op jit(solution)/shard_map/dot_general | solution.py:29
  159.8 4.1 %collective-permute-done.21 = bf16[480,1920]{1,0:T(8,128)(2,1)} collective-permute-done((bf16[480,1920]{1,0:T(8,128)(2,1)}, bf16[480,1920]{1,0:T(8,128)(2,1)}, u32[]{:S(2)}, u32[]{:S(2)}) %collective-permute-start.21) | collective-permute-done | bytes 1843232 | tf_op jit(solution)/shard_map/ppermute | solution.py:80
  166.8 6.6 %collective-permute-done.22 = bf16[192,960]{1,0:T(8,128)(2,1)S(1)} collective-permute-done((bf16[192,960]{1,0:T(8,128)(2,1)}, bf16[192,960]{1,0:T(8,128)(2,1)S(1)}, u32[]{:S(2)}, u32[]{:S(2)}) %collective-permute-start.22) | collective-permute-done | bytes 368672 | tf_op jit(solution)/shard_map/ppermute | solution.py:111
  181.2 10.1 %attend_back.1 = (bf16[192,960]{1,0:T(8,128)(2,1)S(1)}, bf16[768,640]{1,0:T(8,128)(2,1)S(1)}) custom-call(bf16[192,960]{1,0:T(8,128)(2,1)S(1)} %copy-done.1, bf16[768,320]{1,0:T(8,128)(2,1)S(1)} %get-tuple-element.54.k_ref, bf16[768,320]{1,0:T(8,128)(2,1)S(1)} %slice.642.v_ref, bf16[192,960]{1,0:T(8,128)(2,1)S(1)} %get-tuple-element.55.mix_ref, ...), custom_call_target="tpu_custom_call" | custom-call | flops 1415577600 | bytes 6000000 | tf_op jit(solution)/shard_map/attend_back/pallas_call | solution.py:239
  191.2 8.0 %collective-permute-done.23 = bf16[480,960]{1,0:T(8,128)(2,1)S(1)} collective-permute-done((bf16[480,960]{1,0:T(8,128)(2,1)S(1)}, bf16[480,960]{1,0:T(8,128)(2,1)S(1)}, u32[]{:S(2)}, u32[]{:S(2)}) %collective-permute-start.23) | collective-permute-done | bytes 921632 | tf_op jit(solution)/shard_map/ppermute | solution.py:80
  205.1 5.6 %concatenate.189 = bf16[960,1601]{1,0:T(8,128)(2,1)} concatenate(bf16[960,640]{1,0:T(8,128)(2,1)S(1)} %convolution_convert_fusion.3, bf16[960,960]{1,0:T(8,128)(2,1)} %convolution_convert_fusion.1, bf16[960,1]{1,0:T(8,128)(2,1)S(1)} %copy-done.31), dimensions={1} | concatenate | bytes 6147840 | tf_op jit(solution)/shard_map/concatenate | solution.py:393
  212.5 3.4 collective-permute-done.27
  220.6 12.9 %collective-permute-done.29 = bf16[384,640]{1,0:T(8,128)(2,1)} collective-permute-done((bf16[384,640]{1,0:T(8,128)(2,1)S(1)}, bf16[384,640]{1,0:T(8,128)(2,1)}, u32[]{:S(2)}, u32[]{:S(2)}) %collective-permute-start.29) | collective-permute-done | bytes 491552 | tf_op jit(solution)/shard_map/ppermute | solution.py:80
  239.5 3.6 %all-to-all-start = ((bf16[8,32,1601]{2,1,0:T(8,128)(2,1)}), bf16[8,32,1601]{2,1,0:T(8,128)(2,1)S(1)}, u32[]{:S(2)}, u32[]{:S(2)}) async-start(bf16[8,32,1601]{2,1,0:T(8,128)(2,1)} %bitcast.17), calls=%async_computation | async-start | bytes 1703936 | tf_op jit(solution)/shard_map/all_to_all | solution.py:126
  248.9 15.9 %collective-permute-done.31 = bf16[192,640]{1,0:T(8,128)(2,1)S(1)} collective-permute-done((bf16[192,640]{1,0:T(8,128)(2,1)S(1)}, bf16[192,640]{1,0:T(8,128)(2,1)S(1)}, u32[]{:S(2)}, u32[]{:S(2)}) %collective-permute-start.31) | collective-permute-done | bytes 245792 | tf_op jit(solution)/shard_map/ppermute | solution.py:80
  267.0 9.4 %collective-permute-done.32 = bf16[192,960]{1,0:T(8,128)(2,1)S(1)} collective-permute-done((bf16[192,960]{1,0:T(8,128)(2,1)S(1)}, bf16[192,960]{1,0:T(8,128)(2,1)S(1)}, u32[]{:S(2)}, u32[]{:S(2)}) %collective-permute-start.32) | collective-permute-done | bytes 368672 | tf_op jit(solution)/shard_map/ppermute | solution.py:111
  281.0 5.1 %all-to-all-start.1 = ((bf16[8,32,1601]{2,1,0:T(8,128)(2,1)}), bf16[8,32,1601]{2,1,0:T(8,128)(2,1)S(1)}, u32[]{:S(2)}, u32[]{:S(2)}) async-start(bf16[8,32,1601]{2,1,0:T(8,128)(2,1)} %broadcast_in_dim.31), calls=%async_computation.1 | async-start | bytes 1703936 | tf_op jit(solution)/shard_map/all_to_all | solution.py:136
  286.5 31.8 %all-reduce.3.cloned.1.call-done = bf16[960,240]{0,1:T(8,128)(2,1)} async-done(((bf16[960,240]{0,1:T(8,128)(2,1)}), bf16[960,240]{0,1:T(8,128)(2,1)}) %all-reduce.3.cloned.1.call-update) | async-done | bytes 460816 | tf_op jit(solution)/shard_map/psum | solution.py:392
  323.6 9.9 %collective-permute-done.35 = bf16[240,960]{1,0:T(8,128)(2,1)S(1)} collective-permute-done((bf16[240,960]{1,0:T(8,128)(2,1)S(1)}, bf16[240,960]{1,0:T(8,128)(2,1)S(1)}, u32[]{:S(2)}, u32[]{:S(2)}) %collective-permute-start.35) | collective-permute-done | bytes 460832 | tf_op jit(solution)/shard_map/ppermute | solution.py:80
  (396 shorter events, 112.7 us)
Async XLA Ops:
  7.2 311.2 %all-reduce.3.cloned.1.call-start = ((), (), s32[]{:S(2)}) async-start(), calls=%async_computation.2 | async-start | bytes 983040 | tf_op jit(solution)/shard_map/psum | solution.py:392
  18.6 52.4 %collective-permute-start.8 = (bf16[240,2624]{1,0:T(8,128)(2,1)}, bf16[240,2624]{1,0:T(8,128)(2,1)}, u32[]{:S(2)}, u32[]{:S(2)}) collective-permute-start(bf16[240,2624]{1,0:T(8,128)(2,1)} %concatenate.163), channel_id=1, source_target_pairs={{0,16},{8,24},{16,0},{24,8},{1,17},{9,25},{17,1},{25,9},{2,18},{10... | collective-permute-start | bytes 3778568 | tf_op jit(solution)/shard_map/ppermute | solution.py:80
  21.1 47.3 %collective-permute-start.15 = (bf16[240,1920]{1,0:T(8,128)(2,1)}, bf16[240,1920]{1,0:T(8,128)(2,1)}, u32[]{:S(2)}, u32[]{:S(2)}) collective-permute-start(bf16[240,1920]{1,0:T(8,128)(2,1)} %pad_maximum_fusion.8), channel_id=1, source_target_pairs={{0,8},{8,0},{16,24},{24,16},{1,9},{9,1},{17,25},{25,17},{2,10},{10... | collective-permute-start | bytes 2764808 | tf_op jit(solution)/shard_map/ppermute | solution.py:80
  27.3 24.0 %collective-permute-start.1 = (bf16[192,960]{1,0:T(8,128)(2,1)}, bf16[192,960]{1,0:T(8,128)(2,1)}, u32[]{:S(2)}, u32[]{:S(2)}) collective-permute-start(bf16[192,960]{1,0:T(8,128)(2,1)} %pad_maximum_fusion.9), channel_id=1, source_target_pairs={{0,1},{1,0},{2,3},{3,2},{4,5},{5,4},{6,7},{7,6},{8,9},{9,8},{10,11... | collective-permute-start | bytes 1105928 | tf_op jit(solution)/shard_map/ppermute | solution.py:80
  28.9 22.4 %collective-permute-start.2 = (bf16[192,960]{1,0:T(8,128)(2,1)}, bf16[192,960]{1,0:T(8,128)(2,1)}, u32[]{:S(2)}, u32[]{:S(2)}) collective-permute-start(bf16[192,960]{1,0:T(8,128)(2,1)} %pad_maximum_fusion.9), channel_id=1, source_target_pairs={{0,4},{4,0},{1,5},{5,1},{2,6},{6,2},{3,7},{7,3},{8,12},{12,8},{9,1... | collective-permute-start | bytes 1105928 | tf_op jit(solution)/shard_map/ppermute | solution.py:80
  30.4 18.3 %collective-permute-start.5 = (f32[240,2]{0,1:T(2,128)S(1)}, f32[240,2]{0,1:T(2,128)S(1)}, u32[]{:S(2)}, u32[]{:S(2)}) collective-permute-start(f32[240,2]{0,1:T(2,128)S(1)} %pad_maximum_fusion.23), channel_id=1, source_target_pairs={{0,16},{8,24},{16,0},{24,8},{1,17},{9,25},{17,1},{25,9},{2,18},{10... | collective-permute-start | bytes 5768 | tf_op jit(solution)/shard_map/ppermute | solution.py:80
  51.0 21.8 %collective-permute-start.9 = (bf16[240,2624]{1,0:T(8,128)(2,1)}, bf16[240,2624]{1,0:T(8,128)(2,1)S(1)}, u32[]{:S(2)}, u32[]{:S(2)}) collective-permute-start(bf16[240,2624]{1,0:T(8,128)(2,1)} %concatenate.163), channel_id=1, source_target_pairs={{0,8},{8,0},{16,24},{24,16},{1,9},{9,1},{17,25},{25,17},{2,10},{10... | collective-permute-start | bytes 3778568 | tf_op jit(solution)/shard_map/ppermute | solution.py:80
  66.2 24.1 %collective-permute-start.12 = (bf16[2,96,960]{2,1,0:T(8,128)(2,1)S(1)}, bf16[2,96,960]{2,1,0:T(8,128)(2,1)S(1)}, u32[]{:S(2)}, u32[]{:S(2)}) collective-permute-start(bf16[2,96,960]{2,1,0:T(8,128)(2,1)S(1)} %maximum_select_fusion.1), channel_id=1, source_target_pairs={{0,3},{1,0},{2,1},{3,2},{4,7},{5,4},{6,5},{7,6},{8,11},{9,8},{10,9... | collective-permute-start | bytes 1105928 | tf_op jit(solution)/shard_map/ppermute | solution.py:111
  66.2 24.0 %collective-permute-start.11 = (bf16[2,96,960]{2,1,0:T(8,128)(2,1)S(1)}, bf16[2,96,960]{2,1,0:T(8,128)(2,1)S(1)}, u32[]{:S(2)}, u32[]{:S(2)}) collective-permute-start(bf16[2,96,960]{2,1,0:T(8,128)(2,1)S(1)} %collective-permute-done.4), channel_id=1, source_target_pairs={{0,1},{1,2},{2,3},{3,0},{4,5},{5,6},{6,7},{7,4},{8,9},{9,10},{10,1... | collective-permute-start | bytes 1105928 | tf_op jit(solution)/shard_map/ppermute | solution.py:111
  77.5 23.0 %collective-permute-start.14 = (bf16[240,1920]{1,0:T(8,128)(2,1)}, bf16[240,1920]{1,0:T(8,128)(2,1)S(1)}, u32[]{:S(2)}, u32[]{:S(2)}) collective-permute-start(bf16[240,1920]{1,0:T(8,128)(2,1)} %pad_maximum_fusion.8), channel_id=1, source_target_pairs={{0,16},{8,24},{16,0},{24,8},{1,17},{9,25},{17,1},{25,9},{2,18},{10... | collective-permute-start | bytes 2764808 | tf_op jit(solution)/shard_map/ppermute | solution.py:80
  90.3 17.6 %collective-permute-start.13 = (bf16[192,960]{1,0:T(8,128)(2,1)S(1)}, bf16[192,960]{1,0:T(8,128)(2,1)S(1)}, u32[]{:S(2)}, u32[]{:S(2)}) collective-permute-start(bf16[192,960]{1,0:T(8,128)(2,1)S(1)} %multiply_convert_fusion.1), channel_id=1, source_target_pairs={{0,1},{1,2},{2,3},{3,0},{4,5},{5,6},{6,7},{7,4},{8,9},{9,10},{10,1... | collective-permute-start | bytes 1105928 | tf_op jit(solution)/shard_map/ppermute | solution.py:111
  110.2 20.0 %collective-permute-start.19 = (bf16[192,960]{1,0:T(8,128)(2,1)S(1)}, bf16[192,960]{1,0:T(8,128)(2,1)S(1)}, u32[]{:S(2)}, u32[]{:S(2)}) collective-permute-start(bf16[192,960]{1,0:T(8,128)(2,1)S(1)} %convolution_convert_fusion.12), channel_id=1, source_target_pairs={{0,1},{1,2},{2,3},{3,0},{4,5},{5,6},{6,7},{7,4},{8,9},{9,10},{10,1... | collective-permute-start | bytes 1105928 | tf_op jit(solution)/shard_map/ppermute | solution.py:111
  121.7 16.9 %collective-permute-start.18 = (bf16[192,960]{1,0:T(8,128)(2,1)S(1)}, bf16[192,960]{1,0:T(8,128)(2,1)S(1)}, u32[]{:S(2)}, u32[]{:S(2)}) collective-permute-start(bf16[192,960]{1,0:T(8,128)(2,1)S(1)} %collective-permute-done.17), channel_id=1, source_target_pairs={{0,1},{1,2},{2,3},{3,0},{4,5},{5,6},{6,7},{7,4},{8,9},{9,10},{10,1... | collective-permute-start | bytes 1105928 | tf_op jit(solution)/shard_map/ppermute | solution.py:111
  175.0 24.2 %collective-permute-start.23 = (bf16[480,960]{1,0:T(8,128)(2,1)S(1)}, bf16[480,960]{1,0:T(8,128)(2,1)S(1)}, u32[]{:S(2)}, u32[]{:S(2)}) collective-permute-start(bf16[480,960]{1,0:T(8,128)(2,1)S(1)} %get-tuple-element.72), channel_id=1, source_target_pairs={{0,4},{4,0},{1,5},{5,1},{2,6},{6,2},{3,7},{7,3},{8,12},{12,8},{9,1... | collective-permute-start | bytes 2764808 | tf_op jit(solution)/shard_map/ppermute | solution.py:80
  177.8 22.7 %collective-permute-start.25 = (bf16[240,960]{1,0:T(8,128)(2,1)S(1)}, bf16[240,960]{1,0:T(8,128)(2,1)S(1)}, u32[]{:S(2)}, u32[]{:S(2)}) collective-permute-start(bf16[240,960]{1,0:T(8,128)(2,1)S(1)} %slice.519), channel_id=1, source_target_pairs={{0,16},{8,24},{16,0},{24,8},{1,17},{9,25},{17,1},{25,9},{2,18},{10... | collective-permute-start | bytes 1382408 | tf_op jit(solution)/shard_map/ppermute | solution.py:80
  180.0 21.4 %collective-permute-start.26 = (bf16[192,960]{1,0:T(8,128)(2,1)S(1)}, bf16[192,960]{1,0:T(8,128)(2,1)S(1)}, u32[]{:S(2)}, u32[]{:S(2)}) collective-permute-start(bf16[192,960]{1,0:T(8,128)(2,1)S(1)} %convolution_convert_fusion.8), channel_id=1, source_target_pairs={{0,1},{1,2},{2,3},{3,0},{4,5},{5,6},{6,7},{7,4},{8,9},{9,10},{10,1... | collective-permute-start | bytes 1105928 | tf_op jit(solution)/shard_map/ppermute | solution.py:111
  217.1 20.2 %collective-permute-start.28 = (bf16[240,1601]{1,0:T(8,128)(2,1)}, bf16[240,1601]{1,0:T(8,128)(2,1)}, u32[]{:S(2)}, u32[]{:S(2)}) collective-permute-start(bf16[240,1601]{1,0:T(8,128)(2,1)} %slice.523), channel_id=1, source_target_pairs={{0,16},{8,24},{16,0},{24,8},{1,17},{9,25},{17,1},{25,9},{2,18},{10... | collective-permute-start | bytes 2305448 | tf_op jit(solution)/shard_map/ppermute | solution.py:80
  220.6 17.9 %collective-permute-start.30 = (bf16[192,960]{1,0:T(8,128)(2,1)}, bf16[192,960]{1,0:T(8,128)(2,1)}, u32[]{:S(2)}, u32[]{:S(2)}) collective-permute-start(bf16[192,960]{1,0:T(8,128)(2,1)} %fusion.23), channel_id=1, source_target_pairs={{0,1},{1,2},{2,3},{3,0},{4,5},{5,6},{6,7},{7,4},{8,9},{9,10},{10,1... | collective-permute-start | bytes 1105928 | tf_op jit(solution)/shard_map/ppermute | solution.py:111
  239.5 39.6 %all-to-all-start = ((bf16[8,32,1601]{2,1,0:T(8,128)(2,1)}), bf16[8,32,1601]{2,1,0:T(8,128)(2,1)S(1)}, u32[]{:S(2)}, u32[]{:S(2)}) async-start(bf16[8,32,1601]{2,1,0:T(8,128)(2,1)} %bitcast.17), calls=%async_computation | async-start | bytes 1703936 | tf_op jit(solution)/shard_map/all_to_all | solution.py:126
  243.1 21.7 %collective-permute-start.31 = (bf16[192,640]{1,0:T(8,128)(2,1)S(1)}, bf16[192,640]{1,0:T(8,128)(2,1)S(1)}, u32[]{:S(2)}, u32[]{:S(2)}) collective-permute-start(bf16[192,640]{1,0:T(8,128)(2,1)S(1)} %slice.429), channel_id=1, source_target_pairs={{0,1},{1,0},{2,3},{3,2},{4,5},{5,4},{6,7},{7,6},{8,9},{9,8},{10,11... | collective-permute-start | bytes 737288 | tf_op jit(solution)/shard_map/ppermute | solution.py:80
  247.1 29.3 %collective-permute-start.32 = (bf16[192,960]{1,0:T(8,128)(2,1)S(1)}, bf16[192,960]{1,0:T(8,128)(2,1)S(1)}, u32[]{:S(2)}, u32[]{:S(2)}) collective-permute-start(bf16[192,960]{1,0:T(8,128)(2,1)S(1)} %fusion.24), channel_id=1, source_target_pairs={{0,1},{1,2},{2,3},{3,0},{4,5},{5,6},{6,7},{7,4},{8,9},{9,10},{10,1... | collective-permute-start | bytes 1105928 | tf_op jit(solution)/shard_map/ppermute | solution.py:111
  247.4 31.6 %collective-permute-start.33 = (bf16[240,960]{1,0:T(8,128)(2,1)S(1)}, bf16[240,960]{1,0:T(8,128)(2,1)S(1)}, u32[]{:S(2)}, u32[]{:S(2)}) collective-permute-start(bf16[240,960]{1,0:T(8,128)(2,1)S(1)} %slice.451), channel_id=1, source_target_pairs={{0,16},{8,24},{16,0},{24,8},{1,17},{9,25},{17,1},{25,9},{2,18},{10... | collective-permute-start | bytes 1382408 | tf_op jit(solution)/shard_map/ppermute | solution.py:80
  280.1 40.7 %collective-permute-start.34 = (bf16[192,960]{1,0:T(8,128)(2,1)}, bf16[192,960]{1,0:T(8,128)(2,1)}, u32[]{:S(2)}, u32[]{:S(2)}) collective-permute-start(bf16[192,960]{1,0:T(8,128)(2,1)} %pad_maximum_fusion.13), channel_id=1, source_target_pairs={{0,2},{1,3},{2,0},{3,1},{4,6},{5,7},{6,4},{7,5},{8,10},{9,11},{10,... | collective-permute-start | bytes 1105928 | tf_op jit(solution)/shard_map/ppermute | solution.py:80
  281.0 54.0 %all-to-all-start.1 = ((bf16[8,32,1601]{2,1,0:T(8,128)(2,1)}), bf16[8,32,1601]{2,1,0:T(8,128)(2,1)S(1)}, u32[]{:S(2)}, u32[]{:S(2)}) async-start(bf16[8,32,1601]{2,1,0:T(8,128)(2,1)} %broadcast_in_dim.31), calls=%async_computation.1 | async-start | bytes 1703936 | tf_op jit(solution)/shard_map/all_to_all | solution.py:136
  (103 other events, 1087.8 us)
Sparse Core Ops, SparseCore 0:
  220.7 97.5 all-reduce.2

commit v4 on v3

--- a/solution.py
+++ b/solution.py
@@ -206,11 +206,16 @@
 
 
 def attend_back_kernel(
-    q_ref, k_ref, v_ref, mix_ref, gm_ref, log_ref, qt_ref, kt_ref, qp_ref, kp_ref, gq_ref, gkv_ref
+    q_ref, k_ref, v_ref, mix_ref, gm_ref, log_ref, qt_ref, kt_ref, qp_ref, kp_ref, grad_ref
 ):
     hidden = jnp.where(kp_ref[...] <= qp_ref[...], 0.0, -1e30)
     hidden = jnp.concatenate([hidden] * GROUP, 0)
-    rows = q_ref.shape[0]
+    rows, keys = q_ref.shape[0], k_ref.shape[0]
+    kv_cols = 2 * k_ref.shape[1]
+    grad_ref[rows:, kv_cols:] = jnp.zeros((keys - rows, grad_ref.shape[1] - kv_cols), jnp.bfloat16)
+    used = kv_cols + q_ref.shape[1]
+    if used < grad_ref.shape[1]:
+        grad_ref[:rows, used:] = jnp.zeros((rows, grad_ref.shape[1] - used), jnp.bfloat16)
     for g in range(KEY_VALUE_HEADS):
         key, value = k_ref[:, head_cols(g)], v_ref[:, head_cols(g)]
         each = [head_cols(g * GROUP + i) for i in range(GROUP)]
@@ -229,19 +234,17 @@
         grad_value = dot_cols(probs.astype(jnp.bfloat16), grad_mix)
         for i in range(GROUP):
             head = turn_back(grad_query[i * rows : (i + 1) * rows], qt_ref[...])
-            gq_ref[:, each[i]] = head.astype(jnp.bfloat16)
-        gkv_ref[:, head_cols(g)] = turn_back(grad_key, kt_ref[...]).astype(jnp.bfloat16)
-        gkv_ref[:, head_cols(KEY_VALUE_HEADS + g)] = grad_value.astype(jnp.bfloat16)
+            grad_ref[:rows, head_cols(2 * KEY_VALUE_HEADS + g * GROUP + i)] = head.astype(jnp.bfloat16)
+        grad_ref[:, head_cols(g)] = turn_back(grad_key, kt_ref[...]).astype(jnp.bfloat16)
+        grad_ref[:, head_cols(KEY_VALUE_HEADS + g)] = grad_value.astype(jnp.bfloat16)
 
 
 def attend_back(query, key, value, mix, grad_mix, log_total, query_table, key_table, query_pos, key_pos):
     rows, keys = query.shape[0], key.shape[0]
+    used = 2 * key.shape[1] + query.shape[1]
     return pl.pallas_call(
         attend_back_kernel,
-        out_shape=(
-            jax.ShapeDtypeStruct(query.shape, jnp.bfloat16),
-            jax.ShapeDtypeStruct((keys, 2 * key.shape[1]), jnp.bfloat16),
-        ),
+        out_shape=jax.ShapeDtypeStruct((keys, used + -used % 128), jnp.bfloat16),
         compiler_params=pltpu.CompilerParams(vmem_limit_bytes=KERNEL_VMEM),
         cost_estimate=pl.CostEstimate(
             flops=10 * rows * keys * QUERY_HEADS * HEAD_SIZE,
@@ -284,6 +287,9 @@
     query_table, query_pos = key_table[:rows], key_pos[:rows, None]
     key_pos = key_pos[None, :]
 
+    gains = gather_rows(jnp.concatenate([attn_gain[:, None], mlp_gain[:, None]], 1))
+    gain_a, gain_m = gains[:, 0], gains[:, 1]
+
     mine = jnp.where(upper, tokens[1], tokens[0])
     moved = swap(jnp.where(upper, tokens[0], tokens[1]), "tensor", 2)
     own = jnp.concatenate([to_relative(mine, shards, shard), to_relative(moved, shards, shard)], 0)
@@ -299,8 +305,6 @@
     first_pieces = gather_pieces(
         jnp.concatenate([attn_local, jnp.zeros_like(attn_local[:, :gap]), out_local], 1)
     )
-    gains = gather_rows(after(jnp.concatenate([attn_gain[:, None], mlp_gain[:, None]], 1), moved))
-    gain_a, gain_m = gains[:, 0], gains[:, 1]
     ends = (2 * kv_cols, attn_local.shape[1], attn_local.shape[1] + gap)
     w_kv = jnp.concatenate([piece[:, : ends[0]] for piece in first_pieces], 0)
     w_q = jnp.concatenate([piece[:, ends[0] : ends[1]] for piece in first_pieces], 0)
@@ -361,8 +365,9 @@
         if k > 0:
             grad_nm = backs[k] if k == 1 else backs[k] + shift(grad_nm, 1)
     bits = bits_of(shards)
-    group, grad_in = after(jnp.concatenate(group, 0), grad_nm), jnp.concatenate(grads_in, 0)
-    act, cot_group = after(jnp.concatenate(acts, 0), grad_nm), jnp.concatenate(cots, 0)
+    *held, _ = barrier((*grads_in, *acts, grad_nm))
+    group, cot_group = jnp.concatenate(group, 0), jnp.concatenate(cots, 0)
+    grad_in, act = jnp.concatenate(held[:places], 0), jnp.concatenate(held[places:], 0)
     mlp_term = jnp.concatenate(
         [dot_cols(group, grad_in).astype(jnp.bfloat16), dot_cols(cot_group, act).astype(jnp.bfloat16)], 1
     )
@@ -372,55 +377,49 @@
     later = context == 1
     mlp_kept, mlp_sent = jnp.where(later, second, first), jnp.where(later, first, second)
 
-    mlp_kept, mlp_sent, last = barrier((mlp_kept, mlp_sent, backs[0]))
-    grad_nm = (last + shift(grad_nm, 1)).astype(jnp.float32)
+    grad_nm = (backs[0] + shift(grad_nm, 1)).astype(jnp.float32)
     grad_hidden = own_cot.astype(jnp.float32) + norm_back(grad_nm, hidden, scale_m, gain_m)
     gain_m_term = jnp.sum(grad_nm * (hidden * scale_m), axis=0)
     grad_hidden_low = grad_hidden.astype(jnp.bfloat16)
     grad_mix = dot(grad_hidden_low, out_weight).astype(jnp.bfloat16)
-    mlp_half = mlp_kept + swap(mlp_sent, "context", 1)
     out_term = scatter_rows(dot_cols(grad_hidden_low, mix).astype(jnp.bfloat16), 0, bits)
     forward = [dot_rows(act, w_dn).astype(jnp.bfloat16) for act in acts]
     total = shift(after(forward[1], grad_mix), 1)
 
-    grad_query, grad_kv = attend_back(
+    grads = attend_back(
         query_rot, key_rot, value, mix, grad_mix, log_total, query_table, key_table, query_pos, key_pos
     )
-    grad_query, grad_kv, mlp_half, out_term, total = barrier(
-        (grad_query, grad_kv, mlp_half, out_term, total)
-    )
-    out_total = lax.psum(out_term, ("context", "tensor")).astype(jnp.float32).T
-    attn_term = jnp.concatenate(
-        [
-            dot_cols(all_normed, grad_kv).astype(jnp.bfloat16),
-            dot_cols(normed_a, grad_query).astype(jnp.bfloat16),
-            gain_m_term.astype(jnp.bfloat16)[:, None],
-        ],
-        1,
-    )
-    attn_term = scatter_rows(attn_term, 0, bits)
+    grads, out_term, total, mlp_kept, mlp_sent = barrier((grads, out_term, total, mlp_kept, mlp_sent))
+
+    attn_cols = attn_local.shape[1]
+    spot = (jnp.arange(grads.shape[1]) == attn_cols).astype(jnp.float32)
+    attn_term = dot_cols(all_normed, grads) + gain_m_term[:, None] * spot[None, :]
+    attn_term = scatter_rows(attn_term.astype(jnp.bfloat16), 0, 1)
+    mlp_sent = after(mlp_sent, attn_term)
+    attn_term = scatter_rows(attn_term, 1, bits)
+    grad_query, grad_kv = grads[:rows, 2 * kv_cols : attn_cols], grads[:, : 2 * kv_cols]
     pair = grad_kv[: 2 * rows] + swap(grad_kv[2 * rows :], "context", 1)
+    own_kv = pair[:rows] + swap(pair[rows:], "tensor", 1)
+    out_part = group_sum_parts(out_term)
     total = shift(forward[2] + total, 1)
-    attn_term, pair, total, mlp_half = barrier((attn_term, pair, total, mlp_half))
+    total = shift(forward[3] + total, 1)
+    attn_term, own_kv, out_part, total = barrier((attn_term, own_kv, out_part, total))
 
     attn_part = group_sum_parts(attn_term)
-    own_kv = pair[:rows] + swap(pair[rows:], "tensor", 1)
+    mlp_half = mlp_kept + swap(mlp_sent, "context", 1)
+    own_kv, grad_query, mlp_half = barrier((own_kv, grad_query, mlp_half))
+    mlp_half = scatter_rows(mlp_half, 1, bits)
+    block = hidden + forward[0].astype(jnp.float32) + total.astype(jnp.float32)
+    block = from_relative(block.astype(jnp.bfloat16), shards, shard)
     grad_na = dot_rows(grad_query, w_q) + dot_rows(own_kv, w_kv)
     grad_tokens = grad_hidden + norm_back(grad_na, tokens_f, scale_a, gain_a)
     grad_tokens = from_relative(grad_tokens.astype(jnp.bfloat16), shards, shard)
-    total = shift(forward[3] + total, 1)
-    block = hidden + forward[0].astype(jnp.float32) + total.astype(jnp.float32)
-    block = from_relative(block.astype(jnp.bfloat16), shards, shard)
-    mlp_half = scatter_rows(mlp_half, 1, bits)
-    attn_part, grad_tokens, block, mlp_half = barrier((attn_part, grad_tokens, block, mlp_half))
-
+    attn_part, mlp_half, block, grad_tokens = barrier((attn_part, mlp_half, block, grad_tokens))
+
+    parts = group_collect(jnp.concatenate([attn_part, out_part], 1), attn_term.shape[0])
     back_rows = swap(jnp.concatenate([block[length:], grad_tokens[length:]], 0), "tensor", 2)
     block_out = both_sequences(block[:length], back_rows[:length], upper)
     tokens_grad = both_sequences(grad_tokens[:length], back_rows[length:], upper)
-    attn_total = group_collect(attn_part, attn_term.shape[0]).astype(jnp.float32)
-    attn_total, gain_m_total = attn_total[:, :-1], attn_total[:, -1]
-    gain_a_total = jnp.sum(attn_local.astype(jnp.float32) * attn_total, axis=1) / attn_gain
-
     mlp_other = swap(mlp_half, "context", 1)
     mlp_total = jnp.concatenate(
         [jnp.where(later, mlp_other, mlp_half), jnp.where(later, mlp_half, mlp_other)], 1
@@ -428,6 +427,10 @@
     gate_total = mlp_total[:, :hidden_cols]
     up_total = mlp_total[:, hidden_cols : 2 * hidden_cols]
     down_total = mlp_total[:, 2 * hidden_cols :].T
+    parts = parts.astype(jnp.float32)
+    attn_total, gain_m_total = parts[:, :attn_cols], parts[:, attn_cols]
+    out_total = parts[:, attn_part.shape[1] :].T
+    gain_a_total = jnp.sum(attn_local.astype(jnp.float32) * attn_total, axis=1) / attn_gain
     return (
         block_out,
         tokens_grad,

time: 352 us -> 317 us (0.901)
  waiting for transfers between devices: 179 us -> 140 us
  between operations: 16.6 us -> 3.22 us
  starting transfers between devices: 34.4 us -> 44.9 us
  other arithmetic: 26.8 us -> 34.3 us
  matrix products: 33.9 us -> 29.3 us
    psum x1 -> x0, waiting for transfers between devices: 31.8 us -> none  [body(): out_total = lax.psum(out_term, ('context', 'tensor')).astype(jnp.float32).T]
    ppermute x12, waiting for transfers between devices: 50.7 us -> 42.5 us  [shift(): lax.ppermute(value, 'tensor', [(i, (i + count) % size) for i in range(siz...]
    unnamed x191 -> x209, local copies, waits for them, and re-layouts: 10.8 us -> 18.6 us
    dot_general x5 -> x4, matrix products: 14.5 us -> 7.49 us  [dot_cols(): lax.dot_general(left, right, (((0,), (0,)), ((), ())), preferred_element_...]
    concatenate x1 -> x0, local copies, waits for them, and re-layouts: 5.63 us -> none  [body(): jnp.concatenate([dot_cols(all_normed, grad_kv).astype(jnp.bfloat16), dot_...]
    all_to_all x1 -> x2, starting transfers between devices: 3.55 us -> 9.16 us  [group_sum_parts(): lax.all_to_all(padded, axes, split_axis=0, concat_axis=0, tiled=True)]
    ppermute x24, starting transfers between devices: 20.9 us -> 24.7 us  [swap(): return lax.ppermute(value, axis, [(i, i ^ bit) for i in range(size)])]
  transfers between devices with their start and end apart: 39 -> 39, of which waited for: 22 -> 19; matrix products, arithmetic and copies ran while one was open for 18% -> 24% of each run, Pallas kernels for 6% -> 6%
where the time goes in v4:
time: 317 us; the launch traced here: 312 us
  waiting for transfers between devices  140 us (44%)
  starting transfers between devices  44.9 us (14%)
  local copies, waits for them, and re-layouts  40.2 us (13%)
  other arithmetic  34.3 us (11%)
  matrix products  29.3 us (9%)
  Pallas kernels  19.7 us (6%)
  between operations  3.22 us (1%)
    ppermute x24, waiting for transfers between devices, swap(): return lax.ppermute(value, axis, [(i, i ^ bit) for i in range(size)])  97.4 us
    ppermute x12, waiting for transfers between devices, shift(): lax.ppermute(value, 'tensor', [(i, (i + count) % size) for i in range(siz...  42.5 us
    ppermute x24, starting transfers between devices, swap(): return lax.ppermute(value, axis, [(i, i ^ bit) for i in range(size)])  24.7 us
    unnamed x209, local copies, waits for them, and re-layouts  18.6 us
    dot_general x11, matrix products, dot_rows(): lax.dot_general(left, right, (((1,), (1,)), ((), ())), preferred_element_...  14.1 us
    pallas_call x1, Pallas kernels, attend_back(): pl.pallas_call(attend_back_kernel, out_shape=jax.ShapeDtypeStruct((keys,...  10.1 us
    pallas_call x1, Pallas kernels, attend(): pl.pallas_call(attend_kernel, out_shape=(jax.ShapeDtypeStruct(query.shape...  9.67 us
    all_to_all x2, starting transfers between devices, group_sum_parts(): lax.all_to_all(padded, axes, split_axis=0, concat_axis=0, tiled=True)  9.16 us
  transfers between devices with their start and end apart: 39, of which 19 were waited for; matrix products, arithmetic and copies ran while one was open for 24% of the time, Pallas kernels for 6%

profile of v4, /device:TPU:0, one launch (start us, length us, event | category | flops | bytes accessed | tf_op | source)
XLA Modules:
  0.0 311.7 jit_solution(12440158150582252042)
XLA Ops:
  2.5 4.0 %collective-permute-start = (bf16[96,960]{1,0:T(8,128)(2,1)}, bf16[96,960]{1,0:T(8,128)(2,1)}, u32[]{:S(2)}, u32[]{:S(2)}) collective-permute-start(bf16[96,960]{1,0:T(8,128)(2,1)} %get-tuple-element.225), channel_id=1, source_target_pairs={{0,2},{1,3},{2,0},{3,1},{4,6},{5,7},{6,4},{7,5},{8,10},{9,11},{10,... | collective-permute-start | bytes 552968 | tf_op jit(solution)/shard_map/ppermute | solution.py:80
  28.1 5.9 %collective-permute-done.1 = bf16[192,960]{1,0:T(8,128)(2,1)} collective-permute-done((bf16[192,960]{1,0:T(8,128)(2,1)}, bf16[192,960]{1,0:T(8,128)(2,1)}, u32[]{:S(2)}, u32[]{:S(2)}) %collective-permute-start.1) | collective-permute-done | bytes 368672 | tf_op jit(solution)/shard_map/ppermute | solution.py:80
  39.2 6.9 %collective-permute-done.3 = bf16[192,960]{1,0:T(8,128)(2,1)S(1)} collective-permute-done((bf16[192,960]{1,0:T(8,128)(2,1)}, bf16[192,960]{1,0:T(8,128)(2,1)S(1)}, u32[]{:S(2)}, u32[]{:S(2)}) %collective-permute-start.3) | collective-permute-done | bytes 368672 | tf_op jit(solution)/shard_map/ppermute | solution.py:80
  58.0 9.7 %attend.1 = (bf16[192,960]{1,0:T(8,128)(2,1)S(1)}, f32[576,8]{1,0:T(8,128)S(1)}, bf16[192,960]{1,0:T(8,128)(2,1)S(1)}, bf16[768,320]{1,0:T(8,128)(2,1)S(1)}) custom-call(f32[192,960]{1,0:T(8,128)S(1)} %fusion.39.q_ref, f32[768,320]{1,0:T(8,128)S(1)} %slice.500.k_ref, bf16[768,320]{1,0:T(8,128)(2,1)S(1)} %slice.652.v_ref, ...), custom_call_target="tpu_custom_call" | custom-call | flops 566231040 | bytes 4000000 | tf_op jit(solution)/shard_map/attend/pallas_call | solution.py:190
  69.6 9.7 %collective-permute-done.13 = bf16[240,1920]{1,0:T(8,128)(2,1)S(1)} collective-permute-done((bf16[240,1920]{1,0:T(8,128)(2,1)}, bf16[240,1920]{1,0:T(8,128)(2,1)S(1)}, u32[]{:S(2)}, u32[]{:S(2)}) %collective-permute-start.13) | collective-permute-done | bytes 921632 | tf_op jit(solution)/shard_map/ppermute | solution.py:80
  81.8 2.3 pad_maximum_fusion
  90.3 10.2 %collective-permute-done.17 = bf16[192,960]{1,0:T(8,128)(2,1)S(1)} collective-permute-done((bf16[192,960]{1,0:T(8,128)(2,1)S(1)}, bf16[192,960]{1,0:T(8,128)(2,1)S(1)}, u32[]{:S(2)}, u32[]{:S(2)}) %collective-permute-start.17) | collective-permute-done | bytes 368672 | tf_op jit(solution)/shard_map/ppermute | solution.py:111
  101.8 7.1 %collective-permute-done.19 = bf16[192,960]{1,0:T(8,128)(2,1)S(1)} collective-permute-done((bf16[192,960]{1,0:T(8,128)(2,1)S(1)}, bf16[192,960]{1,0:T(8,128)(2,1)S(1)}, u32[]{:S(2)}, u32[]{:S(2)}) %collective-permute-start.19) | collective-permute-done | bytes 368672 | tf_op jit(solution)/shard_map/ppermute | solution.py:111
  109.9 7.4 %collective-permute-done.18 = bf16[192,960]{1,0:T(8,128)(2,1)S(1)} collective-permute-done((bf16[192,960]{1,0:T(8,128)(2,1)S(1)}, bf16[192,960]{1,0:T(8,128)(2,1)S(1)}, u32[]{:S(2)}, u32[]{:S(2)}) %collective-permute-start.18) | collective-permute-done | bytes 368672 | tf_op jit(solution)/shard_map/ppermute | solution.py:111
  118.7 6.5 %collective-permute-done.20 = bf16[192,960]{1,0:T(8,128)(2,1)S(1)} collective-permute-done((bf16[192,960]{1,0:T(8,128)(2,1)S(1)}, bf16[192,960]{1,0:T(8,128)(2,1)S(1)}, u32[]{:S(2)}, u32[]{:S(2)}) %collective-permute-start.20) | collective-permute-done | bytes 368672 | tf_op jit(solution)/shard_map/ppermute | solution.py:111
  129.8 8.7 %collective-permute-done.21 = bf16[192,960]{1,0:T(8,128)(2,1)S(1)} collective-permute-done((bf16[192,960]{1,0:T(8,128)(2,1)S(1)}, bf16[192,960]{1,0:T(8,128)(2,1)S(1)}, u32[]{:S(2)}, u32[]{:S(2)}) %collective-permute-start.21) | collective-permute-done | bytes 368672 | tf_op jit(solution)/shard_map/ppermute | solution.py:111
  149.3 10.1 %attend_back.1 = bf16[768,1664]{1,0:T(8,128)(2,1)S(1)} custom-call(bf16[192,960]{1,0:T(8,128)(2,1)S(1)} %copy-done.5, bf16[768,320]{1,0:T(8,128)(2,1)S(1)} %copy-done.1, bf16[768,320]{1,0:T(8,128)(2,1)S(1)} %slice.652.v_ref, bf16[192,960]{1,0:T(8,128)(2,1)S(1)} %get-tuple-element.58.mix_ref, bf16[192,960]{1,0:T(8,128)(2,1)S(1)} %convolution_convert_fusion.7.gm_ref, ...), custom_call_target="tpu_custom_call" | custom-call | flops 1415577600 | bytes 6000000 | tf_op jit(solution)/shard_map/attend_back/pallas_call | solution.py:245
  164.2 3.2 %add_convert_fusion = bf16[960,1664]{1,0:T(8,128)(2,1)S(1)} fusion(bf16[768,960]{1,0:T(8,128)(2,1)S(1)} %copy-done.41, bf16[768,1664]{1,0:T(8,128)(2,1)S(1)} %attend_back.1, f32[1664]{0:T(1024)S(1)} %fusion.56, f32[960]{0:T(1024)S(1)} %copy-done.88), kind=kOutput, calls=%fused_computation | convolution fusion | flops 2458460160 | bytes 7235840 | tf_op jit(solution)/shard_map/dot_general | solution.py:29
  174.9 5.6 %all-to-all-start = ((bf16[8,32,960]{2,1,0:T(8,128)(2,1)}), bf16[8,32,960]{2,1,0:T(8,128)(2,1)}, u32[]{:S(2)}, u32[]{:S(2)}) async-start(bf16[8,32,960]{2,1,0:T(8,128)(2,1)} %bitcast.74), calls=%async_computation | async-start | bytes 1048576 | tf_op jit(solution)/shard_map/all_to_all | solution.py:126
  188.9 2.4 fusion.22
  192.6 10.3 %collective-permute-done.29 = bf16[192,640]{1,0:T(8,128)(2,1)S(1)} collective-permute-done((bf16[192,640]{1,0:T(8,128)(2,1)S(1)}, bf16[192,640]{1,0:T(8,128)(2,1)S(1)}, u32[]{:S(2)}, u32[]{:S(2)}) %collective-permute-start.29) | collective-permute-done | bytes 245792 | tf_op jit(solution)/shard_map/ppermute | solution.py:80
  207.6 2.3 collective-permute-done.31
  210.8 3.6 %all-to-all-start.1 = ((bf16[8,32,1664]{2,1,0:T(8,128)(2,1)}), bf16[8,32,1664]{2,1,0:T(8,128)(2,1)S(1)}, u32[]{:S(2)}, u32[]{:S(2)}) async-start(bf16[8,32,1664]{2,1,0:T(8,128)(2,1)} %bitcast.18), calls=%async_computation.1 | async-start | bytes 1703936 | tf_op jit(solution)/shard_map/all_to_all | solution.py:126
  216.7 16.4 %collective-permute-done.32 = bf16[480,960]{1,0:T(8,128)(2,1)} collective-permute-done((bf16[480,960]{1,0:T(8,128)(2,1)}, bf16[480,960]{1,0:T(8,128)(2,1)}, u32[]{:S(2)}, u32[]{:S(2)}) %collective-permute-start.32) | collective-permute-done | bytes 921632 | tf_op jit(solution)/shard_map/ppermute | solution.py:80
  242.4 5.9 %collective-permute-done.33 = bf16[240,960]{1,0:T(8,128)(2,1)S(1)} collective-permute-done((bf16[240,960]{1,0:T(8,128)(2,1)S(1)}, bf16[240,960]{1,0:T(8,128)(2,1)S(1)}, u32[]{:S(2)}, u32[]{:S(2)}) %collective-permute-start.33) | collective-permute-done | bytes 460832 | tf_op jit(solution)/shard_map/ppermute | solution.py:80
  249.7 4.3 %all-to-all-start.2 = ((bf16[8,32,2624]{2,1,0:T(8,128)(2,1)}), bf16[8,32,2624]{2,1,0:T(8,128)(2,1)}, u32[]{:S(2)}, u32[]{:S(2)}) async-start(bf16[8,32,2624]{2,1,0:T(8,128)(2,1)} %broadcast_in_dim.32), calls=%async_computation.2 | async-start | bytes 2752512 | tf_op jit(solution)/shard_map/all_to_all | solution.py:136
  254.9 2.8 collective-permute-start.34
  259.6 35.8 %collective-permute-done.34 = bf16[192,960]{1,0:T(8,128)(2,1)} collective-permute-done((bf16[192,960]{1,0:T(8,128)(2,1)}, bf16[192,960]{1,0:T(8,128)(2,1)}, u32[]{:S(2)}, u32[]{:S(2)}) %collective-permute-start.34) | collective-permute-done | bytes 368672 | tf_op jit(solution)/shard_map/ppermute | solution.py:80
  304.4 2.5 copy.64
  (419 shorter events, 125.0 us)
Async XLA Ops:
  2.5 17.6 %collective-permute-start = (bf16[96,960]{1,0:T(8,128)(2,1)}, bf16[96,960]{1,0:T(8,128)(2,1)}, u32[]{:S(2)}, u32[]{:S(2)}) collective-permute-start(bf16[96,960]{1,0:T(8,128)(2,1)} %get-tuple-element.225), channel_id=1, source_target_pairs={{0,2},{1,3},{2,0},{3,1},{4,6},{5,7},{6,4},{7,5},{8,10},{9,11},{10,... | collective-permute-start | bytes 552968 | tf_op jit(solution)/shard_map/ppermute | solution.py:80
  7.2 18.3 %collective-permute-start.5 = (f32[240,2]{0,1:T(2,128)S(1)}, f32[240,2]{0,1:T(2,128)S(1)}, u32[]{:S(2)}, u32[]{:S(2)}) collective-permute-start(f32[240,2]{0,1:T(2,128)S(1)} %pad_maximum_fusion.26), channel_id=1, source_target_pairs={{0,16},{8,24},{16,0},{24,8},{1,17},{9,25},{17,1},{25,9},{2,18},{10... | collective-permute-start | bytes 5768 | tf_op jit(solution)/shard_map/ppermute | solution.py:80
  14.3 35.2 %collective-permute-start.8 = (bf16[240,2624]{1,0:T(8,128)(2,1)}, bf16[240,2624]{1,0:T(8,128)(2,1)}, u32[]{:S(2)}, u32[]{:S(2)}) collective-permute-start(bf16[240,2624]{1,0:T(8,128)(2,1)} %concatenate.163), channel_id=1, source_target_pairs={{0,16},{8,24},{16,0},{24,8},{1,17},{9,25},{17,1},{25,9},{2,18},{10... | collective-permute-start | bytes 3778568 | tf_op jit(solution)/shard_map/ppermute | solution.py:80
  15.8 33.2 %collective-permute-start.14 = (bf16[240,1920]{1,0:T(8,128)(2,1)}, bf16[240,1920]{1,0:T(8,128)(2,1)S(1)}, u32[]{:S(2)}, u32[]{:S(2)}) collective-permute-start(bf16[240,1920]{1,0:T(8,128)(2,1)} %pad_maximum_fusion.6), channel_id=1, source_target_pairs={{0,8},{8,0},{16,24},{24,16},{1,9},{9,1},{17,25},{25,17},{2,10},{10... | collective-permute-start | bytes 2764808 | tf_op jit(solution)/shard_map/ppermute | solution.py:80
  27.9 23.7 %collective-permute-start.9 = (bf16[240,2624]{1,0:T(8,128)(2,1)}, bf16[240,2624]{1,0:T(8,128)(2,1)S(1)}, u32[]{:S(2)}, u32[]{:S(2)}) collective-permute-start(bf16[240,2624]{1,0:T(8,128)(2,1)} %concatenate.163), channel_id=1, source_target_pairs={{0,8},{8,0},{16,24},{24,16},{1,9},{9,1},{17,25},{25,17},{2,10},{10... | collective-permute-start | bytes 3778568 | tf_op jit(solution)/shard_map/ppermute | solution.py:80
  46.8 22.5 %collective-permute-start.12 = (bf16[2,96,960]{2,1,0:T(8,128)(2,1)S(1)}, bf16[2,96,960]{2,1,0:T(8,128)(2,1)S(1)}, u32[]{:S(2)}, u32[]{:S(2)}) collective-permute-start(bf16[2,96,960]{2,1,0:T(8,128)(2,1)S(1)} %maximum_select_fusion.1), channel_id=1, source_target_pairs={{0,3},{1,0},{2,1},{3,2},{4,7},{5,4},{6,5},{7,6},{8,11},{9,8},{10,9... | collective-permute-start | bytes 1105928 | tf_op jit(solution)/shard_map/ppermute | solution.py:111
  48.8 20.5 %collective-permute-start.11 = (bf16[2,96,960]{2,1,0:T(8,128)(2,1)S(1)}, bf16[2,96,960]{2,1,0:T(8,128)(2,1)S(1)}, u32[]{:S(2)}, u32[]{:S(2)}) collective-permute-start(bf16[2,96,960]{2,1,0:T(8,128)(2,1)S(1)} %collective-permute-done.4), channel_id=1, source_target_pairs={{0,1},{1,2},{2,3},{3,0},{4,5},{5,6},{6,7},{7,4},{8,9},{9,10},{10,1... | collective-permute-start | bytes 1105928 | tf_op jit(solution)/shard_map/ppermute | solution.py:111
  56.5 22.8 %collective-permute-start.13 = (bf16[240,1920]{1,0:T(8,128)(2,1)}, bf16[240,1920]{1,0:T(8,128)(2,1)S(1)}, u32[]{:S(2)}, u32[]{:S(2)}) collective-permute-start(bf16[240,1920]{1,0:T(8,128)(2,1)} %pad_maximum_fusion.6), channel_id=1, source_target_pairs={{0,16},{8,24},{16,0},{24,8},{1,17},{9,25},{17,1},{25,9},{2,18},{10... | collective-permute-start | bytes 2764808 | tf_op jit(solution)/shard_map/ppermute | solution.py:80
  69.3 17.4 %collective-permute-start.16 = (bf16[192,960]{1,0:T(8,128)(2,1)S(1)}, bf16[192,960]{1,0:T(8,128)(2,1)S(1)}, u32[]{:S(2)}, u32[]{:S(2)}) collective-permute-start(bf16[192,960]{1,0:T(8,128)(2,1)S(1)} %multiply_convert_fusion.1), channel_id=1, source_target_pairs={{0,1},{1,2},{2,3},{3,0},{4,5},{5,6},{6,7},{7,4},{8,9},{9,10},{10,1... | collective-permute-start | bytes 1105928 | tf_op jit(solution)/shard_map/ppermute | solution.py:111
  89.0 19.9 %collective-permute-start.19 = (bf16[192,960]{1,0:T(8,128)(2,1)S(1)}, bf16[192,960]{1,0:T(8,128)(2,1)S(1)}, u32[]{:S(2)}, u32[]{:S(2)}) collective-permute-start(bf16[192,960]{1,0:T(8,128)(2,1)S(1)} %convolution_convert_fusion.10), channel_id=1, source_target_pairs={{0,1},{1,2},{2,3},{3,0},{4,5},{5,6},{6,7},{7,4},{8,9},{9,10},{10,1... | collective-permute-start | bytes 1105928 | tf_op jit(solution)/shard_map/ppermute | solution.py:111
  100.4 16.9 %collective-permute-start.18 = (bf16[192,960]{1,0:T(8,128)(2,1)S(1)}, bf16[192,960]{1,0:T(8,128)(2,1)S(1)}, u32[]{:S(2)}, u32[]{:S(2)}) collective-permute-start(bf16[192,960]{1,0:T(8,128)(2,1)S(1)} %collective-permute-done.17), channel_id=1, source_target_pairs={{0,1},{1,2},{2,3},{3,0},{4,5},{5,6},{6,7},{7,4},{8,9},{9,10},{10,1... | collective-permute-start | bytes 1105928 | tf_op jit(solution)/shard_map/ppermute | solution.py:111
  109.8 15.4 %collective-permute-start.20 = (bf16[192,960]{1,0:T(8,128)(2,1)S(1)}, bf16[192,960]{1,0:T(8,128)(2,1)S(1)}, u32[]{:S(2)}, u32[]{:S(2)}) collective-permute-start(bf16[192,960]{1,0:T(8,128)(2,1)S(1)} %fusion.24), channel_id=1, source_target_pairs={{0,1},{1,2},{2,3},{3,0},{4,5},{5,6},{6,7},{7,4},{8,9},{9,10},{10,1... | collective-permute-start | bytes 1105928 | tf_op jit(solution)/shard_map/ppermute | solution.py:111
  142.9 17.1 %collective-permute-start.25 = (bf16[480,1920]{1,0:T(8,128)(2,1)}, bf16[480,1920]{1,0:T(8,128)(2,1)}, u32[]{:S(2)}, u32[]{:S(2)}) collective-permute-start(bf16[480,1920]{1,0:T(8,128)(2,1)} %pad_maximum_fusion.3), channel_id=1, source_target_pairs={{0,8},{8,0},{16,24},{24,16},{1,9},{9,1},{17,25},{25,17},{2,10},{10... | collective-permute-start | bytes 5529608 | tf_op jit(solution)/shard_map/ppermute | solution.py:80
  148.9 15.0 %collective-permute-start.24 = (bf16[192,960]{1,0:T(8,128)(2,1)S(1)}, bf16[192,960]{1,0:T(8,128)(2,1)S(1)}, u32[]{:S(2)}, u32[]{:S(2)}) collective-permute-start(bf16[192,960]{1,0:T(8,128)(2,1)S(1)} %convolution_convert_fusion.6), channel_id=1, source_target_pairs={{0,1},{1,2},{2,3},{3,0},{4,5},{5,6},{6,7},{7,4},{8,9},{9,10},{10,1... | collective-permute-start | bytes 1105928 | tf_op jit(solution)/shard_map/ppermute | solution.py:111
  172.6 16.3 %collective-permute-start.30 = (bf16[192,960]{1,0:T(8,128)(2,1)}, bf16[192,960]{1,0:T(8,128)(2,1)}, u32[]{:S(2)}, u32[]{:S(2)}) collective-permute-start(bf16[192,960]{1,0:T(8,128)(2,1)} %fusion.23), channel_id=1, source_target_pairs={{0,1},{1,2},{2,3},{3,0},{4,5},{5,6},{6,7},{7,4},{8,9},{9,10},{10,1... | collective-permute-start | bytes 1105928 | tf_op jit(solution)/shard_map/ppermute | solution.py:111
  174.9 28.8 %all-to-all-start = ((bf16[8,32,960]{2,1,0:T(8,128)(2,1)}), bf16[8,32,960]{2,1,0:T(8,128)(2,1)}, u32[]{:S(2)}, u32[]{:S(2)}) async-start(bf16[8,32,960]{2,1,0:T(8,128)(2,1)} %bitcast.74), calls=%async_computation | async-start | bytes 1048576 | tf_op jit(solution)/shard_map/all_to_all | solution.py:126
  183.6 22.7 %collective-permute-start.27 = (bf16[240,1664]{1,0:T(8,128)(2,1)}, bf16[240,1664]{1,0:T(8,128)(2,1)}, u32[]{:S(2)}, u32[]{:S(2)}) collective-permute-start(bf16[240,1664]{1,0:T(8,128)(2,1)} %slice.534), channel_id=1, source_target_pairs={{0,16},{8,24},{16,0},{24,8},{1,17},{9,25},{17,1},{25,9},{2,18},{10... | collective-permute-start | bytes 2396168 | tf_op jit(solution)/shard_map/ppermute | solution.py:80
  188.0 14.9 %collective-permute-start.29 = (bf16[192,640]{1,0:T(8,128)(2,1)S(1)}, bf16[192,640]{1,0:T(8,128)(2,1)S(1)}, u32[]{:S(2)}, u32[]{:S(2)}) collective-permute-start(bf16[192,640]{1,0:T(8,128)(2,1)S(1)} %slice.536), channel_id=1, source_target_pairs={{0,1},{1,0},{2,3},{3,2},{4,5},{5,4},{6,7},{7,6},{8,9},{9,8},{10,11... | collective-permute-start | bytes 737288 | tf_op jit(solution)/shard_map/ppermute | solution.py:80
  191.3 18.5 %collective-permute-start.31 = (bf16[192,960]{1,0:T(8,128)(2,1)}, bf16[192,960]{1,0:T(8,128)(2,1)}, u32[]{:S(2)}, u32[]{:S(2)}) collective-permute-start(bf16[192,960]{1,0:T(8,128)(2,1)} %fusion.22), channel_id=1, source_target_pairs={{0,1},{1,2},{2,3},{3,0},{4,5},{5,6},{6,7},{7,4},{8,9},{9,10},{10,1... | collective-permute-start | bytes 1105928 | tf_op jit(solution)/shard_map/ppermute | solution.py:111
  205.5 27.6 %collective-permute-start.32 = (bf16[480,960]{1,0:T(8,128)(2,1)}, bf16[480,960]{1,0:T(8,128)(2,1)}, u32[]{:S(2)}, u32[]{:S(2)}) collective-permute-start(bf16[480,960]{1,0:T(8,128)(2,1)} %get-tuple-element.85), channel_id=1, source_target_pairs={{0,4},{4,0},{1,5},{5,1},{2,6},{6,2},{3,7},{7,3},{8,12},{12,8},{9,1... | collective-permute-start | bytes 2764808 | tf_op jit(solution)/shard_map/ppermute | solution.py:80
  210.8 37.5 %all-to-all-start.1 = ((bf16[8,32,1664]{2,1,0:T(8,128)(2,1)}), bf16[8,32,1664]{2,1,0:T(8,128)(2,1)S(1)}, u32[]{:S(2)}, u32[]{:S(2)}) async-start(bf16[8,32,1664]{2,1,0:T(8,128)(2,1)} %bitcast.18), calls=%async_computation.1 | async-start | bytes 1703936 | tf_op jit(solution)/shard_map/all_to_all | solution.py:126
  249.7 49.9 %all-to-all-start.2 = ((bf16[8,32,2624]{2,1,0:T(8,128)(2,1)}), bf16[8,32,2624]{2,1,0:T(8,128)(2,1)}, u32[]{:S(2)}, u32[]{:S(2)}) async-start(bf16[8,32,2624]{2,1,0:T(8,128)(2,1)} %broadcast_in_dim.32), calls=%async_computation.2 | async-start | bytes 2752512 | tf_op jit(solution)/shard_map/all_to_all | solution.py:136
  254.9 40.5 %collective-permute-start.34 = (bf16[192,960]{1,0:T(8,128)(2,1)}, bf16[192,960]{1,0:T(8,128)(2,1)}, u32[]{:S(2)}, u32[]{:S(2)}) collective-permute-start(bf16[192,960]{1,0:T(8,128)(2,1)} %pad_maximum_fusion.15), channel_id=1, source_target_pairs={{0,2},{1,3},{2,0},{3,1},{4,6},{5,7},{6,4},{7,5},{8,10},{9,11},{10,... | collective-permute-start | bytes 1105928 | tf_op jit(solution)/shard_map/ppermute | solution.py:80
  258.0 40.0 %collective-permute-start.35 = (bf16[240,960]{1,0:T(8,128)(2,1)S(1)}, bf16[240,960]{1,0:T(8,128)(2,1)S(1)}, u32[]{:S(2)}, u32[]{:S(2)}) collective-permute-start(bf16[240,960]{1,0:T(8,128)(2,1)S(1)} %slice_add_fusion.4), channel_id=1, source_target_pairs={{0,4},{4,0},{1,5},{5,1},{2,6},{6,2},{3,7},{7,3},{8,12},{12,8},{9,1... | collective-permute-start | bytes 1382408 | tf_op jit(solution)/shard_map/ppermute | solution.py:80
  (113 other events, 1127.7 us)
